TPU v7x, 32 devices: a whole 2x2x4 slice. The times are simulated.
32 devices in a mesh: seq: 8 (over y, x, core), head: 4 (over z).
Axes of the slice: x: 2, y: 2, z: 4, core: 2. Of those that a mesh axis runs over, the one named last changes fastest.
Arguments:
- tokens: bfloat16 [32768, 512], P(('seq', 'head')), may hold values from -8.4 to 8.4
- cotangent: bfloat16 [32768, 512], P(('seq', 'head')), may hold values from -6 to 6
- w_qkv: bfloat16 [512, 1536], P(('seq', 'head')), may hold values from -0.25 to 0.25
- w_out: bfloat16 [512, 512], P(('seq', 'head')), may hold values from -0.5 to 0.5
- w_up: bfloat16 [512, 2048], P(None, ('seq', 'head')), may hold values from -0.25 to 0.25
- w_down: bfloat16 [2048, 512], P(('seq', 'head')), may hold values from -0.1875 to 0.1875
- gain_one: bfloat16 [512], P(('seq', 'head')), may hold values from 0.099609375 to 1.8984375
- shift_one: bfloat16 [512], P(('seq', 'head')), may hold values from -1.5 to 1.5
- gain_two: bfloat16 [512], P(('seq', 'head')), may hold values from 0.099609375 to 1.8984375
- shift_two: bfloat16 [512], P(('seq', 'head')), may hold values from -1.5 to 1.5
- span_doc: int32 [128], replicated, may hold values from 0 to 15, never falling along the last dimension, each value on 1 to 16 neighbouring positions
Outputs:
- out_tokens: bfloat16 [32768, 512], P(('seq', 'head'))
- d_tokens: float32 [32768, 512], P(('seq', 'head'))
- d_w_qkv: float32 [512, 1536], P(('seq', 'head'))
- d_w_out: float32 [512, 512], P(('seq', 'head'))
- d_w_up: float32 [512, 2048], P(None, ('seq', 'head'))
- d_w_down: float32 [2048, 512], P(('seq', 'head'))
- d_gain_one: float32 [512], P(('seq', 'head'))
- d_shift_one: float32 [512], P(('seq', 'head'))
- d_gain_two: float32 [512], P(('seq', 'head'))
- d_shift_two: float32 [512], P(('seq', 'head'))
Inputs may be any that keep to these rules, and one draw needn't show every extreme that they name: span_doc[j] is the document of continuation span j; the numbers never fall along j, every continuation holds 1 to 16 spans, and one holds exactly 16.
All inputs are finite; a program needn't handle non-finite values.
Results may differ from a plain program's by a relative error of at most 0.012.
Values may be sent and summed in bfloat16 or wider, within the bound.
A program may use at most 128 MiB of HBM per device.

v0:
```python
import math

import jax
import jax.numpy as jnp
from jax import lax
from jax.sharding import PartitionSpec as P

H = 8
HD = 64
S = 128
QB = 512
MOST = 16
PSPANS = 128


epsilon = 1e-05
masked_score = -1e30


def layer_norm(values, gain, shift):
    row_mean = jnp.mean(values, axis=-1, keepdims=True)
    centred = values - row_mean
    variance = jnp.mean(centred * centred, axis=-1, keepdims=True)
    return centred * lax.rsqrt(variance + epsilon) * gain + shift


def gelu_tanh(values):
    return jax.nn.gelu(values, approximate=True)


def window_rows(first_span, sum_keys_all, sum_vals_all, docs_all):
    spans_blk = QB // S
    window = MOST + spans_blk
    win_start = jnp.maximum(first_span - MOST, 0)
    win_keys = lax.dynamic_slice_in_dim(sum_keys_all, win_start, window, 0)
    win_vals = lax.dynamic_slice_in_dim(sum_vals_all, win_start, window, 0)
    win_docs = lax.dynamic_slice_in_dim(docs_all, win_start, window, 0)
    sum_keys = jnp.concatenate([sum_keys_all[:PSPANS], win_keys], axis=0)
    sum_vals = jnp.concatenate([sum_vals_all[:PSPANS], win_vals], axis=0)
    sum_index = jnp.concatenate(
        [jnp.arange(PSPANS, dtype=jnp.int32), win_start + jnp.arange(window, dtype=jnp.int32)]
    )
    row_docs = jnp.concatenate([jnp.full((PSPANS,), -2, jnp.int32), win_docs])
    prompt_row = jnp.arange(PSPANS + window) < PSPANS
    query_span = first_span + jnp.arange(spans_blk, dtype=jnp.int32)
    query_doc = lax.dynamic_slice_in_dim(docs_all, first_span, spans_blk, 0)
    earlier = sum_index[None, :] < query_span[:, None]
    same_doc = (sum_index[None, :] >= PSPANS) & (row_docs[None, :] == query_doc[:, None])
    allowed = (earlier & (prompt_row[None, :] | same_doc))[:, None, :]
    return (sum_keys, sum_vals, allowed, win_start)


def block_logits(q_spans, k_blk, sum_keys, allowed):
    score_scale = 1.0 / math.sqrt(HD)
    direct = (
        jnp.einsum("nihe,njhe->hnij", q_spans, k_blk, preferred_element_type=jnp.float32)
        * score_scale
    )
    causal = jnp.arange(S)[:, None] >= jnp.arange(S)[None, :]
    direct = jnp.where(causal, direct, masked_score)
    summary = (
        jnp.einsum("nihe,the->hnit", q_spans, sum_keys, preferred_element_type=jnp.float32)
        * score_scale
    )
    summary = jnp.where(allowed, summary, masked_score)
    return (direct, summary)


def shards(
    tokens,
    cotangent,
    w_qkv,
    w_out,
    w_up,
    w_down,
    gain_one,
    shift_one,
    gain_two,
    shift_two,
    span_doc,
):
    seq_count = lax.axis_size("seq")
    head_count = lax.axis_size("head")
    tok_rows = tokens.shape[0]
    spans_blk = QB // S
    score_scale = 1.0 / math.sqrt(HD)
    grad_scale = 1.0 / math.sqrt(tok_rows * seq_count * head_count)
    docs_all = jnp.concatenate([jnp.full((PSPANS,), -1, jnp.int32), span_doc])
    qkv_mat, out_mat, up_mat, down_mat, gone_full, sone_full, gtwo_full, stwo_full = (
        lax.all_gather(w_qkv, ("seq", "head"), axis=0, tiled=True),
        lax.all_gather(w_out, ("seq", "head"), axis=0, tiled=True),
        lax.all_gather(w_up, ("seq", "head"), axis=1, tiled=True),
        lax.all_gather(w_down, ("seq", "head"), axis=0, tiled=True),
        lax.all_gather(gain_one, ("seq", "head"), axis=0, tiled=True),
        lax.all_gather(shift_one, ("seq", "head"), axis=0, tiled=True),
        lax.all_gather(gain_two, ("seq", "head"), axis=0, tiled=True),
        lax.all_gather(shift_two, ("seq", "head"), axis=0, tiled=True),
    )
    gone_full = gone_full.astype(jnp.float32)
    sone_full = sone_full.astype(jnp.float32)
    gtwo_full = gtwo_full.astype(jnp.float32)
    stwo_full = stwo_full.astype(jnp.float32)
    x_rows = tokens.astype(jnp.float32)
    norm_one, back_one = jax.vjp(layer_norm, x_rows, gone_full, sone_full)
    act_one = norm_one.astype(jnp.bfloat16)
    qkv_rows = jnp.dot(act_one, qkv_mat, preferred_element_type=jnp.float32).astype(jnp.bfloat16)
    heads_dev = H // head_count
    tok_grp = tok_rows * head_count
    group_index = lax.axis_index("seq")
    qkv_local = lax.all_to_all(qkv_rows, "head", split_axis=1, concat_axis=0, tiled=True)
    spans_grp = tok_grp // S
    all_spans = spans_grp * seq_count
    block_count = tok_grp // QB
    grouped = qkv_local.reshape(tok_grp, heads_dev, 3, HD)
    pair_part = grouped[:, :, 1:].reshape(spans_grp, S, heads_dev * 2 * HD)
    span_kv = (jnp.sum(pair_part, axis=1, dtype=jnp.float32) / S).astype(jnp.bfloat16)
    all_kv = lax.all_gather(span_kv, "seq", axis=0, tiled=True)
    all_kv = all_kv.reshape(all_spans, heads_dev, 2, HD)
    sum_keys_all = all_kv[:, :, 0]
    sum_vals_all = all_kv[:, :, 1]
    block_ids = jnp.arange(block_count, dtype=jnp.int32)
    q_blocks = grouped[:, :, 0].reshape(block_count, spans_blk, S, heads_dev, HD)
    k_blocks = grouped[:, :, 1].reshape(block_count, spans_blk, S, heads_dev, HD)
    v_blocks = grouped[:, :, 2].reshape(block_count, spans_blk, S, heads_dev, HD)

    def forward_block(inputs):
        block_id, q_spans, k_blk, v_blk = inputs
        first_span = group_index * spans_grp + block_id * spans_blk
        sum_keys, sum_vals, allowed, win_start = window_rows(
            first_span, sum_keys_all, sum_vals_all, docs_all
        )
        direct, summary = block_logits(q_spans, k_blk, sum_keys, allowed)
        row_top = jnp.maximum(jnp.max(direct, axis=-1), jnp.max(summary, axis=-1))
        exp_dir = jnp.exp(direct - row_top[..., None])
        exp_sum = jnp.exp(summary - row_top[..., None])
        denominator = jnp.sum(exp_dir, axis=-1) + jnp.sum(exp_sum, axis=-1)
        low_dir = (exp_dir / denominator[..., None]).astype(jnp.bfloat16)
        lower_total_sum = (exp_sum / denominator[..., None]).astype(jnp.bfloat16)
        mixed_rows = jnp.einsum(
            "hnij,njhe->nihe", low_dir, v_blk, preferred_element_type=jnp.float32
        )
        mixed_rows = mixed_rows + jnp.einsum(
            "hnit,the->nihe", lower_total_sum, sum_vals, preferred_element_type=jnp.float32
        )
        return (
            mixed_rows.astype(jnp.bfloat16).reshape(QB, heads_dev * HD),
            row_top + jnp.log(denominator),
        )

    local_attention, log_totals = lax.map(forward_block, (block_ids, q_blocks, k_blocks, v_blocks))
    local_attention = local_attention.reshape(tok_grp, heads_dev * HD)
    attn_rows = lax.all_to_all(local_attention, "head", split_axis=0, concat_axis=1, tiled=True)
    resid = x_rows + jnp.dot(attn_rows, out_mat, preferred_element_type=jnp.float32)
    norm_two, back_two = jax.vjp(layer_norm, resid, gtwo_full, stwo_full)
    act_two = norm_two.astype(jnp.bfloat16)
    hidden = jnp.dot(act_two, up_mat, preferred_element_type=jnp.float32)
    acted, back_gelu = jax.vjp(gelu_tanh, hidden)
    acted_low = acted.astype(jnp.bfloat16)
    out_rows = resid + jnp.dot(acted_low, down_mat, preferred_element_type=jnp.float32)
    d_acted = jnp.dot(cotangent, down_mat.T, preferred_element_type=jnp.float32)
    d_hidden = back_gelu(d_acted)[0].astype(jnp.bfloat16)
    grad_down = jnp.dot(acted_low.T, cotangent, preferred_element_type=jnp.float32)
    grad_up = jnp.dot(act_two.T, d_hidden, preferred_element_type=jnp.float32)
    d_norm_two = jnp.dot(d_hidden, up_mat.T, preferred_element_type=jnp.float32)
    out_tokens = out_rows.astype(jnp.bfloat16)
    d_resid_norm, grad_gain_two, grad_shift_two = back_two(d_norm_two)
    d_resid = cotangent.astype(jnp.float32) + d_resid_norm
    d_branch = d_resid.astype(jnp.bfloat16)
    grad_out = jnp.dot(attn_rows.T, d_branch, preferred_element_type=jnp.float32)
    d_attn = jnp.dot(d_branch, out_mat.T, preferred_element_type=jnp.float32).astype(jnp.bfloat16)
    local_gradient = lax.all_to_all(d_attn, "head", split_axis=1, concat_axis=0, tiled=True)
    do_blocks = local_gradient.reshape(block_count, spans_blk, S, heads_dev, HD)

    def backward_block(sum_grads, inputs):
        block_id, q_spans, k_blk, v_blk, output_span_gradient, log_blk = inputs
        first_span = group_index * spans_grp + block_id * spans_blk
        sum_keys, sum_vals, allowed, win_start = window_rows(
            first_span, sum_keys_all, sum_vals_all, docs_all
        )
        direct, summary = block_logits(q_spans, k_blk, sum_keys, allowed)
        prob_dir = jnp.exp(direct - log_blk[..., None])
        prob_sum = jnp.exp(summary - log_blk[..., None])
        low_dir = prob_dir.astype(jnp.bfloat16)
        lower_total_sum = prob_sum.astype(jnp.bfloat16)
        grad_dir = jnp.einsum(
            "nihe,njhe->hnij", output_span_gradient, v_blk, preferred_element_type=jnp.float32
        )
        grad_sum = jnp.einsum(
            "nihe,the->hnit", output_span_gradient, sum_vals, preferred_element_type=jnp.float32
        )
        delta = jnp.sum(prob_dir * grad_dir, axis=-1) + jnp.sum(prob_sum * grad_sum, axis=-1)
        ds_dir = (prob_dir * (grad_dir - delta[..., None])).astype(jnp.bfloat16)
        ds_sum = (prob_sum * (grad_sum - delta[..., None])).astype(jnp.bfloat16)
        d_query = jnp.einsum("hnij,njhe->nihe", ds_dir, k_blk, preferred_element_type=jnp.float32)
        d_query = (
            d_query
            + jnp.einsum("hnit,the->nihe", ds_sum, sum_keys, preferred_element_type=jnp.float32)
        ) * score_scale
        d_key = (
            jnp.einsum("hnij,nihe->njhe", ds_dir, q_spans, preferred_element_type=jnp.float32)
            * score_scale
        )
        d_value = jnp.einsum(
            "hnij,nihe->njhe", low_dir, output_span_gradient, preferred_element_type=jnp.float32
        )
        summary_key_gradient = (
            jnp.einsum("kord,orkj->dkj", ds_sum, q_spans, preferred_element_type=jnp.float32)
            * score_scale
        )
        summary_value_gradient = jnp.einsum(
            "kord,orkj->dkj",
            lower_total_sum,
            output_span_gradient,
            preferred_element_type=jnp.float32,
        )
        paired_gradient = jnp.stack([summary_key_gradient, summary_value_gradient], axis=2)
        sum_grads = sum_grads.at[:PSPANS].add(paired_gradient[:PSPANS])
        current = lax.dynamic_slice_in_dim(sum_grads, win_start, MOST + spans_blk, 0)
        sum_grads = lax.dynamic_update_slice_in_dim(
            sum_grads, current + paired_gradient[PSPANS:], win_start, 0
        )
        return (sum_grads, (d_query, d_key, d_value))

    start_grads = jnp.zeros((all_spans, heads_dev, 2, HD), jnp.float32)
    sum_grads, (dq_blocks, dk_blocks, dv_blocks) = lax.scan(
        backward_block,
        start_grads,
        (block_ids, q_blocks, k_blocks, v_blocks, do_blocks, log_totals),
    )
    flat_grads = sum_grads.reshape(all_spans, heads_dev * 2 * HD)
    span_grads = lax.psum_scatter(
        flat_grads.astype(jnp.bfloat16), "seq", scatter_dimension=0, tiled=True
    ).astype(jnp.float32)
    span_grads = span_grads.reshape(spans_grp, 1, heads_dev, 2, HD) / S
    d_key_all = dk_blocks.reshape(spans_grp, S, heads_dev, HD) + span_grads[:, :, :, 0]
    d_val_all = dv_blocks.reshape(spans_grp, S, heads_dev, HD) + span_grads[:, :, :, 1]
    d_qkv_local = jnp.stack(
        [
            dq_blocks.reshape(tok_grp, heads_dev, HD),
            d_key_all.reshape(tok_grp, heads_dev, HD),
            d_val_all.reshape(tok_grp, heads_dev, HD),
        ],
        axis=2,
    )
    d_qkv_local = d_qkv_local.astype(jnp.bfloat16).reshape(tok_grp, heads_dev * 3 * HD)
    d_qkv_rows = lax.all_to_all(d_qkv_local, "head", split_axis=0, concat_axis=1, tiled=True)
    grad_qkv = jnp.dot(act_one.T, d_qkv_rows, preferred_element_type=jnp.float32)
    d_norm_one = jnp.dot(d_qkv_rows, qkv_mat.T, preferred_element_type=jnp.float32)
    d_x_norm, grad_gain_one, first_shift_gradient = back_one(d_norm_one)
    d_tokens = d_resid + d_x_norm
    (
        grad_qkv,
        grad_out,
        grad_up,
        grad_down,
        grad_gain_one,
        first_shift_gradient,
        grad_gain_two,
        grad_shift_two,
    ) = (
        lax.psum_scatter(grad_qkv, ("seq", "head"), scatter_dimension=0, tiled=True),
        lax.psum_scatter(grad_out, ("seq", "head"), scatter_dimension=0, tiled=True),
        lax.psum_scatter(grad_up, ("seq", "head"), scatter_dimension=1, tiled=True),
        lax.psum_scatter(grad_down, ("seq", "head"), scatter_dimension=0, tiled=True),
        lax.psum_scatter(grad_gain_one, ("seq", "head"), scatter_dimension=0, tiled=True),
        lax.psum_scatter(first_shift_gradient, ("seq", "head"), scatter_dimension=0, tiled=True),
        lax.psum_scatter(grad_gain_two, ("seq", "head"), scatter_dimension=0, tiled=True),
        lax.psum_scatter(grad_shift_two, ("seq", "head"), scatter_dimension=0, tiled=True),
    )
    return (
        out_tokens,
        d_tokens,
        grad_qkv * grad_scale,
        grad_out * grad_scale,
        grad_up * grad_scale,
        grad_down * grad_scale,
        grad_gain_one * grad_scale,
        first_shift_gradient * grad_scale,
        grad_gain_two * grad_scale,
        grad_shift_two * grad_scale,
    )


def solution(mesh):
    in_specs = (
        P(("seq", "head"), None),
        P(("seq", "head"), None),
        P(("seq", "head"), None),
        P(("seq", "head"), None),
        P(None, ("seq", "head")),
        P(("seq", "head"), None),
        P(("seq", "head")),
        P(("seq", "head")),
        P(("seq", "head")),
        P(("seq", "head")),
        P(),
    )
    out_specs = (
        P(("seq", "head"), None),
        P(("seq", "head"), None),
        P(("seq", "head"), None),
        P(("seq", "head"), None),
        P(None, ("seq", "head")),
        P(("seq", "head"), None),
        P(("seq", "head")),
        P(("seq", "head")),
        P(("seq", "head")),
        P(("seq", "head")),
    )
    return jax.shard_map(shards, mesh=mesh, in_specs=in_specs, out_specs=out_specs, check_vma=False)
```

profile of v0, /device:TPU:0, one launch (start us, length us, event | category | flops | bytes accessed | tf_op | source)
XLA Modules:
  0.0 1171.2 jit_solution(1539304039287238738)
XLA Ops:
  11.3 42.1 %all-reduce.12 = (bf16[512]{0:T(512)(128)(2,1)S(1)}, bf16[512]{0:T(512)(128)(2,1)S(1)}, bf16[512]{0:T(512)(128)(2,1)}, bf16[512]{0:T(512)(128)(2,1)}) all-reduce(bf16[512]{0:T(512)(128)(2,1)S(1)} %dynamic-update-slice.7, bf16[512]{0:T(512)(128)(2,1)S(1)} %dynamic-update-slice.6, ...), channel_id=1, replica_groups=mesh['seq'=8,'head'=4] {'seq','head'}, use_global_device_ids=true, to_apply=%add.4 | all-reduce | flops 2048 | bytes 8192
  56.0 12.7 %all-gather.4.cloned.1.call-done = bf16[512,1536]{1,0:T(8,128)(2,1)} async-done(((bf16[16,1536]{1,0:T(8,128)(2,1)}), bf16[512,1536]{1,0:T(8,128)(2,1)}) %all-gather.4.cloned.1.call-update) | async-done | bytes 1572880 | tf_op jit(solution)/shard_map/all_gather | solution.py:90
  68.7 5.1 convolution_convert_fusion
  84.8 74.1 %all-to-all-done = bf16[1024,4,384]{0,2,1:T(8,128)(2,1)} async-done(((bf16[1024,4,384]{0,2,1:T(8,128)(2,1)}), bf16[1024,4,384]{0,2,1:T(8,128)(2,1)}, u32[]{:S(2)}, u32[]{:S(2)}) %all-to-all-start) | async-done | bytes 3145760 | tf_op jit(solution)/shard_map/all_to_all | solution.py:110
  158.9 6.0 copy.163
  164.8 6.1 reshape.339
  192.5 9.2 all_gather.30
  202.9 68.9 %while.33 = (s32[]{:T(128)}, bf16[8,512,128]{2,1,0:T(8,128)(2,1)}, f32[8,2,4,128]{3,2,1,0:T(4,128)}, bf16[8,4,128,2,64]{2,1,0,4,3:T(4,128)(2,1)}, bf16[8,4,128,2...) while((s32[]{:T(128)}, bf16[8,512,128]{2,1,0:T(8,128)(2,1)}, ...), condition=%wide.region_8.9_spmd, body=%wide.region_3.8_spmd.sunk | while | flops 74914296 | bytes 5989179 | solution.py:150
  279.1 90.4 %all_gather.31 = bf16[512,512]{1,0:T(8,128)(2,1)} all-gather(bf16[16,512]{1,0:T(8,128)(2,1)S(1)} %copy-done.18), channel_id=1, replica_groups=mesh['seq'=8,'head'=4] {'seq','head'}, dimensions={0}, use_global_device_ids=true | all-gather | bytes 540672 | tf_op jit(solution)/shard_map/all_gather | solution.py:91
  374.6 7.6 fusion.83
  382.2 9.7 fusion.63
  408.7 20.7 %all-to-all-done.2 = bf16[1024,4,128]{0,2,1:T(8,128)(2,1)S(1)} async-done(((bf16[1024,4,128]{0,2,1:T(8,128)(2,1)}), bf16[1024,4,128]{0,2,1:T(8,128)(2,1)S(1)}, u32[]{:S(2)}, u32[]{:S(2)}) %all-to-all-start.2) | async-done | bytes 1048608 | tf_op jit(solution)/shard_map/all_to_all | solution.py:171
  433.5 120.3 %while.34 = (s32[]{:T(128)}, f32[256,2,2,64]{0,3,1,2:T(8,128)S(1)}, bf16[8,4,128,2,64]{2,4,3,1,0:T(8,128)(2,1)}, f32[8,4,128,2,64]{2,1,0,4,3:T(4,128)}, f32[8,4,...) while((s32[]{:T(128)}, f32[256,2,2,64]{0,3,1,2:T(8,128)S(1)}, ...), condition=%wide.region_16.17_spmd, body=%wide.region_13.16_spmd.sunk | while | flops 183960576 | bytes 14116731 | solution.py:225
  558.1 9.1 fusion.84
  568.8 6.7 fusion.82
  604.7 6.2 convert_element_type.128
  620.5 76.6 %all-to-all-done.3 = bf16[4,1024,384]{1,2,0:T(8,128)(2,1)} async-done(((bf16[4,1024,384]{1,2,0:T(8,128)(2,1)}), bf16[4,1024,384]{1,2,0:T(8,128)(2,1)}, u32[]{:S(2)}, u32[]{:S(2)}) %all-to-all-start.3) | async-done | bytes 3145760 | tf_op jit(solution)/shard_map/all_to_all | solution.py:246
  697.2 5.6 fusion.79
  702.8 8.4 add_convert_fusion.2
  713.6 45.6 %reduce-scatter.10.cloned.1.call-done = f32[16,512]{1,0:T(8,128)} async-done(((f32[512,512]{1,0:T(8,128)}), f32[16,512]{1,0:T(8,128)}) %reduce-scatter.10.cloned.1.call-update) | async-done | bytes 32784 | tf_op jit(solution)/shard_map/reduce_scatter | solution.py:262
  775.2 38.2 %all-reduce.11 = (f32[512]{0:T(512)S(1)}, f32[512]{0:T(512)S(1)}, f32[512]{0:T(512)S(1)}, f32[512]{0:T(512)S(1)}) all-reduce(f32[512]{0:T(512)S(1)} %get-tuple-element.526, f32[512]{0:T(512)S(1)} %get-tuple-element.617, f32[512]{0:T(512)S(1)} %get-tuple-element.524, ...), channel_id=7, replica_groups=mesh['seq'=8,'head'=4] {'seq','head'}, use_global_device_ids=true, to_apply=%region_25.26.clone | all-reduce | flops 2048 | bytes 16384
  815.8 92.5 %reduce-scatter.14.cloned.1.call-done = f32[64,512]{1,0:T(8,128)} async-done(((f32[2048,512]{1,0:T(8,128)}), f32[64,512]{1,0:T(8,128)}) %reduce-scatter.14.cloned.1.call-update) | async-done | bytes 131088 | tf_op jit(solution)/shard_map/reduce_scatter | solution.py:264
  909.8 147.4 %reduce-scatter.12.cloned.1.call-done = f32[512,64]{0,1:T(8,128)} async-done(((f32[512,2048]{0,1:T(8,128)}), f32[512,64]{0,1:T(8,128)}) %reduce-scatter.12.cloned.1.call-update) | async-done | bytes 131088 | tf_op jit(solution)/shard_map/reduce_scatter | solution.py:263
  1058.9 103.8 %reduce-scatter.8.cloned.1.call-done = f32[16,1536]{1,0:T(8,128)} async-done(((f32[512,1536]{1,0:T(8,128)}), f32[16,1536]{1,0:T(8,128)}) %reduce-scatter.8.cloned.1.call-update) | async-done | bytes 98320 | tf_op jit(solution)/shard_map/reduce_scatter | solution.py:261
  (671 shorter events, 320.6 us)
Async XLA Ops:
  7.2 61.6 %all-gather.4.cloned.1.call-start = ((), (), s32[]{:S(2)}) async-start(), calls=%async_computation.9 | async-start | bytes 1622016 | tf_op jit(solution)/shard_map/all_gather | solution.py:90
  53.4 15.3 %copy-start.19 = (f32[512]{0:T(512)}, f32[512]{0:T(512)S(1)}, u32[]{:S(2)}) copy-start(f32[512]{0:T(512)S(1)} %convert_element_type.110) | copy-start | bytes 6148
  78.5 6.3 copy-start.26
  78.5 80.4 %all-to-all-start = ((bf16[1024,4,384]{0,2,1:T(8,128)(2,1)}), bf16[1024,4,384]{0,2,1:T(8,128)(2,1)}, u32[]{:S(2)}, u32[]{:S(2)}) async-start(bf16[1024,4,384]{0,2,1:T(8,128)(2,1)} %bitcast.293), calls=%async_computation | async-start | bytes 6291456 | tf_op jit(solution)/shard_map/all_to_all | solution.py:110
  83.2 291.1 %all-gather.6.cloned.1.call-start = ((), (), s32[]{:S(2)}) async-start(), calls=%async_computation.10 | async-start | bytes 2162688 | tf_op jit(solution)/shard_map/all_gather | solution.py:92
  84.0 298.2 %all-gather.8.cloned.1.call-start = ((), (), s32[]{:S(2)}) async-start(), calls=%async_computation.11 | async-start | bytes 2162688 | tf_op jit(solution)/shard_map/all_gather | solution.py:93
  271.8 4.4 copy-start.24
  271.8 7.3 copy-start.2
  271.8 7.3 copy-start.10
  271.8 4.4 copy-start.23
  271.8 4.5 copy-start.22
  271.9 7.3 copy-start.18
  271.9 97.7 %all-to-all-start.1 = ((bf16[4,1024,128]{2,1,0:T(8,128)(2,1)}), bf16[4,1024,128]{2,1,0:T(8,128)(2,1)}, u32[]{:S(2)}, u32[]{:S(2)}) async-start(bf16[4,1024,128]{2,1,0:T(8,128)(2,1)} %bitcast.297), calls=%async_computation.1 | async-start | bytes 2097152 | tf_op jit(solution)/shard_map/all_to_all | solution.py:152
  373.9 26.9 %copy-start = (f32[1024,512]{0,1:T(8,128)}, f32[1024,512]{0,1:T(8,128)S(1)}, u32[]{:S(2)}) copy-start(f32[1024,512]{0,1:T(8,128)S(1)} %get-tuple-element.616) | copy-start | bytes 6291460
  382.2 9.7 copy-start.27
  404.9 24.6 %all-to-all-start.2 = ((bf16[1024,4,128]{0,2,1:T(8,128)(2,1)}), bf16[1024,4,128]{0,2,1:T(8,128)(2,1)S(1)}, u32[]{:S(2)}, u32[]{:S(2)}) async-start(bf16[1024,4,128]{0,2,1:T(8,128)(2,1)} %bitcast.43), calls=%async_computation.2 | async-start | bytes 2097152 | tf_op jit(solution)/shard_map/all_to_all | solution.py:171
  408.4 179.6 %reduce-scatter.16.cloned.1.call-start = ((), (), s32[]{:S(2)}) async-start(), calls=%async_computation.16 | async-start | bytes 147456
  554.6 204.5 %reduce-scatter.10.cloned.1.call-start = ((), (), s32[]{:S(2)}) async-start(), calls=%async_computation.13 | async-start | bytes 1081344 | tf_op jit(solution)/shard_map/reduce_scatter | solution.py:262
  558.0 350.2 %reduce-scatter.14.cloned.1.call-start = ((), (), s32[]{:S(2)}) async-start(), calls=%async_computation.15 | async-start | bytes 4325376 | tf_op jit(solution)/shard_map/reduce_scatter | solution.py:264
  567.2 490.1 %reduce-scatter.12.cloned.1.call-start = ((), (), s32[]{:S(2)}) async-start(), calls=%async_computation.14 | async-start | bytes 4325376 | tf_op jit(solution)/shard_map/reduce_scatter | solution.py:263
  615.5 81.7 %copy-start.20 = (f32[512]{0:T(512)S(1)}, f32[512]{0:T(512)}, u32[]{:S(2)}) copy-start(f32[512]{0:T(512)} %copy-done.19) | copy-start | bytes 6148
  615.5 81.7 %all-to-all-start.3 = ((bf16[4,1024,384]{1,2,0:T(8,128)(2,1)}), bf16[4,1024,384]{1,2,0:T(8,128)(2,1)}, u32[]{:S(2)}, u32[]{:S(2)}) async-start(bf16[4,1024,384]{1,2,0:T(8,128)(2,1)} %copy.184), calls=%async_computation.3 | async-start | bytes 6291456 | tf_op jit(solution)/shard_map/all_to_all | solution.py:246
  620.3 542.4 %reduce-scatter.8.cloned.1.call-start = ((), (), s32[]{:S(2)}) async-start(), calls=%async_computation.12 | async-start | bytes 3244032 | tf_op jit(solution)/shard_map/reduce_scatter | solution.py:261
  711.2 49.3 %copy-start.28 = (bf16[512,1536]{1,0:T(8,128)(2,1)S(1)}, bf16[512,1536]{1,0:T(8,128)(2,1)}, u32[]{:S(2)}) copy-start(bf16[512,1536]{1,0:T(8,128)(2,1)} %all-gather.4.cloned.1.call-done) | copy-start | bytes 4718596
  (18 other events, 40.4 us)
Sparse Core Ops, SparseCore 0:
  10.9 57.8 all-gather.3
  87.0 90.1 all-gather.5
  180.1 55.4 all-gather.7
  554.7 33.2 reduce-scatter.15
  590.2 168.9 reduce-scatter.9
  761.3 146.9 reduce-scatter.13
  910.5 146.7 reduce-scatter.11
  1062.7 99.9 reduce-scatter.7
where the time goes:
time: 1180 us; the launch traced here: 1170 us
  waiting for transfers between devices  576 us (49%)
  local copies, waits for them, and re-layouts  213 us (18%)
  blocking collectives  180 us (15%)
  matrix products  118 us (10%)
  other arithmetic  38 us (3%)
  starting transfers between devices  19.1 us (2%)
  between operations  14.8 us (1%)
  loops' own time  12 us (1%)
    reduce_scatter x1, waiting for transfers between devices, shards(): lax.psum_scatter(grad_up, ('seq', 'head'), scatter_dimension=1, tiled=True)  147 us
    reduce_scatter x1, waiting for transfers between devices, shards(): lax.psum_scatter(grad_qkv, ('seq', 'head'), scatter_dimension=0, tiled=True)  104 us
    reduce_scatter x1, waiting for transfers between devices, shards(): lax.psum_scatter(grad_down, ('seq', 'head'), scatter_dimension=0, tiled=T...  92.5 us
    all_gather x1, blocking collectives, shards(): lax.all_gather(w_out, ('seq', 'head'), axis=0, tiled=True)  90.4 us
    unnamed x2, blocking collectives  80.3 us
    all_to_all x1, waiting for transfers between devices, shards(): lax.all_to_all(d_qkv_local, 'head', split_axis=0, concat_axis=1, tiled=True)  76.6 us
    all_to_all x1, waiting for transfers between devices, shards(): lax.all_to_all(qkv_rows, 'head', split_axis=1, concat_axis=0, tiled=True)  74.1 us
    reduce_scatter x1, waiting for transfers between devices, shards(): lax.psum_scatter(grad_out, ('seq', 'head'), scatter_dimension=0, tiled=True)  45.6 us
  transfers between devices with their start and end apart: 12, of which 9 were waited for; matrix products, arithmetic and copies ran while one was open for 18% of the time, Pallas kernels for 0%

commit v1 on v0

v1 whole, which is shorter than its diff:
```python
import functools
import math

import jax
import jax.numpy as jnp
from jax import lax
from jax.experimental import pallas as pl
from jax.experimental.pallas import tpu as pltpu
from jax.sharding import PartitionSpec as P

H = 8
HD = 64
D = H * HD
S = 128
MOST = 16
PSPANS = 128
WIN = 2 * MOST
PAIRS = H // 2
LANES = 2 * HD
KEYS = S + PSPANS + WIN
EPS = 1e-05
MASKED = -1e30
F32 = jnp.float32
BF16 = jnp.bfloat16
VMEM = pltpu.MemorySpace.VMEM
VMEM_LIMIT = 60 * 2**20


def nn(a, b):
    return lax.dot_general(a, b, (((1,), (0,)), ((), ())), preferred_element_type=F32)


def nt(a, b):
    return lax.dot_general(a, b, (((1,), (1,)), ((), ())), preferred_element_type=F32)


def tn(a, b):
    return lax.dot_general(a, b, (((0,), (0,)), ((), ())), preferred_element_type=F32)


def window_base(first):
    return jnp.maximum((first - (MOST - 1)) // MOST, 0) * MOST


def summary_bias(first, span, docs_ref):
    base = pl.multiple_of(window_base(first), MOST)
    index = first + span
    row = lax.broadcasted_iota(jnp.int32, (PSPANS, S), 0)
    prompt = jnp.where(row < index, 0.0, MASKED)
    wrow = base + lax.broadcasted_iota(jnp.int32, (WIN, S), 0)
    same = docs_ref[pl.ds(base, WIN), :] == docs_ref[pl.ds(index, 1), :]
    window = jnp.where(same & (wrow >= PSPANS) & (wrow < index), 0.0, MASKED)
    return jnp.concatenate([prompt, window], axis=0).astype(F32)


def head_masks(scale):
    lane = lax.broadcasted_iota(jnp.int32, (1, LANES), 1)
    first = jnp.where(lane < HD, scale, 0.0).astype(BF16)
    second = jnp.where(lane < HD, 0.0, scale).astype(BF16)
    return first, second


def stack_heads(block, masks):
    return jnp.concatenate([block * masks[0], block * masks[1]], axis=0)


def pair_cols(part, pair):
    return slice(part * D + pair * LANES, part * D + (pair + 1) * LANES)


def all_keys(part, pair, rows, qkv_ref, psum_ref, wsum_ref):
    cols = pair_cols(part, pair)
    scols = pair_cols(part - 1, pair)
    return jnp.concatenate([qkv_ref[rows, cols], psum_ref[:, scols], wsum_ref[:, scols]], axis=0)


def unstack(pair_t):
    return jnp.concatenate([pair_t[:HD, :S], pair_t[HD:, S:]], axis=0)


def attend_span(span, first, qkv_ref, psum_ref, wsum_ref, docs_ref, attn_t_ref, probs_ref):
    rows = pl.ds(pl.multiple_of(span * S, S), S)
    bias = summary_bias(first, span, docs_ref)
    key_row = lax.broadcasted_iota(jnp.int32, (S, S), 0)
    query = lax.broadcasted_iota(jnp.int32, (S, S), 1)
    causal = jnp.where(key_row <= query, 0.0, MASKED).astype(F32)
    bias = jnp.concatenate([causal, bias], axis=0)
    bias = jnp.concatenate([bias, bias], axis=1)
    masks = head_masks(1.0 / math.sqrt(HD))
    for pair in range(PAIRS):
        queries = stack_heads(qkv_ref[rows, pair_cols(0, pair)], masks)
        keys = all_keys(1, pair, rows, qkv_ref, psum_ref, wsum_ref)
        vals = all_keys(2, pair, rows, qkv_ref, psum_ref, wsum_ref)
        scores = nt(keys, queries) + bias
        top = jnp.max(scores, axis=0, keepdims=True)
        grown = jnp.exp(scores - top)
        share = 1.0 / jnp.sum(grown, axis=0, keepdims=True)
        probs = (grown * share).astype(BF16)
        probs_ref[span * PAIRS + pair] = probs
        mixed = nn(vals.T, probs)
        attn_t_ref[pair * LANES : (pair + 1) * LANES, rows] = unstack(mixed).astype(BF16)


def attend_span_back(
    span, qkv_ref, psum_ref, wsum_ref, probs_ref, dattn_ref, dq_ref, dkv_ref, dsum_ref
):
    rows = pl.ds(pl.multiple_of(span * S, S), S)
    scale = 1.0 / math.sqrt(HD)
    masks = head_masks(scale)
    ones = head_masks(1.0)
    for pair in range(PAIRS):
        cols = pair_cols(0, pair)
        queries = stack_heads(qkv_ref[rows, cols], masks)
        keys = all_keys(1, pair, rows, qkv_ref, psum_ref, wsum_ref)
        vals = all_keys(2, pair, rows, qkv_ref, psum_ref, wsum_ref)
        grads = stack_heads(dattn_ref[rows, cols], ones)
        probs = probs_ref[span * PAIRS + pair]
        wide = probs.astype(F32)
        dprobs = nt(vals, grads)
        delta = jnp.sum(wide * dprobs, axis=0, keepdims=True)
        dscores = (wide * (dprobs - delta)).astype(BF16)
        dq_t = unstack(nn(keys.T, dscores)) * scale
        dq_ref[rows, cols] = dq_t.T.astype(BF16)
        dkeys = nn(dscores, queries)
        dvals = nn(probs, grads)
        vcols = pair_cols(1, pair)
        dkv_ref[rows, cols] = dkeys[:S]
        dkv_ref[rows, vcols] = dvals[:S]
        dsum_ref[:, cols] += dkeys[S:]
        dsum_ref[:, vcols] += dvals[S:]


def attention_kernel(spans, qkv_ref, psum_ref, wsum_ref, docs_ref, attn_t_ref, probs_ref):
    first = (lax.axis_index("seq") * lax.axis_size("head") + lax.axis_index("head")) * spans

    def step(span, carry):
        attend_span(span, first, qkv_ref, psum_ref, wsum_ref, docs_ref, attn_t_ref, probs_ref)
        return carry

    lax.fori_loop(0, spans, step, 0)


def attention_back_kernel(
    spans, qkv_ref, psum_ref, wsum_ref, probs_ref, dattn_ref, dq_ref, dkv_ref, dsum_ref
):
    dsum_ref[...] = jnp.zeros_like(dsum_ref)

    def step(span, carry):
        attend_span_back(
            span, qkv_ref, psum_ref, wsum_ref, probs_ref, dattn_ref, dq_ref, dkv_ref, dsum_ref
        )
        return carry

    lax.fori_loop(0, spans, step, 0)


def attention(qkv, psum, wsum, docs):
    tok = qkv.shape[0]
    spans = tok // S
    whole = pl.BlockSpec(memory_space=VMEM)
    return pl.pallas_call(
        functools.partial(attention_kernel, spans),
        out_shape=(
            jax.ShapeDtypeStruct((D, tok), BF16),
            jax.ShapeDtypeStruct((spans * PAIRS, KEYS, 2 * S), BF16),
        ),
        in_specs=[whole] * 4,
        out_specs=(whole, whole),
        compiler_params=pltpu.CompilerParams(vmem_limit_bytes=VMEM_LIMIT),
        name="attention",
    )(qkv, psum, wsum, docs)


def attention_back(qkv, psum, wsum, probs, dattn):
    tok = qkv.shape[0]
    spans = tok // S
    whole = pl.BlockSpec(memory_space=VMEM)
    return pl.pallas_call(
        functools.partial(attention_back_kernel, spans),
        out_shape=(
            jax.ShapeDtypeStruct((tok, D), BF16),
            jax.ShapeDtypeStruct((tok, 2 * D), F32),
            jax.ShapeDtypeStruct((PSPANS + WIN, 2 * D), F32),
        ),
        in_specs=[whole] * 5,
        out_specs=(whole, whole, whole),
        compiler_params=pltpu.CompilerParams(vmem_limit_bytes=VMEM_LIMIT),
        name="attention_back",
    )(qkv, psum, wsum, probs, dattn)


def layer_norm(values, gain, shift):
    row_mean = jnp.mean(values, axis=-1, keepdims=True)
    centred = values - row_mean
    variance = jnp.mean(centred * centred, axis=-1, keepdims=True)
    return centred * lax.rsqrt(variance + EPS) * gain + shift


def gelu_tanh(values):
    return jax.nn.gelu(values, approximate=True)


BOTH = ("seq", "head")


def split_parts(weight):
    rows = weight.shape[0]
    return weight.reshape(rows, H, 3, HD).transpose(0, 2, 1, 3).reshape(rows, 3 * D)


def join_parts(weight):
    rows = weight.shape[0]
    return weight.reshape(rows, 3, H, HD).transpose(0, 2, 1, 3).reshape(rows, 3 * D)


def shards(tokens, cotangent, w_qkv, w_out, w_up, w_down, gain_one, shift_one, gain_two, shift_two, span_doc):
    tok = tokens.shape[0]
    spans = tok // S
    devices = lax.axis_size("seq") * lax.axis_size("head")
    me = lax.axis_index("seq") * lax.axis_size("head") + lax.axis_index("head")
    first = me * spans
    grad_scale = 1.0 / math.sqrt(tok * devices)
    docs = jnp.concatenate([jnp.full((PSPANS,), -1, jnp.int32), span_doc])
    docs = jnp.broadcast_to(docs[:, None], (docs.shape[0], S))

    def gather(x, axis=0):
        return lax.all_gather(x, BOTH, axis=axis, tiled=True)

    def scatter(x, axis=0):
        return lax.psum_scatter(x, BOTH, scatter_dimension=axis, tiled=True)

    qkv_mat = gather(split_parts(w_qkv))
    out_mat = gather(w_out)
    up_mat = gather(w_up.T)
    down_mat = gather(w_down)
    small = gather(jnp.stack([gain_one, shift_one, gain_two, shift_two]), 1).astype(F32)
    x_rows = tokens.astype(F32)
    norm_one, back_one = jax.vjp(layer_norm, x_rows, small[0], small[1])
    act_one = norm_one.astype(BF16)
    qkv = jnp.dot(act_one, qkv_mat, preferred_element_type=F32).astype(BF16)
    span_kv = jnp.mean(qkv[:, D:].astype(F32).reshape(spans, S, 2 * D), axis=1).astype(BF16)
    all_kv = gather(span_kv)
    base = window_base(first)
    psum = all_kv[:PSPANS]
    wsum = lax.dynamic_slice_in_dim(all_kv, base, WIN, 0)
    attn_t, probs = attention(qkv, psum, wsum, docs)
    resid = x_rows + tn(attn_t, out_mat)
    norm_two, back_two = jax.vjp(layer_norm, resid, small[2], small[3])
    act_two = norm_two.astype(BF16)
    hidden = nt(act_two, up_mat)
    acted, back_gelu = jax.vjp(gelu_tanh, hidden)
    acted = acted.astype(BF16)
    out_tokens = (resid + nn(acted, down_mat)).astype(BF16)
    d_hidden = back_gelu(nt(cotangent, down_mat))[0].astype(BF16)
    grad_down = tn(acted, cotangent)
    grad_up = tn(d_hidden, act_two)
    d_resid_norm, grad_gain_two, grad_shift_two = back_two(nn(d_hidden, up_mat))
    d_resid = cotangent.astype(F32) + d_resid_norm
    d_branch = d_resid.astype(BF16)
    grad_out = nn(attn_t, d_branch)
    d_attn = nt(d_branch, out_mat).astype(BF16)
    dq, dkv, dsum = attention_back(qkv, psum, wsum, probs, d_attn)
    flat = jnp.zeros((all_kv.shape[0], 2 * D), F32)
    flat = lax.dynamic_update_slice_in_dim(flat, dsum[PSPANS:], base, 0)
    row = jnp.arange(flat.shape[0])[:, None]
    flat = jnp.where(row < PSPANS, 0.0, flat)
    flat = flat.at[:PSPANS].add(dsum[:PSPANS])
    span_grads = scatter(flat.astype(BF16)).astype(F32) / S
    dkv = (dkv.reshape(spans, S, 2 * D) + span_grads[:, None]).reshape(tok, 2 * D)
    dqkv = jnp.concatenate([dq, dkv.astype(BF16)], axis=1)
    grad_qkv = tn(act_one, dqkv)
    d_x_norm, grad_gain_one, grad_shift_one = back_one(nt(dqkv, qkv_mat))
    d_tokens = d_resid + d_x_norm
    small_grads = scatter(jnp.stack([grad_gain_one, grad_shift_one, grad_gain_two, grad_shift_two]), 1) * grad_scale
    return (
        out_tokens,
        d_tokens,
        join_parts(scatter(grad_qkv) * grad_scale),
        scatter(grad_out) * grad_scale,
        scatter(grad_up).T * grad_scale,
        scatter(grad_down) * grad_scale,
        small_grads[0],
        small_grads[1],
        small_grads[2],
        small_grads[3],
    )


def solution(mesh):
    rows, cols, vec = P(BOTH, None), P(None, BOTH), P(BOTH)
    in_specs = (rows, rows, rows, rows, cols, rows, vec, vec, vec, vec, P())
    out_specs = (rows, rows, rows, rows, cols, rows, vec, vec, vec, vec)
    return jax.shard_map(shards, mesh=mesh, in_specs=in_specs, out_specs=out_specs, check_vma=False)
```

time: 1180 us -> 1130 us (0.958)
  local copies, waits for them, and re-layouts: 213 us -> 25.3 us
  waiting for transfers between devices: 576 us -> 749 us
  matrix products: 118 us -> 64.7 us
  Pallas kernels: 0 us -> 38 us
  blocking collectives: 180 us -> 214 us
  starting transfers between devices: 19.1 us -> 0.63 us
  other arithmetic: 38 us -> 24.5 us
  loops' own time: 12 us -> 0 us
    reduce_scatter x4 -> x5, waiting for transfers between devices: 389 us -> 661 us  [scatter(): return lax.psum_scatter(x, BOTH, scatter_dimension=axis, tiled=True)]
    all_to_all x4 -> x0, waiting for transfers between devices: 171 us -> none  [the longest x1 76.6 us: shards(): lax.all_to_all(d_qkv_local, 'head', split_axis=0, concat_axis=1, tiled=True)]
    all_gather x2 -> x3, blocking collectives: 99.6 us -> 214 us  [gather(): return lax.all_gather(x, BOTH, axis=axis, tiled=True)]
    unnamed x9 -> x10, waiting for transfers between devices: 2.4 us -> 88.5 us
    unnamed x2 -> x0, blocking collectives: 80.3 us -> none
    dynamic_slice x96 -> x1, local copies, waits for them, and re-layouts: 62.4 us -> 0.63 us  [shards(): wsum = lax.dynamic_slice_in_dim(all_kv, base, WIN, 0)]
    dot_general x124 -> x12, matrix products: 118 us -> 64.7 us  [the longest x4 23.7 us: tn(): lax.dot_general(a, b, (((0,), (0,)), ((), ())), preferred_element_type=F32)]
    pallas_call x0 -> x2, Pallas kernels: none -> 38 us  [the longest x1 20.4 us: attention_back(): pl.pallas_call(functools.partial(attention_back_kernel, spans), out_shape...]
  transfers between devices with their start and end apart: 12 -> 9, of which waited for: 9 -> 6; matrix products, arithmetic and copies ran while one was open for 18% -> 6% of each run, Pallas kernels for 0% -> 2%
where the time goes in v1:
time: 1130 us
  waiting for transfers between devices  749 us (66%)
  blocking collectives  214 us (19%)
  matrix products  64.7 us (6%)
  Pallas kernels  38 us (3%)
  local copies, waits for them, and re-layouts  25.3 us (2%)
  other arithmetic  24.5 us (2%)
  between operations  14.2 us (1%)
    reduce_scatter x5, waiting for transfers between devices, scatter(): return lax.psum_scatter(x, BOTH, scatter_dimension=axis, tiled=True)  661 us
    all_gather x3, blocking collectives, gather(): return lax.all_gather(x, BOTH, axis=axis, tiled=True)  214 us
    unnamed x10, waiting for transfers between devices  88.5 us
    dot_general x4, matrix products, tn(): lax.dot_general(a, b, (((0,), (0,)), ((), ())), preferred_element_type=F32)  23.7 us
  transfers between devices with their start and end apart: 9, of which 6 were waited for; matrix products, arithmetic and copies ran while one was open for 6% of the time, Pallas kernels for 2%

profile of v1, /device:TPU:0, one launch (start us, length us, event | category | flops | bytes accessed | tf_op | source)
XLA Modules:
  0.0 1130.8 jit_solution(17335199804103745356)
XLA Ops:
  12.0 69.8 %all-gather = bf16[32,16,4]{1,2,0:T(4,128)(2,1)S(1)} all-gather(bf16[1,16,4]{1,2,0:T(4,128)(2,1)S(1)} %maximum_bitcast_fusion), channel_id=1, replica_groups=mesh['seq'=8,'head'=4] {'seq','head'}, dimensions={0}, use_global_device_ids=true | all-gather | bytes 4224 | tf_op jit(solution)/shard_map/all_gather | solution.py:227
  85.5 74.3 %all_gather.21 = bf16[512,512]{1,0:T(8,128)(2,1)} all-gather(bf16[16,512]{1,0:T(8,128)(2,1)S(1)} %copy-done.11), channel_id=1, replica_groups=mesh['seq'=8,'head'=4] {'seq','head'}, dimensions={0}, use_global_device_ids=true | all-gather | bytes 540672 | tf_op jit(solution)/shard_map/all_gather | solution.py:227
  159.8 3.4 convolution_convert_fusion.qkv_ref
  165.3 70.2 %all_gather.20 = bf16[256,1024]{1,0:T(8,128)(2,1)S(1)} all-gather(bf16[8,1024]{1,0:T(8,128)(2,1)S(1)} %multiply_convert_fusion.1), channel_id=1, replica_groups=mesh['seq'=8,'head'=4] {'seq','head'}, dimensions={0}, use_global_device_ids=true | all-gather | bytes 540672 | tf_op jit(solution)/shard_map/all_gather | solution.py:227
  237.6 17.7 %attention.1 = (bf16[512,1024]{1,0:T(8,128)(2,1)}, bf16[32,288,256]{2,1,0:T(8,128)(2,1)}) custom-call(bf16[1024,1536]{1,0:T(8,128)(2,1)} %copy-done.2, bf16[128,1024]{1,0:T(8,128)(2,1)} %slice.71.psum_ref, bf16[32,1024]{1,0:T(8,128)(2,1)} %constant_dynamic-slice_fusion.wsum_ref, s32[256,128]{1,0:T(8,128)} %broadcast_in_dim.40.docs_ref), custom_call_target="tpu_custom_call" | custom-call | tf_op jit(solution)/shard_map/attention/pallas_call | solution.py:161
  257.6 7.7 fusion.31
  265.3 9.7 fusion.6
  275.0 3.6 fusion.36
  278.7 2.9 copy.61
  288.1 20.4 %attention_back.1 = (bf16[1024,512]{1,0:T(8,128)(2,1)}, f32[1024,1024]{1,0:T(8,128)}, f32[160,1024]{1,0:T(8,128)}) custom-call(bf16[1024,1536]{1,0:T(8,128)(2,1)} %copy-done.2, bf16[128,1024]{1,0:T(8,128)(2,1)} %slice.71.psum_ref, bf16[32,1024]{1,0:T(8,128)(2,1)} %constant_dynamic-slice_fusion.wsum_ref, bf16[32,288,256]{2,1,0:T(8,128)(2,1)} %get-tuple-element.28.probs_ref, ...), custom_call_target="tpu_custom_call" | custom-call | tf_op jit(solution)/shard_map/attention_back/pallas_call | solution.py:178
  311.7 130.2 %reduce-scatter.9.cloned.1.call-done = bf16[8,1024]{1,0:T(8,128)(2,1)} async-done(((bf16[256,1024]{1,0:T(8,128)(2,1)}), bf16[8,1024]{1,0:T(8,128)(2,1)}) %reduce-scatter.9.cloned.1.call-update) | async-done | bytes 16400 | tf_op jit(solution)/shard_map/reduce_scatter | solution.py:230
  442.6 2.9 fusion.7
  445.6 3.1 fusion.37
  455.7 3.3 fusion.38
  459.1 5.5 fusion.19
  464.9 9.4 fusion.32
  474.4 6.8 fusion.30
  481.3 8.4 add_convert_fusion
  492.1 4.1 add_add_fusion.2
  499.1 87.0 %reduce-scatter.19.cloned.1.call-done = f32[16,4]{1,0:T(8,128)} async-done(((f32[512,4]{1,0:T(8,128)}), f32[16,4]{1,0:T(8,128)}) %reduce-scatter.19.cloned.1.call-update) | async-done | bytes 272
  587.4 132.8 %reduce-scatter.13.cloned.1.call-done = f32[16,512]{1,0:T(8,128)} async-done(((f32[512,512]{1,0:T(8,128)}), f32[16,512]{1,0:T(8,128)}) %reduce-scatter.13.cloned.1.call-update) | async-done | bytes 32784 | tf_op jit(solution)/shard_map/reduce_scatter | solution.py:230
  721.6 102.9 %reduce-scatter.11.cloned.1.call-done = f32[16,1536]{1,0:T(8,128)} async-done(((f32[512,1536]{1,0:T(8,128)}), f32[16,1536]{1,0:T(8,128)}) %reduce-scatter.11.cloned.1.call-update) | async-done | bytes 98320 | tf_op jit(solution)/shard_map/reduce_scatter | solution.py:230
  826.4 147.4 %reduce-scatter.17.cloned.1.call-done = f32[64,512]{1,0:T(8,128)} async-done(((f32[2048,512]{1,0:T(8,128)}), f32[64,512]{1,0:T(8,128)}) %reduce-scatter.17.cloned.1.call-update) | async-done | bytes 131088 | tf_op jit(solution)/shard_map/reduce_scatter | solution.py:230
  975.4 147.3 %reduce-scatter.15.cloned.1.call-done = f32[64,512]{1,0:T(8,128)} async-done(((f32[2048,512]{1,0:T(8,128)}), f32[64,512]{1,0:T(8,128)}) %reduce-scatter.15.cloned.1.call-update) | async-done | bytes 131088 | tf_op jit(solution)/shard_map/reduce_scatter | solution.py:230
  (108 shorter events, 45.7 us)
Async XLA Ops:
  7.2 76.7 %copy-start.10 = (bf16[1024,512]{1,0:T(8,128)(2,1)S(1)}, bf16[1024,512]{1,0:T(8,128)(2,1)}, u32[]{:S(2)}) copy-start(bf16[1024,512]{1,0:T(8,128)(2,1)} %param.14) | copy-start | bytes 3145732
  7.2 152.6 %all-gather.5.cloned.1.call-start = ((), (), s32[]{:S(2)}) async-start(), calls=%async_computation.6 | async-start | bytes 1622016 | tf_op jit(solution)/shard_map/all_gather | solution.py:227
  9.1 248.5 %all-gather.7.cloned.1.call-start = ((), (), s32[]{:S(2)}) async-start(), calls=%async_computation.7 | async-start | bytes 2162688 | tf_op jit(solution)/shard_map/all_gather | solution.py:227
  9.8 255.5 %all-gather.9.cloned.1.call-start = ((), (), s32[]{:S(2)}) async-start(), calls=%async_computation.8 | async-start | bytes 2162688 | tf_op jit(solution)/shard_map/all_gather | solution.py:227
  10.6 431.3 %reduce-scatter.9.cloned.1.call-start = ((), (), s32[]{:S(2)}) async-start(), calls=%async_computation.9 | async-start | bytes 540672 | tf_op jit(solution)/shard_map/reduce_scatter | solution.py:230
  83.6 1.9 copy-start.11
  163.2 1.7 copy-start.2
  235.5 19.8 %copy-start.7 = (bf16[512,512]{1,0:T(8,128)(2,1)S(1)}, bf16[512,512]{1,0:T(8,128)(2,1)}, u32[]{:S(2)}) copy-start(bf16[512,512]{1,0:T(8,128)(2,1)} %all_gather.21) | copy-start | bytes 1572868
  265.3 9.7 copy-start.12
  275.0 3.7 copy-start.15
  281.6 2.4 copy-start.3
  284.0 1.2 copy-start.5
  284.6 1.3 copy-start.4
  286.3 1.7 copy-start.9
  311.6 274.4 %reduce-scatter.19.cloned.1.call-start = ((), (), s32[]{:S(2)}) async-start(), calls=%async_computation.14 | async-start | bytes 270336
  442.6 3.0 copy-start.13
  442.6 3.0 copy-start.14
  445.6 3.2 copy-start.6
  451.6 2.2 copy-start
  455.7 264.5 %reduce-scatter.13.cloned.1.call-start = ((), (), s32[]{:S(2)}) async-start(), calls=%async_computation.11 | async-start | bytes 1081344 | tf_op jit(solution)/shard_map/reduce_scatter | solution.py:230
  459.0 365.5 %reduce-scatter.11.cloned.1.call-start = ((), (), s32[]{:S(2)}) async-start(), calls=%async_computation.10 | async-start | bytes 3244032 | tf_op jit(solution)/shard_map/reduce_scatter | solution.py:230
  464.6 509.3 %reduce-scatter.17.cloned.1.call-start = ((), (), s32[]{:S(2)}) async-start(), calls=%async_computation.13 | async-start | bytes 4325376 | tf_op jit(solution)/shard_map/reduce_scatter | solution.py:230
  474.4 648.3 %reduce-scatter.15.cloned.1.call-start = ((), (), s32[]{:S(2)}) async-start(), calls=%async_computation.12 | async-start | bytes 4325376 | tf_op jit(solution)/shard_map/reduce_scatter | solution.py:230
  489.7 2.4 copy-start.1
  (1 other events, 1.1 us)
Sparse Core Ops, SparseCore 0:
  11.5 57.7 all-gather.4
  72.2 55.4 all-gather.6
  130.6 56.1 all-gather.8
  311.7 130.1 reduce-scatter.8
  455.8 130.2 reduce-scatter.18
  588.1 131.9 reduce-scatter.12
  726.5 97.9 reduce-scatter.10
  826.8 146.9 reduce-scatter.16
  976.2 146.4 reduce-scatter.14

commit v2 on v1

--- a/solution.py
+++ b/solution.py
@@ -38,17 +38,12 @@
     return lax.dot_general(a, b, (((0,), (0,)), ((), ())), preferred_element_type=F32)
 
 
-def window_base(first):
-    return jnp.maximum((first - (MOST - 1)) // MOST, 0) * MOST
-
-
 def summary_bias(first, span, docs_ref):
-    base = pl.multiple_of(window_base(first), MOST)
     index = first + span
     row = lax.broadcasted_iota(jnp.int32, (PSPANS, S), 0)
     prompt = jnp.where(row < index, 0.0, MASKED)
-    wrow = base + lax.broadcasted_iota(jnp.int32, (WIN, S), 0)
-    same = docs_ref[pl.ds(base, WIN), :] == docs_ref[pl.ds(index, 1), :]
+    wrow = first - MOST + lax.broadcasted_iota(jnp.int32, (WIN, S), 0)
+    same = docs_ref[pl.ds(pl.multiple_of(first, 8), WIN), :] == docs_ref[pl.ds(index + MOST, 1), :]
     window = jnp.where(same & (wrow >= PSPANS) & (wrow < index), 0.0, MASKED)
     return jnp.concatenate([prompt, window], axis=0).astype(F32)
 
@@ -130,14 +125,263 @@
         dsum_ref[:, vcols] += dvals[S:]
 
 
-def attention_kernel(spans, qkv_ref, psum_ref, wsum_ref, docs_ref, attn_t_ref, probs_ref):
-    first = (lax.axis_index("seq") * lax.axis_size("head") + lax.axis_index("head")) * spans
+MESH = pl.DeviceIdType.MESH
+BOTH = ("seq", "head")
+
+
+class Place:
+    def __init__(self):
+        seq, self.z = lax.axis_index("seq"), lax.axis_index("head")
+        self.side = math.isqrt(lax.axis_size("seq") // 2)
+        self.deep = lax.axis_size("head")
+        self.devices = lax.axis_size("seq") * self.deep
+        self.c = lax.rem(seq, 2)
+        self.x = lax.rem(seq // 2, self.side)
+        self.y = seq // 2 // self.side
+        self.me = seq * self.deep + self.z
+
+    def seq(self, y, x, c):
+        return (y * self.side + x) * 2 + c
+
+    def along(self, axis, step):
+        n, turn = self.side, self.c if axis == 0 else 1 - self.c
+        return lax.rem(self.y + turn * step, n), lax.rem(self.x + (1 - turn) * step, n)
+
+    def sibling(self):
+        return (self.seq(self.y, self.x, 1 - self.c), self.z)
+
+    def peers(self, axis):
+        if axis == "z":
+            seq = self.seq(self.y, self.x, self.c)
+            return [(seq, lax.rem(self.z + d, self.deep)) for d in range(1, self.deep)]
+        return [(self.seq(*self.along(axis, d), self.c), self.z) for d in range(1, self.side)]
+
+    def greet(self):
+        barrier = pltpu.get_barrier_semaphore()
+        others = [self.sibling(), *self.peers(0), *self.peers(1), *self.peers("z")]
+        for other in others:
+            pl.semaphore_signal(barrier, inc=1, device_id=other, device_id_type=MESH)
+        pl.semaphore_wait(barrier, len(others))
+
+
+class Wires:
+    def __init__(self, send, recv):
+        self.send, self.recv, self.used, self.sent = send, recv, 0, []
+
+    def copy(self, src, dst, device):
+        i = self.used
+        self.used += 1
+        move = pltpu.make_async_remote_copy(
+            src_ref=src, dst_ref=dst, send_sem=self.send.at[i], recv_sem=self.recv.at[i],
+            device_id=device, device_id_type=MESH,
+        )
+        move.start()
+        self.sent.append(move)
+        return move
+
+    def local(self, src, dst):
+        i = self.used
+        self.used += 1
+        move = pltpu.make_async_copy(src, dst, self.send.at[i])
+        move.start()
+        return move
+
+    def finish(self):
+        for move in self.sent:
+            move.wait_send()
+
+
+def copies_of_gather(side, deep, with_z):
+    return 1 + (deep - 1 if with_z else 0) + (side - 1) + (side - 1) * side + side * side
+
+
+class Gather:
+    def __init__(self, wires, place, shard, full, rows, with_z):
+        self.w, self.p, self.full, self.shard = wires, place, full, shard
+        self.rows, self.with_z = rows, with_z
+        self.group = rows * place.deep if with_z else rows
+
+    def block(self, y, x):
+        start = self.p.seq(y, x, self.p.c) * self.group
+        return self.full.at[pl.ds(pl.multiple_of(start, self.group), self.group)]
+
+    def step0(self):
+        p = self.p
+        start = pl.multiple_of(p.me * self.rows, self.rows) if self.with_z else p.seq(p.y, p.x, p.c) * self.rows
+        own = self.full.at[pl.ds(start, self.rows)]
+        self.moves = [self.w.copy(self.shard, own, d) for d in p.peers("z")] if self.with_z else []
+        self.placed = self.w.local(self.shard, own)
+
+    def _next(self, sources, axis, fresh):
+        for move in self.moves:
+            move.wait_recv()
+        p = self.p
+        self.moves = []
+        if axis is not None:
+            self.moves = [self.w.copy(self.block(*s), self.block(*s), d) for d in p.peers(axis) for s in sources]
+        self.across += [self.w.copy(self.block(*s), self.block(*s), p.sibling()) for s in fresh]
+
+    def step1(self):
+        self.placed.wait()
+        self.across = []
+        here = [(self.p.y, self.p.x)]
+        self._next(here, 0, here)
+
+    def _line(self, step):
+        p, n = self.p, self.p.side
+        mine = [p.along(0, d) for d in range(n)]
+        if step == 0:
+            return mine
+        y1, x1 = p.along(1, step)
+        turn = 1 - p.c
+        return [(turn * y1 + (1 - turn) * y, turn * x + (1 - turn) * x1) for y, x in mine]
+
+    def step2(self):
+        line = self._line(0)
+        self._next(line, 1, line[1:])
+
+    def step3(self):
+        self._next([], None, [s for e in range(1, self.p.side) for s in self._line(e)])
+
+    def step4(self):
+        for move in self.across:
+            move.wait_recv()
+
+
+def layer_norm_rows(values, gain, shift):
+    mean = jnp.mean(values, axis=-1, keepdims=True)
+    centred = values - mean
+    variance = jnp.mean(centred * centred, axis=-1, keepdims=True)
+    return centred * lax.rsqrt(variance + EPS) * gain + shift
+
+
+def spread_small(gathered, devices):
+    width = D // devices
+    table = gathered.reshape(devices * 8, LANES).astype(BF16)
+    pick = lax.broadcasted_iota(jnp.int32, (LANES, D), 0) == lax.broadcasted_iota(jnp.int32, (LANES, D), 1) % width
+    every = nn(table, jnp.where(pick, 1.0, 0.0).astype(BF16))
+    owner = lax.broadcasted_iota(jnp.int32, (devices * 8, D), 0) // 8
+    column = lax.broadcasted_iota(jnp.int32, (devices * 8, D), 1) // width
+    return jnp.sum(jnp.where(owner == column, every, 0.0).reshape(devices, 8, D), axis=0)
+
+
+def forward_kernel(
+    with_z,
+    x_ref, wq_ref, wo_ref, wu_ref, wd_ref, small_ref, docs_ref,
+    act_ref, qkv_ref, probs_ref, attn_t_ref, psum_ref, wsum_ref,
+    qkv_mat, out_mat, up_mat, down_mat, gains_ref,
+    small_all, own_sums, sums_all, send, recv,
+):
+    place = Place()
+    wires = Wires(send, recv)
+    tok = x_ref.shape[0]
+    spans = tok // S
+    first = place.me * spans
+    small = Gather(wires, place, small_ref, small_all, 1, True)
+    gathers = [
+        Gather(wires, place, shard, full, shard.shape[0], with_z)
+        for shard, full in ((wq_ref, qkv_mat), (wo_ref, out_mat), (wd_ref, down_mat), (wu_ref, up_mat))
+    ]
+    g_qkv, g_out, g_down, g_up = gathers
+    place.greet()
+    small.step0()
+    for g in gathers:
+        g.step0()
+    small.step1()
+    g_qkv.step1()
+    small.step2()
+    g_qkv.step2()
+    small.step3()
+    g_qkv.step3()
+    g_out.step1()
+    g_down.step1()
+    small.step4()
+    gains_ref[...] = spread_small(small_all[...], place.devices)
+
+    def norm(i, carry):
+        rows = pl.ds(pl.multiple_of(i * S, S), S)
+        normed = layer_norm_rows(x_ref[rows, :].astype(F32), gains_ref[0:1, :], gains_ref[1:2, :])
+        act_ref[rows, :] = normed.astype(BF16)
+        return carry
+
+    lax.fori_loop(0, spans, norm, 0)
+    g_qkv.step4()
+    for part in (1, 2):
+        cols = slice(part * D, (part + 1) * D)
+        block = nn(act_ref[...], qkv_mat[:, cols]).astype(BF16)
+        qkv_ref[:, cols] = block
+        mean = jnp.sum(block.astype(F32).reshape(spans, S, D), axis=1) * (1.0 / S)
+        own_sums[0, :, (part - 1) * D : part * D] = mean.astype(BF16)
+    sums = Gather(wires, place, own_sums, sums_all, 1, True)
+    sums.step0()
+    qkv_ref[:, :D] = nn(act_ref[...], qkv_mat[:, :D]).astype(BF16)
+    sums.step1()
+    g_up.step1()
+    sums.step2()
+    sums.step3()
+    g_out.step2()
+    g_down.step2()
+    sums.step4()
+    for i in range(PSPANS // MOST):
+        two = sums_all[pl.ds(2 * i, 2)].astype(F32)
+        psum_ref[MOST * i : MOST * (i + 1), :] = two.reshape(MOST, 2 * D).astype(BF16)
+    before = sums_all[pl.ds(lax.rem(place.me + place.devices - 2, place.devices), 1)].astype(F32)
+    last = sums_all[pl.ds(lax.rem(place.me + place.devices - 1, place.devices), 1)].astype(F32)
+    here = sums_all[pl.ds(place.me, 1)].astype(F32)
+    wsum_ref[:MOST, :] = jnp.concatenate([before, last], axis=0).reshape(MOST, 2 * D).astype(BF16)
+    wsum_ref[MOST:, :] = jnp.concatenate([here, jnp.zeros_like(here)], axis=0).reshape(MOST, 2 * D).astype(BF16)
 
     def step(span, carry):
         attend_span(span, first, qkv_ref, psum_ref, wsum_ref, docs_ref, attn_t_ref, probs_ref)
         return carry
 
-    lax.fori_loop(0, spans, step, 0)
+    lax.fori_loop(0, spans // 2, step, 0)
+    g_out.step3()
+    g_down.step3()
+    g_up.step2()
+    lax.fori_loop(spans // 2, spans, step, 0)
+    g_up.step3()
+    for g in (g_out, g_down, g_up):
+        g.step4()
+    wires.finish()
+
+
+def forward(x, wq, wo, wu, wd, small, docs, with_z):
+    tok = x.shape[0]
+    spans = tok // S
+    deep = lax.axis_size("head")
+    side = math.isqrt(lax.axis_size("seq") // 2)
+    devices = 2 * side * side * deep
+    whole = pl.BlockSpec(memory_space=VMEM)
+    n = copies_of_gather(side, deep, True) * 6
+    shape = jax.ShapeDtypeStruct
+    return pl.pallas_call(
+        functools.partial(forward_kernel, with_z),
+        out_shape=(
+            shape((tok, D), BF16),
+            shape((tok, 3 * D), BF16),
+            shape((spans * PAIRS, KEYS, 2 * S), BF16),
+            shape((D, tok), BF16),
+            shape((PSPANS, 2 * D), BF16),
+            shape((WIN, 2 * D), BF16),
+            shape((D, 3 * D), BF16),
+            shape((D, D), BF16),
+            shape((4 * D, D), BF16),
+            shape((4 * D, D), BF16),
+            shape((8, D), F32),
+        ),
+        in_specs=[whole] * 7,
+        out_specs=(whole,) * 11,
+        scratch_shapes=[
+            pltpu.VMEM((devices, 8, LANES), F32),
+            pltpu.VMEM((1, spans, 2 * D), BF16),
+            pltpu.VMEM((devices, spans, 2 * D), BF16),
+            pltpu.SemaphoreType.DMA((n,)),
+            pltpu.SemaphoreType.DMA((n,)),
+        ],
+        compiler_params=pltpu.CompilerParams(vmem_limit_bytes=VMEM_LIMIT, collective_id=0, has_side_effects=True),
+        name="gather_and_attend",
+    )(x, wq, wo, wu, wd, small, docs)
 
 
 def attention_back_kernel(
@@ -152,23 +396,6 @@
         return carry
 
     lax.fori_loop(0, spans, step, 0)
-
-
-def attention(qkv, psum, wsum, docs):
-    tok = qkv.shape[0]
-    spans = tok // S
-    whole = pl.BlockSpec(memory_space=VMEM)
-    return pl.pallas_call(
-        functools.partial(attention_kernel, spans),
-        out_shape=(
-            jax.ShapeDtypeStruct((D, tok), BF16),
-            jax.ShapeDtypeStruct((spans * PAIRS, KEYS, 2 * S), BF16),
-        ),
-        in_specs=[whole] * 4,
-        out_specs=(whole, whole),
-        compiler_params=pltpu.CompilerParams(vmem_limit_bytes=VMEM_LIMIT),
-        name="attention",
-    )(qkv, psum, wsum, docs)
 
 
 def attention_back(qkv, psum, wsum, probs, dattn):
@@ -200,9 +427,6 @@
     return jax.nn.gelu(values, approximate=True)
 
 
-BOTH = ("seq", "head")
-
-
 def split_parts(weight):
     rows = weight.shape[0]
     return weight.reshape(rows, H, 3, HD).transpose(0, 2, 1, 3).reshape(rows, 3 * D)
@@ -220,32 +444,25 @@
     me = lax.axis_index("seq") * lax.axis_size("head") + lax.axis_index("head")
     first = me * spans
     grad_scale = 1.0 / math.sqrt(tok * devices)
-    docs = jnp.concatenate([jnp.full((PSPANS,), -1, jnp.int32), span_doc])
+    docs = jnp.concatenate([jnp.full((PSPANS + MOST,), -1, jnp.int32), span_doc, jnp.full((MOST,), -1, jnp.int32)])
     docs = jnp.broadcast_to(docs[:, None], (docs.shape[0], S))
-
-    def gather(x, axis=0):
-        return lax.all_gather(x, BOTH, axis=axis, tiled=True)
 
     def scatter(x, axis=0):
         return lax.psum_scatter(x, BOTH, scatter_dimension=axis, tiled=True)
 
-    qkv_mat = gather(split_parts(w_qkv))
-    out_mat = gather(w_out)
-    up_mat = gather(w_up.T)
-    down_mat = gather(w_down)
-    small = gather(jnp.stack([gain_one, shift_one, gain_two, shift_two]), 1).astype(F32)
+    with_z = w_qkv.shape[0] % 16 == 0
+    weights = (split_parts(w_qkv), w_out, w_up.T, w_down)
+    if not with_z:
+        weights = tuple(lax.all_gather(w, "head", axis=0, tiled=True) for w in weights)
+    small = jnp.stack([gain_one, shift_one, gain_two, shift_two]).astype(F32)
+    small = jnp.pad(small, ((0, 4), (0, LANES - small.shape[1])))[None]
+    act_one, qkv, probs, attn_t, psum, wsum, qkv_mat, out_mat, up_mat, down_mat, gains = forward(
+        tokens, *weights, small, docs, with_z
+    )
     x_rows = tokens.astype(F32)
-    norm_one, back_one = jax.vjp(layer_norm, x_rows, small[0], small[1])
-    act_one = norm_one.astype(BF16)
-    qkv = jnp.dot(act_one, qkv_mat, preferred_element_type=F32).astype(BF16)
-    span_kv = jnp.mean(qkv[:, D:].astype(F32).reshape(spans, S, 2 * D), axis=1).astype(BF16)
-    all_kv = gather(span_kv)
-    base = window_base(first)
-    psum = all_kv[:PSPANS]
-    wsum = lax.dynamic_slice_in_dim(all_kv, base, WIN, 0)
-    attn_t, probs = attention(qkv, psum, wsum, docs)
+    _, back_one = jax.vjp(layer_norm, x_rows, gains[0], gains[1])
     resid = x_rows + tn(attn_t, out_mat)
-    norm_two, back_two = jax.vjp(layer_norm, resid, small[2], small[3])
+    norm_two, back_two = jax.vjp(layer_norm, resid, gains[2], gains[3])
     act_two = norm_two.astype(BF16)
     hidden = nt(act_two, up_mat)
     acted, back_gelu = jax.vjp(gelu_tanh, hidden)
@@ -260,8 +477,8 @@
     grad_out = nn(attn_t, d_branch)
     d_attn = nt(d_branch, out_mat).astype(BF16)
     dq, dkv, dsum = attention_back(qkv, psum, wsum, probs, d_attn)
-    flat = jnp.zeros((all_kv.shape[0], 2 * D), F32)
-    flat = lax.dynamic_update_slice_in_dim(flat, dsum[PSPANS:], base, 0)
+    flat = jnp.zeros((devices * spans + 2 * MOST, 2 * D), F32)
+    flat = lax.dynamic_update_slice_in_dim(flat, dsum[PSPANS:], first, 0)[MOST:-MOST]
     row = jnp.arange(flat.shape[0])[:, None]
     flat = jnp.where(row < PSPANS, 0.0, flat)
     flat = flat.at[:PSPANS].add(dsum[:PSPANS])

time: 1130 us -> 961 us (0.85)
  blocking collectives: 214 us -> 0 us
  Pallas kernels: 38 us -> 92.5 us
    all_gather x3 -> x0, blocking collectives: 214 us -> none  [gather(): return lax.all_gather(x, BOTH, axis=axis, tiled=True)]
    pallas_call x1, Pallas kernels: 17.7 us -> 72.1 us  [forward(): pl.pallas_call(functools.partial(forward_kernel, with_z), out_shape=(shap...]
    unnamed x10 -> x7, waiting for transfers between devices: 88.5 us -> 86.7 us
  transfers between devices with their start and end apart: 9 -> 6, of which waited for: 6 -> 6; matrix products, arithmetic and copies ran while one was open for 6% -> 5% of each run, Pallas kernels for 2% -> 0%
where the time goes in v2:
time: 961 us; the launch traced here: 960 us
  waiting for transfers between devices  751 us (78%)
  Pallas kernels  92.5 us (10%)
  matrix products  54.6 us (6%)
  local copies, waits for them, and re-layouts  24.9 us (3%)
  other arithmetic  22.1 us (2%)
  between operations  14.5 us (2%)
    reduce_scatter x5, waiting for transfers between devices, scatter(): return lax.psum_scatter(x, BOTH, scatter_dimension=axis, tiled=True)  665 us
    unnamed x7, waiting for transfers between devices  86.7 us
    pallas_call x1, Pallas kernels, forward(): pl.pallas_call(functools.partial(forward_kernel, with_z), out_shape=(shap...  72.1 us
    dot_general x4, matrix products, tn(): lax.dot_general(a, b, (((0,), (0,)), ((), ())), preferred_element_type=F32)  24.1 us
    pallas_call x1, Pallas kernels, attention_back(): pl.pallas_call(functools.partial(attention_back_kernel, spans), out_shape...  20.5 us
  transfers between devices with their start and end apart: 6, of which 6 were waited for; matrix products, arithmetic and copies ran while one was open for 5% of the time, Pallas kernels for 0%

profile of v2, /device:TPU:0, one launch (start us, length us, event | category | flops | bytes accessed | tf_op | source)
XLA Modules:
  0.0 960.4 jit_solution(8726040513637574834)
XLA Ops:
  13.5 72.1 %gather_and_attend.1 = (bf16[1024,512]{1,0:T(8,128)(2,1)}, bf16[1024,1536]{1,0:T(8,128)(2,1)}, bf16[32,288,256]{2,1,0:T(8,128)(2,1)}, bf16[512,1024]{1,0:T(8,128...) custom-call(bf16[1024,512]{1,0:T(8,128)(2,1)} %x_ref.1, ...), custom_call_target="tpu_custom_call" | custom-call | tf_op jit(solution)/shard_map/gather_and_attend/pallas_call | solution.py:358
  90.1 2.7 fusion.43
  92.8 7.6 fusion.6
  100.4 3.6 fusion.48
  104.1 2.9 copy.50
  107.0 2.4 multiply_reduce_fusion
  114.0 20.5 %attention_back.1 = (bf16[1024,512]{1,0:T(8,128)(2,1)}, f32[1024,1024]{1,0:T(8,128)}, f32[160,1024]{1,0:T(8,128)}) custom-call(bf16[1024,1536]{1,0:T(8,128)(2,1)} %get-tuple-element.41.qkv_ref, bf16[128,1024]{1,0:T(8,128)(2,1)} %get-tuple-element.42.psum_ref, bf16[32,1024]{1,0:T(8,128)(2,1)} %get-tuple-element.43.wsum_ref, ...), custom_call_target="tpu_custom_call" | custom-call | tf_op jit(solution)/shard_map/attention_back/pallas_call | solution.py:405
  137.0 134.0 %reduce-scatter.9.cloned.1.call-done = bf16[8,1024]{1,0:T(8,128)(2,1)} async-done(((bf16[256,1024]{1,0:T(8,128)(2,1)}), bf16[8,1024]{1,0:T(8,128)(2,1)}) %reduce-scatter.9.cloned.1.call-update) | async-done | bytes 16400 | tf_op jit(solution)/shard_map/reduce_scatter | solution.py:451
  271.7 2.9 fusion.10
  274.7 3.2 fusion.49
  277.8 2.9 copy.51
  284.9 3.3 fusion.50
  288.5 5.7 fusion.19
  294.3 9.5 fusion.44
  303.8 6.9 fusion.42
  310.7 8.4 add_convert_fusion
  319.1 2.4 copy.55
  321.6 4.1 add_add_fusion.2
  325.7 2.9 copy.56
  328.6 86.6 %reduce-scatter.19.cloned.1.call-done = f32[16,4]{1,0:T(8,128)} async-done(((f32[512,4]{1,0:T(8,128)}), f32[16,4]{1,0:T(8,128)}) %reduce-scatter.19.cloned.1.call-update) | async-done | bytes 272
  416.5 133.0 %reduce-scatter.13.cloned.1.call-done = f32[16,512]{1,0:T(8,128)} async-done(((f32[512,512]{1,0:T(8,128)}), f32[16,512]{1,0:T(8,128)}) %reduce-scatter.13.cloned.1.call-update) | async-done | bytes 32784 | tf_op jit(solution)/shard_map/reduce_scatter | solution.py:451
  550.8 102.9 %reduce-scatter.11.cloned.1.call-done = f32[16,1536]{1,0:T(8,128)} async-done(((f32[512,1536]{1,0:T(8,128)}), f32[16,1536]{1,0:T(8,128)}) %reduce-scatter.11.cloned.1.call-update) | async-done | bytes 98320 | tf_op jit(solution)/shard_map/reduce_scatter | solution.py:451
  655.6 147.5 %reduce-scatter.17.cloned.1.call-done = f32[64,512]{1,0:T(8,128)} async-done(((f32[2048,512]{1,0:T(8,128)}), f32[64,512]{1,0:T(8,128)}) %reduce-scatter.17.cloned.1.call-update) | async-done | bytes 131088 | tf_op jit(solution)/shard_map/reduce_scatter | solution.py:451
  804.7 147.4 %reduce-scatter.15.cloned.1.call-done = f32[64,512]{1,0:T(8,128)} async-done(((f32[2048,512]{1,0:T(8,128)}), f32[64,512]{1,0:T(8,128)}) %reduce-scatter.15.cloned.1.call-update) | async-done | bytes 131088 | tf_op jit(solution)/shard_map/reduce_scatter | solution.py:451
  (101 shorter events, 30.8 us)
Async XLA Ops:
  7.2 3.5 copy-start.7
  7.2 263.8 %reduce-scatter.9.cloned.1.call-start = ((), (), s32[]{:S(2)}) async-start(), calls=%async_computation.6 | async-start | bytes 540672 | tf_op jit(solution)/shard_map/reduce_scatter | solution.py:451
  9.1 2.9 copy-start.15
  9.1 3.0 copy-start.11
  9.1 3.0 copy-start.12
  9.1 3.0 copy-start.13
  9.1 3.0 copy-start.14
  88.5 1.6 copy-start.17
  90.1 2.7 copy-start.8
  90.1 2.7 copy-start.16
  92.8 7.6 copy-start.20
  100.4 3.7 copy-start.21
  107.0 2.4 copy-start.2
  110.6 1.7 copy-start.10
  136.8 278.4 %reduce-scatter.19.cloned.1.call-start = ((), (), s32[]{:S(2)}) async-start(), calls=%async_computation.11 | async-start | bytes 270336
  271.7 3.0 copy-start.18
  271.7 3.0 copy-start.19
  274.6 3.2 copy-start.5
  280.7 2.3 copy-start
  284.9 264.6 %reduce-scatter.13.cloned.1.call-start = ((), (), s32[]{:S(2)}) async-start(), calls=%async_computation.8 | async-start | bytes 1081344 | tf_op jit(solution)/shard_map/reduce_scatter | solution.py:451
  288.3 365.5 %reduce-scatter.11.cloned.1.call-start = ((), (), s32[]{:S(2)}) async-start(), calls=%async_computation.7 | async-start | bytes 3244032 | tf_op jit(solution)/shard_map/reduce_scatter | solution.py:451
  294.2 508.9 %reduce-scatter.17.cloned.1.call-start = ((), (), s32[]{:S(2)}) async-start(), calls=%async_computation.10 | async-start | bytes 4325376 | tf_op jit(solution)/shard_map/reduce_scatter | solution.py:451
  303.8 648.2 %reduce-scatter.15.cloned.1.call-start = ((), (), s32[]{:S(2)}) async-start(), calls=%async_computation.9 | async-start | bytes 4325376 | tf_op jit(solution)/shard_map/reduce_scatter | solution.py:451
  319.1 2.4 copy-start.1
  (4 other events, 4.8 us)
Sparse Core Ops, SparseCore 0:
  136.9 134.0 reduce-scatter.8
  285.0 130.1 reduce-scatter.18
  417.4 131.9 reduce-scatter.12
  555.6 98.0 reduce-scatter.10
  655.9 147.1 reduce-scatter.16
  805.3 146.6 reduce-scatter.14

commit v3 on v2

--- a/solution.py
+++ b/solution.py
@@ -246,13 +246,6 @@
     def step4(self):
         for move in self.across:
             move.wait_recv()
-
-
-def layer_norm_rows(values, gain, shift):
-    mean = jnp.mean(values, axis=-1, keepdims=True)
-    centred = values - mean
-    variance = jnp.mean(centred * centred, axis=-1, keepdims=True)
-    return centred * lax.rsqrt(variance + EPS) * gain + shift
 
 
 def spread_small(gathered, devices):
@@ -300,8 +293,8 @@
 
     def norm(i, carry):
         rows = pl.ds(pl.multiple_of(i * S, S), S)
-        normed = layer_norm_rows(x_ref[rows, :].astype(F32), gains_ref[0:1, :], gains_ref[1:2, :])
-        act_ref[rows, :] = normed.astype(BF16)
+        xhat, _ = normed_parts(x_ref[rows, :].astype(F32))
+        act_ref[rows, :] = (xhat * gains_ref[0:1, :] + gains_ref[1:2, :]).astype(BF16)
         return carry
 
     lax.fori_loop(0, spans, norm, 0)
@@ -384,47 +377,373 @@
     )(x, wq, wo, wu, wd, small, docs)
 
 
-def attention_back_kernel(
-    spans, qkv_ref, psum_ref, wsum_ref, probs_ref, dattn_ref, dq_ref, dkv_ref, dsum_ref
+def normed_parts(values):
+    mean = jnp.mean(values, axis=-1, keepdims=True)
+    centred = values - mean
+    inverse = lax.rsqrt(jnp.mean(centred * centred, axis=-1, keepdims=True) + EPS)
+    return centred * inverse, inverse
+
+
+def norm_back(dnormed, xhat, inverse, gain):
+    grown = dnormed * gain
+    along = jnp.mean(grown * xhat, axis=-1, keepdims=True)
+    return (grown - jnp.mean(grown, axis=-1, keepdims=True) - xhat * along) * inverse
+
+
+def gelu_parts(h):
+    square = h * h
+    t = jnp.tanh(0.7978845608 * (h + 0.044715 * h * square))
+    half = 0.5 * (1.0 + t)
+    slope = 0.7978845608 * (1.0 + 3 * 0.044715 * square)
+    return h * half, half + 0.5 * h * (1.0 - t * t) * slope
+
+
+TILE = 256
+CHUNK = 256
+
+
+def dense_kernel(
+    x_ref, cot_ref, attn_t_ref, out_mat, up_mat, down_mat, gains_ref,
+    out_ref, dresid_ref, dattn_ref, gdown_ref, gup_ref, gout_ref, small_ref,
+    resid_ref, act_ref, acted_ref, dhid_ref, branch_ref,
 ):
+    tok = x_ref.shape[0]
+    hidden_size = up_mat.shape[0]
+
+    def residual(i, carry):
+        rows = pl.ds(pl.multiple_of(i * TILE, TILE), TILE)
+        resid = x_ref[rows, :].astype(F32) + tn(attn_t_ref[:, rows], out_mat[...])
+        resid_ref[rows, :] = resid
+        xhat, _ = normed_parts(resid)
+        act_ref[rows, :] = (xhat * gains_ref[2:3, :] + gains_ref[3:4, :]).astype(BF16)
+        return carry
+
+    lax.fori_loop(0, tok // TILE, residual, 0)
+
+    def feed(i, carry):
+        part = pl.ds(pl.multiple_of(i * CHUNK, CHUNK), CHUNK)
+        acted, slope = gelu_parts(nt(act_ref[...], up_mat[part, :]))
+        acted = acted.astype(BF16)
+        acted_ref[:, part] = acted
+        dhid = (nt(cot_ref[...], down_mat[part, :]) * slope).astype(BF16)
+        dhid_ref[:, part] = dhid
+        gdown_ref[part, :] = tn(acted, cot_ref[...]).astype(BF16)
+        gup_ref[part, :] = tn(dhid, act_ref[...]).astype(BF16)
+        return carry
+
+    lax.fori_loop(0, hidden_size // CHUNK, feed, 0)
+    small_ref[...] = jnp.zeros_like(small_ref)
+
+    def finish(i, carry):
+        rows = pl.ds(pl.multiple_of(i * TILE, TILE), TILE)
+        resid = resid_ref[rows, :]
+        out_ref[rows, :] = (resid + nn(acted_ref[rows, :], down_mat[...])).astype(BF16)
+        dnormed = nn(dhid_ref[rows, :], up_mat[...])
+        xhat, inverse = normed_parts(resid)
+        small_ref[2:3, :] += jnp.sum(dnormed * xhat, axis=0, keepdims=True)
+        small_ref[3:4, :] += jnp.sum(dnormed, axis=0, keepdims=True)
+        dresid = cot_ref[rows, :].astype(F32) + norm_back(dnormed, xhat, inverse, gains_ref[2:3, :])
+        dresid_ref[rows, :] = dresid
+        branch = dresid.astype(BF16)
+        branch_ref[rows, :] = branch
+        dattn_ref[rows, :] = nt(branch, out_mat[...]).astype(BF16)
+        return carry
+
+    lax.fori_loop(0, tok // TILE, finish, 0)
+    gout_ref[...] = nn(attn_t_ref[...], branch_ref[...]).astype(BF16)
+
+
+def dense(x, cotangent, attn_t, out_mat, up_mat, down_mat, gains):
+    tok = x.shape[0]
+    hidden_size = up_mat.shape[0]
+    whole = pl.BlockSpec(memory_space=VMEM)
+    shape = jax.ShapeDtypeStruct
+    return pl.pallas_call(
+        dense_kernel,
+        out_shape=(
+            shape((tok, D), BF16),
+            shape((tok, D), F32),
+            shape((tok, D), BF16),
+            shape((hidden_size, D), BF16),
+            shape((hidden_size, D), BF16),
+            shape((D, D), BF16),
+            shape((8, D), F32),
+        ),
+        in_specs=[whole] * 7,
+        out_specs=(whole,) * 7,
+        scratch_shapes=[
+            pltpu.VMEM((tok, D), F32),
+            pltpu.VMEM((tok, D), BF16),
+            pltpu.VMEM((tok, hidden_size), BF16),
+            pltpu.VMEM((tok, hidden_size), BF16),
+            pltpu.VMEM((tok, D), BF16),
+        ],
+        compiler_params=pltpu.CompilerParams(vmem_limit_bytes=VMEM_LIMIT),
+        name="dense",
+    )(x, cotangent, attn_t, out_mat, up_mat, down_mat, gains)
+
+
+def add_into(held, index, others):
+    total = held[index].astype(F32)
+    for other in others:
+        total = total + other.astype(F32)
+    held[index] = total.astype(held.dtype)
+
+
+class Scatter:
+    def __init__(self, wires, place, grads, held, hop1, hop2, hopz):
+        self.w, self.p, self.grads, self.held = wires, place, grads, held
+        self.hop1, self.hop2, self.hopz = hop1, hop2, hopz
+        self.group = held.shape[1]
+
+    def at(self, turn, d, e):
+        p, n = self.p, self.p.side
+        y = lax.rem(p.y + turn * d + (1 - turn) * e, n)
+        x = lax.rem(p.x + turn * e + (1 - turn) * d, n)
+        return y * n + x
+
+    def rows_of(self, j, core):
+        return pl.ds(pl.multiple_of((2 * j + core) * self.group, self.group), self.group)
+
+    def order(self):
+        n = self.p.side
+        return [(d, e) for d in [*range(1, n), 0] for e in range(n)]
+
+    def step0(self):
+        p = self.p
+        self.moves = {}
+        for d, e in self.order():
+            j = self.at(1 - p.c, d, e)
+            self.moves[d, e] = self.w.copy(self.grads.at[self.rows_of(j, 1 - p.c)], self.held.at[j], p.sibling())
+
+    def step1(self):
+        p, came = self.p, self.moves
+        self.moves = {}
+        peers = p.peers(0)
+        for d, e in self.order():
+            j = self.at(p.c, d, e)
+            came[d, e].wait_recv()
+            add_into(self.held, j, [self.grads[self.rows_of(j, p.c)]])
+            if d:
+                self.moves[d, e] = self.w.copy(self.held.at[j], self.hop1.at[d - 1, e], peers[d - 1])
+
+    def step2(self):
+        p, n, came = self.p, self.p.side, self.moves
+        self.moves = []
+        peers = p.peers(1)
+        for e in [*range(1, n), 0]:
+            j = self.at(p.c, 0, e)
+            for d in range(1, n):
+                came[d, e].wait_recv()
+            add_into(self.held, j, [self.hop1[d - 1, e] for d in range(1, n)])
+            if e:
+                self.moves.append(self.w.copy(self.held.at[j], self.hop2.at[e - 1], peers[e - 1]))
+
+    def step3(self):
+        p = self.p
+        for move in self.moves:
+            move.wait_recv()
+        self.mine = self.at(p.c, 0, 0)
+        add_into(self.held, self.mine, [self.hop2[e - 1] for e in range(1, p.side)])
+        self.moves = []
+        if self.hopz is not None:
+            self.unit = self.group // p.deep
+            for d, other in enumerate(p.peers("z"), 1):
+                self.moves.append(self.w.copy(self.held.at[self.mine, self.unit_rows(d)], self.hopz.at[d - 1], other))
+
+    def unit_rows(self, d):
+        p = self.p
+        return pl.ds(pl.multiple_of(lax.rem(p.z + d, p.deep) * self.unit, self.unit), self.unit)
+
+    def step4(self):
+        if self.hopz is None:
+            return self.held[self.mine].astype(F32)
+        total = self.held[self.mine, self.unit_rows(0)].astype(F32)
+        for d, move in enumerate(self.moves):
+            move.wait_recv()
+            total = total + self.hopz[d].astype(F32)
+        return total
+
+
+def scatter_scratch(side, deep, unit, tail, with_z):
+    group = deep * unit
+    shapes = [(side * side, group), (side - 1, side, group), (side - 1, group)]
+    if with_z:
+        shapes.append((deep - 1, unit))
+    return [pltpu.VMEM((*shape, *tail), BF16) for shape in shapes]
+
+
+class Total:
+    def __init__(self, wires, place, sums, came):
+        self.w, self.p, self.sums, self.came = wires, place, sums, came
+        self.slot = 0
+
+    def send(self, level):
+        p = self.p
+        peers = [[p.sibling()], p.peers(0), p.peers(1), p.peers("z")][level]
+        self.moves = []
+        for peer in peers:
+            self.moves.append(self.w.copy(self.sums.at[level], self.came.at[self.slot], peer))
+            self.slot += 1
+
+    def take(self, level):
+        total = self.sums[level]
+        for i, move in enumerate(self.moves):
+            move.wait_recv()
+            total = total + self.came[self.slot - len(self.moves) + i]
+        self.sums[level + 1] = total
+
+
+def backward_kernel(
+    with_z, grad_scale,
+    x_ref, act_ref, qkv_ref, probs_ref, psum_ref, wsum_ref, qkv_mat, gains_ref,
+    dattn_ref, dresid_ref, gdown_ref, gup_ref, gout_ref, small_ref,
+    dtok_ref, wqkv_ref, wout_ref, wup_ref, wdown_ref, total_ref,
+    dqkv_ref, dkv_ref, dsum_ref, dsums_ref, gq_ref, gkv_ref, dnorm_ref, sums_ref, came_ref, send, recv, *held,
+):
+    place = Place()
+    wires = Wires(send, recv)
+    tok = x_ref.shape[0]
+    spans = tok // S
+    per = 4 if with_z else 3
+    held = list(held)
+
+    def scatter(grads, z):
+        count = 4 if z else 3
+        parts = [held.pop(0) for _ in range(count)]
+        return Scatter(wires, place, grads, *parts, *([] if z else [None]))
+
+    s_sum = scatter(dsums_ref, True)
+    s_down, s_up, s_out, s_q, s_kv = [scatter(g, with_z) for g in (gdown_ref, gup_ref, gout_ref, gq_ref, gkv_ref)]
+    place.greet()
+    s_down.step0()
+    s_up.step0()
+    s_out.step0()
     dsum_ref[...] = jnp.zeros_like(dsum_ref)
 
     def step(span, carry):
         attend_span_back(
-            span, qkv_ref, psum_ref, wsum_ref, probs_ref, dattn_ref, dq_ref, dkv_ref, dsum_ref
+            span, qkv_ref, psum_ref, wsum_ref, probs_ref, dattn_ref, dqkv_ref, dkv_ref, dsum_ref
         )
         return carry
 
-    lax.fori_loop(0, spans, step, 0)
-
-
-def attention_back(qkv, psum, wsum, probs, dattn):
-    tok = qkv.shape[0]
+    quarter = spans // 4
+    lax.fori_loop(0, quarter, step, 0)
+    s_down.step1()
+    s_up.step1()
+    s_out.step1()
+    lax.fori_loop(quarter, 2 * quarter, step, 0)
+    s_down.step2()
+    lax.fori_loop(2 * quarter, 3 * quarter, step, 0)
+    s_up.step2()
+    s_out.step2()
+    s_down.step3()
+    lax.fori_loop(3 * quarter, spans, step, 0)
+
+    dsums_ref[...] = jnp.zeros_like(dsums_ref)
+    for i in range(3):
+        block = lax.rem(place.me + place.devices - 2 + i, place.devices)
+        rows = slice(PSPANS + i * spans, PSPANS + (i + 1) * spans)
+        dsums_ref[pl.ds(block, 1)] = dsum_ref[rows, :].astype(BF16)[None]
+    for i in range(PSPANS // spans):
+        dsums_ref[i] = dsum_ref[i * spans : (i + 1) * spans, :].astype(BF16)
+    s_sum.step0()
+    gq_ref[...] = tn(act_ref[...], dqkv_ref[:, :D]).astype(BF16)
+    s_q.step0()
+    s_sum.step1()
+    s_up.step3()
+    s_out.step3()
+    dnorm_ref[...] = nt(dqkv_ref[:, :D], qkv_mat[:, :D])
+    s_sum.step2()
+    wdown_ref[...] = s_down.step4() * grad_scale
+    s_sum.step3()
+    s_q.step1()
+    wup_ref[...] = s_up.step4() * grad_scale
+    wout_ref[...] = s_out.step4() * grad_scale
+    shares = s_sum.step4()[0] * (1.0 / S)
+    for span in range(spans):
+        rows = slice(span * S, (span + 1) * S)
+        dqkv_ref[rows, D:] = (dkv_ref[rows, :] + shares[span : span + 1, :]).astype(BF16)
+    gkv_ref[...] = tn(act_ref[...], dqkv_ref[:, D:]).astype(BF16)
+    s_kv.step0()
+    s_q.step2()
+    sums_ref[0] = small_ref[...]
+
+    def finish(i, carry):
+        rows = pl.ds(pl.multiple_of(i * TILE, TILE), TILE)
+        dnormed = dnorm_ref[rows, :] + nt(dqkv_ref[rows, D:], qkv_mat[:, D:])
+        xhat, inverse = normed_parts(x_ref[rows, :].astype(F32))
+        sums_ref[0, 0:1, :] += jnp.sum(dnormed * xhat, axis=0, keepdims=True)
+        sums_ref[0, 1:2, :] += jnp.sum(dnormed, axis=0, keepdims=True)
+        dtok_ref[rows, :] = dresid_ref[rows, :] + norm_back(dnormed, xhat, inverse, gains_ref[0:1, :])
+        return carry
+
+    half = tok // TILE // 2
+    lax.fori_loop(0, half, finish, 0)
+    s_kv.step1()
+    s_q.step3()
+    lax.fori_loop(half, 2 * half, finish, 0)
+    small = Total(wires, place, sums_ref, came_ref)
+    small.send(0)
+    s_kv.step2()
+    small.take(0)
+    small.send(1)
+    wqkv_ref[:, :D] = s_q.step4() * grad_scale
+    s_kv.step3()
+    small.take(1)
+    small.send(2)
+    small.take(2)
+    small.send(3)
+    wqkv_ref[:, D:] = s_kv.step4() * grad_scale
+    small.take(3)
+    total_ref[...] = sums_ref[4] * grad_scale
+    wires.finish()
+
+
+def backward(with_z, grad_scale, x, act, qkv, probs, psum, wsum, qkv_mat, gains, dattn, dresid, gdown, gup, gout, small):
+    tok = x.shape[0]
     spans = tok // S
+    deep = lax.axis_size("head")
+    side = math.isqrt(lax.axis_size("seq") // 2)
+    devices = 2 * side * side * deep
+    hidden_size = gup.shape[0]
     whole = pl.BlockSpec(memory_space=VMEM)
+    shape = jax.ShapeDtypeStruct
+    owned = devices if with_z else devices // deep
+    peers = 1 + 2 * (side - 1) + deep - 1
+    n = 6 * (side * side + (side - 1) * side + side - 1 + deep - 1) + peers
+    scratch = scatter_scratch(side, deep, 1, (spans, 2 * D), True)
+    for total, columns in ((hidden_size, D), (hidden_size, D), (D, D), (D, D), (D, 2 * D)):
+        scratch += scatter_scratch(side, deep, total // devices, (columns,), with_z)
     return pl.pallas_call(
-        functools.partial(attention_back_kernel, spans),
+        functools.partial(backward_kernel, with_z, grad_scale),
         out_shape=(
-            jax.ShapeDtypeStruct((tok, D), BF16),
-            jax.ShapeDtypeStruct((tok, 2 * D), F32),
-            jax.ShapeDtypeStruct((PSPANS + WIN, 2 * D), F32),
+            shape((tok, D), F32),
+            shape((D // owned, 3 * D), F32),
+            shape((D // owned, D), F32),
+            shape((hidden_size // owned, D), F32),
+            shape((hidden_size // owned, D), F32),
+            shape((8, D), F32),
         ),
-        in_specs=[whole] * 5,
-        out_specs=(whole, whole, whole),
-        compiler_params=pltpu.CompilerParams(vmem_limit_bytes=VMEM_LIMIT),
-        name="attention_back",
-    )(qkv, psum, wsum, probs, dattn)
-
-
-def layer_norm(values, gain, shift):
-    row_mean = jnp.mean(values, axis=-1, keepdims=True)
-    centred = values - row_mean
-    variance = jnp.mean(centred * centred, axis=-1, keepdims=True)
-    return centred * lax.rsqrt(variance + EPS) * gain + shift
-
-
-def gelu_tanh(values):
-    return jax.nn.gelu(values, approximate=True)
+        in_specs=[whole] * 14,
+        out_specs=(whole,) * 6,
+        scratch_shapes=[
+            pltpu.VMEM((tok, 3 * D), BF16),
+            pltpu.VMEM((tok, 2 * D), F32),
+            pltpu.VMEM((PSPANS + WIN, 2 * D), F32),
+            pltpu.VMEM((devices, spans, 2 * D), BF16),
+            pltpu.VMEM((D, D), BF16),
+            pltpu.VMEM((D, 2 * D), BF16),
+            pltpu.VMEM((tok, D), F32),
+            pltpu.VMEM((5, 8, D), F32),
+            pltpu.VMEM((peers, 8, D), F32),
+            pltpu.SemaphoreType.DMA((n,)),
+            pltpu.SemaphoreType.DMA((n,)),
+            *scratch,
+        ],
+        compiler_params=pltpu.CompilerParams(vmem_limit_bytes=VMEM_LIMIT, collective_id=1, has_side_effects=True),
+        name="attend_back_and_scatter",
+    )(x, act, qkv, probs, psum, wsum, qkv_mat, gains, dattn, dresid, gdown, gup, gout, small)
 
 
 def split_parts(weight):
@@ -439,68 +758,33 @@
 
 def shards(tokens, cotangent, w_qkv, w_out, w_up, w_down, gain_one, shift_one, gain_two, shift_two, span_doc):
     tok = tokens.shape[0]
-    spans = tok // S
     devices = lax.axis_size("seq") * lax.axis_size("head")
     me = lax.axis_index("seq") * lax.axis_size("head") + lax.axis_index("head")
-    first = me * spans
     grad_scale = 1.0 / math.sqrt(tok * devices)
     docs = jnp.concatenate([jnp.full((PSPANS + MOST,), -1, jnp.int32), span_doc, jnp.full((MOST,), -1, jnp.int32)])
     docs = jnp.broadcast_to(docs[:, None], (docs.shape[0], S))
-
-    def scatter(x, axis=0):
-        return lax.psum_scatter(x, BOTH, scatter_dimension=axis, tiled=True)
-
     with_z = w_qkv.shape[0] % 16 == 0
     weights = (split_parts(w_qkv), w_out, w_up.T, w_down)
     if not with_z:
         weights = tuple(lax.all_gather(w, "head", axis=0, tiled=True) for w in weights)
     small = jnp.stack([gain_one, shift_one, gain_two, shift_two]).astype(F32)
-    small = jnp.pad(small, ((0, 4), (0, LANES - small.shape[1])))[None]
-    act_one, qkv, probs, attn_t, psum, wsum, qkv_mat, out_mat, up_mat, down_mat, gains = forward(
+    width = small.shape[1]
+    small = jnp.pad(small, ((0, 4), (0, LANES - width)))[None]
+    act, qkv, probs, attn_t, psum, wsum, qkv_mat, out_mat, up_mat, down_mat, gains = forward(
         tokens, *weights, small, docs, with_z
     )
-    x_rows = tokens.astype(F32)
-    _, back_one = jax.vjp(layer_norm, x_rows, gains[0], gains[1])
-    resid = x_rows + tn(attn_t, out_mat)
-    norm_two, back_two = jax.vjp(layer_norm, resid, gains[2], gains[3])
-    act_two = norm_two.astype(BF16)
-    hidden = nt(act_two, up_mat)
-    acted, back_gelu = jax.vjp(gelu_tanh, hidden)
-    acted = acted.astype(BF16)
-    out_tokens = (resid + nn(acted, down_mat)).astype(BF16)
-    d_hidden = back_gelu(nt(cotangent, down_mat))[0].astype(BF16)
-    grad_down = tn(acted, cotangent)
-    grad_up = tn(d_hidden, act_two)
-    d_resid_norm, grad_gain_two, grad_shift_two = back_two(nn(d_hidden, up_mat))
-    d_resid = cotangent.astype(F32) + d_resid_norm
-    d_branch = d_resid.astype(BF16)
-    grad_out = nn(attn_t, d_branch)
-    d_attn = nt(d_branch, out_mat).astype(BF16)
-    dq, dkv, dsum = attention_back(qkv, psum, wsum, probs, d_attn)
-    flat = jnp.zeros((devices * spans + 2 * MOST, 2 * D), F32)
-    flat = lax.dynamic_update_slice_in_dim(flat, dsum[PSPANS:], first, 0)[MOST:-MOST]
-    row = jnp.arange(flat.shape[0])[:, None]
-    flat = jnp.where(row < PSPANS, 0.0, flat)
-    flat = flat.at[:PSPANS].add(dsum[:PSPANS])
-    span_grads = scatter(flat.astype(BF16)).astype(F32) / S
-    dkv = (dkv.reshape(spans, S, 2 * D) + span_grads[:, None]).reshape(tok, 2 * D)
-    dqkv = jnp.concatenate([dq, dkv.astype(BF16)], axis=1)
-    grad_qkv = tn(act_one, dqkv)
-    d_x_norm, grad_gain_one, grad_shift_one = back_one(nt(dqkv, qkv_mat))
-    d_tokens = d_resid + d_x_norm
-    small_grads = scatter(jnp.stack([grad_gain_one, grad_shift_one, grad_gain_two, grad_shift_two]), 1) * grad_scale
-    return (
-        out_tokens,
-        d_tokens,
-        join_parts(scatter(grad_qkv) * grad_scale),
-        scatter(grad_out) * grad_scale,
-        scatter(grad_up).T * grad_scale,
-        scatter(grad_down) * grad_scale,
-        small_grads[0],
-        small_grads[1],
-        small_grads[2],
-        small_grads[3],
+    out_tokens, dresid, dattn, gdown, gup, gout, dsmall = dense(
+        tokens, cotangent, attn_t, out_mat, up_mat, down_mat, gains
     )
+    d_tokens, d_qkv, d_out, d_up, d_down, total = backward(
+        with_z, grad_scale, tokens, act, qkv, probs, psum, wsum, qkv_mat, gains, dattn, dresid, gdown, gup, gout, dsmall
+    )
+    if not with_z:
+        d_qkv, d_out, d_up, d_down = (
+            lax.psum_scatter(g, "head", scatter_dimension=0, tiled=True) for g in (d_qkv, d_out, d_up, d_down)
+        )
+    own = lax.dynamic_slice_in_dim(total, me * width, width, 1)
+    return out_tokens, d_tokens, join_parts(d_qkv), d_out, d_up.T, d_down, own[0], own[1], own[2], own[3]
 
 
 def solution(mesh):

time: 961 us -> 184 us (0.19)
  waiting for transfers between devices: 751 us -> 0 us
  Pallas kernels: 92.5 us -> 170 us
  matrix products: 54.6 us -> 0 us
  other arithmetic: 22.1 us -> 2.04 us
  local copies, waits for them, and re-layouts: 24.9 us -> 10.7 us
  between operations: 14.5 us -> 0.69 us
    reduce_scatter x5 -> x0, waiting for transfers between devices: 665 us -> none  [scatter(): return lax.psum_scatter(x, BOTH, scatter_dimension=axis, tiled=True)]
    unnamed x7 -> x0, waiting for transfers between devices: 86.7 us -> none
    pallas_call x1 -> x2, Pallas kernels: 20.5 us -> 97.8 us  [the longest x1 70.9 us: backward(): pl.pallas_call(functools.partial(backward_kernel, with_z, grad_scale), ou...]
    dot_general x11 -> x0, matrix products: 54.6 us -> none  [the longest x4 24.1 us: tn(): lax.dot_general(a, b, (((0,), (0,)), ((), ())), preferred_element_type=F32)]
  transfers between devices with their start and end apart: 6 -> 0, of which waited for: 6 -> 0; matrix products, arithmetic and copies ran while one was open for 5% -> 0% of each run, Pallas kernels for 0% -> 0%
where the time goes in v3:
time: 184 us; the launch traced here: 183 us
  Pallas kernels  170 us (92%)
  local copies, waits for them, and re-layouts  10.7 us (6%)
  other arithmetic  2.04 us (1%)
    pallas_call x1, Pallas kernels, forward(): pl.pallas_call(functools.partial(forward_kernel, with_z), out_shape=(shap...  72.1 us
    pallas_call x1, Pallas kernels, backward(): pl.pallas_call(functools.partial(backward_kernel, with_z, grad_scale), ou...  70.9 us
    pallas_call x1, Pallas kernels, dense(): pl.pallas_call(dense_kernel, out_shape=(shape((tok, D), BF16), shape((tok...  26.9 us
    unnamed x10, local copies, waits for them, and re-layouts  5.06 us

profile of v3, /device:TPU:0, one launch (start us, length us, event | category | flops | bytes accessed | tf_op | source)
XLA Modules:
  0.0 183.4 jit_solution(2877187803733808548)
XLA Ops:
  0.6 1.0 reshape.33
  1.6 0.8 reshape.34.wq_ref
  2.4 0.7 pad_add_fusion
  3.1 0.8 broadcast_in_dim.17.docs_ref
  3.9 1.3 fusion.10.small_ref
  5.2 72.1 %gather_and_attend.1 = (bf16[1024,512]{1,0:T(8,128)(2,1)}, bf16[1024,1536]{1,0:T(8,128)(2,1)}, bf16[32,288,256]{2,1,0:T(8,128)(2,1)}, bf16[512,1024]{1,0:T(8,128...) custom-call(bf16[1024,512]{1,0:T(8,128)(2,1)} %x_ref.5, ...), custom_call_target="tpu_custom_call" | custom-call | tf_op jit(solution)/shard_map/gather_and_attend/pallas_call | solution.py:351
  77.3 26.9 %dense.1 = (bf16[1024,512]{1,0:T(8,128)(2,1)}, f32[1024,512]{1,0:T(8,128)}, bf16[1024,512]{1,0:T(8,128)(2,1)}, bf16[2048,512]{1,0:T(8,128)(2,1)}, bf16[2048,512]...) custom-call(bf16[1024,512]{1,0:T(8,128)(2,1)} %x_ref.5, bf16[1024,512]{1,0:T(8,128)(2,1)} %cot_ref.1, ...), custom_call_target="tpu_custom_call" | custom-call | tf_op jit(solution)/shard_map/dense/pallas_call | solution.py:461
  104.2 70.9 %attend_back_and_scatter.1 = (f32[1024,512]{1,0:T(8,128)}, f32[16,1536]{1,0:T(8,128)}, f32[16,512]{1,0:T(8,128)}, f32[64,512]{1,0:T(8,128)}, f32[64,512]{1,0:T(8,128)}, /*index=5*/f32[8,512]{1,0:T(8,128)}) custom-call(bf16[1024,512]{1,0:T(8,128)(2,1)} %x_ref.5, bf16[1024,512]{1,0:T(8,128)(2,1)} %get-tuple-element.40.act_ref, ...), custom_call_target="tpu_custom_call" | custom-call | tf_op jit(solution)/shard_map/attend_back_and_scatter/pallas_call | solution.py:718
  175.1 1.0 reshape.35
  176.1 0.1 copy.26
  176.2 0.8 reshape.36
  177.0 0.8 constant_dynamic-slice_fusion
  177.8 0.5 slice_bitcast_fusion
  178.3 0.0 copy-start.2
  178.3 0.0 copy-start.1
  178.3 0.0 copy-start
  178.3 3.1 %copy.31 = f32[1024,512]{1,0:T(8,128)} copy(f32[1024,512]{1,0:T(8,128)} %get-tuple-element.73) | data formatting | bytes 4194304
  181.4 0.0 copy-done.2
  181.4 0.6 copy.32
  182.1 0.0 copy-done.1
  182.1 0.7 copy.33
  182.7 0.0 copy-done
  182.7 0.7 copy.34
  (3 shorter events, 0.0 us)
Async XLA Ops:
  178.3 3.1 %copy-start.2 = (f32[16,512]{1,0:T(8,128)S(1)}, f32[16,512]{1,0:T(8,128)}, u32[]{:S(2)}) copy-start(f32[16,512]{1,0:T(8,128)} %get-tuple-element.75) | copy-start | bytes 98308
  178.3 3.7 %copy-start.1 = (f32[64,512]{1,0:T(8,128)S(1)}, f32[64,512]{1,0:T(8,128)}, u32[]{:S(2)}) copy-start(f32[64,512]{1,0:T(8,128)} %get-tuple-element.55) | copy-start | bytes 393220
  178.3 4.4 %copy-start = (f32[64,512]{1,0:T(8,128)S(1)}, f32[64,512]{1,0:T(8,128)}, u32[]{:S(2)}) copy-start(f32[64,512]{1,0:T(8,128)} %get-tuple-element.77) | copy-start | bytes 393220

commit v4 on v2

--- a/solution.py
+++ b/solution.py
@@ -23,7 +23,9 @@
 F32 = jnp.float32
 BF16 = jnp.bfloat16
 VMEM = pltpu.MemorySpace.VMEM
-VMEM_LIMIT = 60 * 2**20
+VMEM_LIMIT = 67043328
+TILE = 256
+CHUNK = 256
 
 
 def nn(a, b):
@@ -43,7 +45,7 @@
     row = lax.broadcasted_iota(jnp.int32, (PSPANS, S), 0)
     prompt = jnp.where(row < index, 0.0, MASKED)
     wrow = first - MOST + lax.broadcasted_iota(jnp.int32, (WIN, S), 0)
-    same = docs_ref[pl.ds(pl.multiple_of(first, 8), WIN), :] == docs_ref[pl.ds(index + MOST, 1), :]
+    same = docs_ref[...] == docs_ref[pl.ds(span + MOST, 1), :]
     window = jnp.where(same & (wrow >= PSPANS) & (wrow < index), 0.0, MASKED)
     return jnp.concatenate([prompt, window], axis=0).astype(F32)
 
@@ -186,9 +188,14 @@
         move.start()
         return move
 
+    def settle(self, moves):
+        for move in moves:
+            move.wait_send()
+        done = {id(move) for move in moves}
+        self.sent = [move for move in self.sent if id(move) not in done]
+
     def finish(self):
-        for move in self.sent:
-            move.wait_send()
+        self.settle(list(self.sent))
 
 
 def copies_of_gather(side, deep, with_z):
@@ -198,7 +205,7 @@
 class Gather:
     def __init__(self, wires, place, shard, full, rows, with_z):
         self.w, self.p, self.full, self.shard = wires, place, full, shard
-        self.rows, self.with_z = rows, with_z
+        self.rows, self.with_z, self.sent = rows, with_z, []
         self.group = rows * place.deep if with_z else rows
 
     def block(self, y, x):
@@ -210,6 +217,7 @@
         start = pl.multiple_of(p.me * self.rows, self.rows) if self.with_z else p.seq(p.y, p.x, p.c) * self.rows
         own = self.full.at[pl.ds(start, self.rows)]
         self.moves = [self.w.copy(self.shard, own, d) for d in p.peers("z")] if self.with_z else []
+        self.sent += self.moves
         self.placed = self.w.local(self.shard, own)
 
     def _next(self, sources, axis, fresh):
@@ -219,7 +227,9 @@
         self.moves = []
         if axis is not None:
             self.moves = [self.w.copy(self.block(*s), self.block(*s), d) for d in p.peers(axis) for s in sources]
-        self.across += [self.w.copy(self.block(*s), self.block(*s), p.sibling()) for s in fresh]
+        more = [self.w.copy(self.block(*s), self.block(*s), p.sibling()) for s in fresh]
+        self.across += more
+        self.sent += self.moves + more
 
     def step1(self):
         self.placed.wait()
@@ -248,13 +258,6 @@
             move.wait_recv()
 
 
-def layer_norm_rows(values, gain, shift):
-    mean = jnp.mean(values, axis=-1, keepdims=True)
-    centred = values - mean
-    variance = jnp.mean(centred * centred, axis=-1, keepdims=True)
-    return centred * lax.rsqrt(variance + EPS) * gain + shift
-
-
 def spread_small(gathered, devices):
     width = D // devices
     table = gathered.reshape(devices * 8, LANES).astype(BF16)
@@ -265,62 +268,222 @@
     return jnp.sum(jnp.where(owner == column, every, 0.0).reshape(devices, 8, D), axis=0)
 
 
-def forward_kernel(
-    with_z,
-    x_ref, wq_ref, wo_ref, wu_ref, wd_ref, small_ref, docs_ref,
-    act_ref, qkv_ref, probs_ref, attn_t_ref, psum_ref, wsum_ref,
-    qkv_mat, out_mat, up_mat, down_mat, gains_ref,
-    small_all, own_sums, sums_all, send, recv,
+def normed_parts(values):
+    mean = jnp.mean(values, axis=-1, keepdims=True)
+    centred = values - mean
+    inverse = lax.rsqrt(jnp.mean(centred * centred, axis=-1, keepdims=True) + EPS)
+    return centred * inverse, inverse
+
+
+def norm_back(dnormed, xhat, inverse, gain):
+    grown = dnormed * gain
+    along = jnp.mean(grown * xhat, axis=-1, keepdims=True)
+    return (grown - jnp.mean(grown, axis=-1, keepdims=True) - xhat * along) * inverse
+
+
+def gelu_parts(h):
+    square = h * h
+    t = jnp.tanh(0.7978845608 * (h + 0.044715 * h * square))
+    half = 0.5 * (1.0 + t)
+    slope = 0.7978845608 * (1.0 + 3 * 0.044715 * square)
+    return h * half, half + 0.5 * h * (1.0 - t * t) * slope
+
+
+def add_into(held, index, others):
+    total = held[index].astype(F32)
+    for other in others:
+        total = total + other.astype(F32)
+    held[index] = total.astype(held.dtype)
+
+
+class Scatter:
+    def __init__(self, wires, place, grads, held, hop1, hop2, hopz):
+        self.w, self.p, self.grads, self.held = wires, place, grads, held
+        self.hop1, self.hop2, self.hopz = hop1, hop2, hopz
+        self.group = held.shape[1]
+        self.crossed, self.first, self.second, self.third = {}, {}, {}, []
+        n = place.side
+        self.line = [*range(1, n), 0]
+        self.order = [(d, e) for d in self.line for e in self.line]
+
+    def at(self, turn, d, e):
+        p, n = self.p, self.p.side
+        y = lax.rem(p.y + turn * d + (1 - turn) * e, n)
+        x = lax.rem(p.x + turn * e + (1 - turn) * d, n)
+        return y * n + x
+
+    def rows_of(self, j, core):
+        return pl.ds(pl.multiple_of((2 * j + core) * self.group, self.group), self.group)
+
+    def cross(self, d, e):
+        p = self.p
+        j = self.at(1 - p.c, d, e)
+        self.crossed[d, e] = self.w.copy(self.grads.at[self.rows_of(j, 1 - p.c)], self.held.at[j], p.sibling())
+
+    def fold(self, d, e):
+        p = self.p
+        j = self.at(p.c, d, e)
+        self.crossed[d, e].wait_recv()
+        add_into(self.held, j, [self.grads[self.rows_of(j, p.c)]])
+        if d:
+            self.first[d, e] = self.w.copy(self.held.at[j], self.hop1.at[d - 1, e], p.peers(0)[d - 1])
+
+    def turn(self, e):
+        p, n = self.p, self.p.side
+        j = self.at(p.c, 0, e)
+        for d in range(1, n):
+            self.first[d, e].wait_recv()
+        add_into(self.held, j, [self.hop1[d - 1, e] for d in range(1, n)])
+        if e:
+            self.second[e] = self.w.copy(self.held.at[j], self.hop2.at[e - 1], p.peers(1)[e - 1])
+
+    def step0(self):
+        for d, e in self.order:
+            self.cross(d, e)
+
+    def step1(self):
+        for d, e in self.order:
+            self.fold(d, e)
+
+    def step2(self):
+        for e in self.line:
+            self.turn(e)
+
+    def step3(self):
+        p = self.p
+        for move in self.second.values():
+            move.wait_recv()
+        self.mine = self.at(p.c, 0, 0)
+        add_into(self.held, self.mine, [self.hop2[e - 1] for e in range(1, p.side)])
+        if self.hopz is not None:
+            self.unit = self.group // p.deep
+            for d, other in enumerate(p.peers("z"), 1):
+                self.third.append(self.w.copy(self.held.at[self.mine, self.unit_rows(d)], self.hopz.at[d - 1], other))
+
+    def unit_rows(self, d):
+        p = self.p
+        return pl.ds(pl.multiple_of(lax.rem(p.z + d, p.deep) * self.unit, self.unit), self.unit)
+
+    def step4(self):
+        if self.hopz is None:
+            return self.held[self.mine].astype(F32)
+        total = self.held[self.mine, self.unit_rows(0)].astype(F32)
+        for d, move in enumerate(self.third):
+            move.wait_recv()
+            total = total + self.hopz[d].astype(F32)
+        return total
+
+
+def scatter_scratch(side, deep, unit, tail, with_z):
+    group = deep * unit
+    shapes = [(side * side, group), (side - 1, side, group), (side - 1, group)]
+    if with_z:
+        shapes.append((deep - 1, unit))
+    return [pltpu.VMEM((*shape, *tail), BF16) for shape in shapes]
+
+
+class Total:
+    def __init__(self, wires, place, sums, came):
+        self.w, self.p, self.sums, self.came = wires, place, sums, came
+        self.slot = 0
+
+    def send(self, level):
+        p = self.p
+        peers = [[p.sibling()], p.peers(0), p.peers(1), p.peers("z")][level]
+        self.moves = []
+        for peer in peers:
+            self.moves.append(self.w.copy(self.sums.at[level], self.came.at[self.slot], peer))
+            self.slot += 1
+
+    def take(self, level):
+        total = self.sums[level]
+        for i, move in enumerate(self.moves):
+            move.wait_recv()
+            total = total + self.came[self.slot - len(self.moves) + i]
+        self.sums[level + 1] = total
+
+
+def loop(start, stop, body):
+    def step(i, carry):
+        body(i)
+        return carry
+
+    lax.fori_loop(start, stop, step, 0)
+
+
+def tile_rows(i, size):
+    return pl.ds(pl.multiple_of(i * size, size), size)
+
+
+def layer_kernel(
+    with_z, grad_scale,
+    x_ref, cot_ref, wq_ref, wkv_ref, wo_ref, wu_ref, wd_ref, small_ref, docs_ref,
+    out_ref, dtok_ref, dwq_ref, dwkv_ref, dwo_ref, dwu_ref, dwd_ref, total_ref,
+    q_mat, kv_mat, out_mat, up_mat, down_mat, gains_ref, small_all, own_sums, sums_all, psum_ref, wsum_ref,
+    act_ref, qkv_ref, probs_ref, attn_t_ref, resid_ref, act2_ref, acted_ref, dhid_ref, dattn_ref,
+    gdown_ref, gup_ref, gout_ref, gq_ref, gkv_ref, dkv_ref, dsum_ref, sums_ref, came_ref, send, recv, *held,
 ):
     place = Place()
     wires = Wires(send, recv)
     tok = x_ref.shape[0]
     spans = tok // S
     first = place.me * spans
+    held = list(held)
+
+    def gather(shard, full):
+        return Gather(wires, place, shard, full, shard.shape[0], with_z)
+
+    def scatter(grads, z):
+        parts = [held.pop(0) for _ in range(4 if z else 3)]
+        return Scatter(wires, place, grads, *parts, *([] if z else [None]))
+
     small = Gather(wires, place, small_ref, small_all, 1, True)
-    gathers = [
-        Gather(wires, place, shard, full, shard.shape[0], with_z)
-        for shard, full in ((wq_ref, qkv_mat), (wo_ref, out_mat), (wd_ref, down_mat), (wu_ref, up_mat))
-    ]
-    g_qkv, g_out, g_down, g_up = gathers
+    sums = Gather(wires, place, own_sums, sums_all, 1, True)
+    g_kv, g_q, g_out = gather(wkv_ref, kv_mat), gather(wq_ref, q_mat), gather(wo_ref, out_mat)
+    g_down, g_up = gather(wd_ref, down_mat), gather(wu_ref, up_mat)
+    dsums_ref = sums_all
+    s_sum = scatter(dsums_ref, True)
+    s_down, s_up, s_out, s_q, s_kv = [scatter(g, with_z) for g in (gdown_ref, gup_ref, gout_ref, gq_ref, gkv_ref)]
+
     place.greet()
-    small.step0()
-    for g in gathers:
+    for g in (small, g_kv, g_q, g_out, g_down, g_up):
         g.step0()
     small.step1()
-    g_qkv.step1()
+    g_kv.step1()
+    g_q.step1()
     small.step2()
-    g_qkv.step2()
+    g_kv.step2()
+    g_q.step2()
     small.step3()
-    g_qkv.step3()
-    g_out.step1()
-    g_down.step1()
+    g_kv.step3()
     small.step4()
     gains_ref[...] = spread_small(small_all[...], place.devices)
 
-    def norm(i, carry):
-        rows = pl.ds(pl.multiple_of(i * S, S), S)
-        normed = layer_norm_rows(x_ref[rows, :].astype(F32), gains_ref[0:1, :], gains_ref[1:2, :])
-        act_ref[rows, :] = normed.astype(BF16)
-        return carry
-
-    lax.fori_loop(0, spans, norm, 0)
-    g_qkv.step4()
-    for part in (1, 2):
-        cols = slice(part * D, (part + 1) * D)
-        block = nn(act_ref[...], qkv_mat[:, cols]).astype(BF16)
-        qkv_ref[:, cols] = block
+    def norm(i):
+        rows = tile_rows(i, S)
+        xhat, _ = normed_parts(x_ref[rows, :].astype(F32))
+        act_ref[rows, :] = (xhat * gains_ref[0:1, :] + gains_ref[1:2, :]).astype(BF16)
+
+    loop(0, spans, norm)
+    g_kv.step4()
+    g_q.step3()
+    g_out.step1()
+    for part in (0, 1):
+        block = nn(act_ref[...], kv_mat[:, part * D : (part + 1) * D]).astype(BF16)
+        qkv_ref[:, (part + 1) * D : (part + 2) * D] = block
         mean = jnp.sum(block.astype(F32).reshape(spans, S, D), axis=1) * (1.0 / S)
-        own_sums[0, :, (part - 1) * D : part * D] = mean.astype(BF16)
-    sums = Gather(wires, place, own_sums, sums_all, 1, True)
+        own_sums[0, :, part * D : (part + 1) * D] = mean.astype(BF16)
+        if part == 0:
+            g_down.step1()
     sums.step0()
-    qkv_ref[:, :D] = nn(act_ref[...], qkv_mat[:, :D]).astype(BF16)
+    g_q.step4()
+    qkv_ref[:, :D] = nn(act_ref[...], q_mat[...]).astype(BF16)
     sums.step1()
-    g_up.step1()
-    sums.step2()
-    sums.step3()
     g_out.step2()
     g_down.step2()
+    sums.step2()
+    g_up.step1()
+    sums.step3()
     sums.step4()
     for i in range(PSPANS // MOST):
         two = sums_all[pl.ds(2 * i, 2)].astype(F32)
@@ -331,100 +494,225 @@
     wsum_ref[:MOST, :] = jnp.concatenate([before, last], axis=0).reshape(MOST, 2 * D).astype(BF16)
     wsum_ref[MOST:, :] = jnp.concatenate([here, jnp.zeros_like(here)], axis=0).reshape(MOST, 2 * D).astype(BF16)
 
-    def step(span, carry):
+    def attend(span):
         attend_span(span, first, qkv_ref, psum_ref, wsum_ref, docs_ref, attn_t_ref, probs_ref)
-        return carry
-
-    lax.fori_loop(0, spans // 2, step, 0)
+
+    quarter = spans // 4
+    loop(0, quarter, attend)
+    g_up.step2()
     g_out.step3()
+    loop(quarter, 2 * quarter, attend)
     g_down.step3()
-    g_up.step2()
-    lax.fori_loop(spans // 2, spans, step, 0)
+    loop(2 * quarter, 3 * quarter, attend)
     g_up.step3()
-    for g in (g_out, g_down, g_up):
-        g.step4()
+    loop(3 * quarter, spans, attend)
+    g_out.step4()
+
+    def residual(i):
+        rows = tile_rows(i, TILE)
+        resid = x_ref[rows, :].astype(F32) + tn(attn_t_ref[:, rows], out_mat[...])
+        resid_ref[rows, :] = resid
+        xhat, _ = normed_parts(resid)
+        act2_ref[rows, :] = (xhat * gains_ref[2:3, :] + gains_ref[3:4, :]).astype(BF16)
+
+    loop(0, tok // TILE, residual)
+    g_down.step4()
+    g_up.step4()
+
+    def feed(i):
+        part = tile_rows(i, CHUNK)
+        acted, slope = gelu_parts(nt(act2_ref[...], up_mat[part, :]))
+        acted = acted.astype(BF16)
+        acted_ref[:, part] = acted
+        dhid = (nt(cot_ref[...], down_mat[part, :]) * slope).astype(BF16)
+        dhid_ref[:, part] = dhid
+        gdown_ref[part, :] = tn(acted, cot_ref[...]).astype(BF16)
+        gup_ref[part, :] = tn(dhid, act2_ref[...]).astype(BF16)
+
+    both = (s_down, s_up)
+    if s_up.group == CHUNK:
+        for d, e in s_up.order:
+            theirs = 2 * s_up.at(1 - place.c, d, e) + 1 - place.c
+            ours = 2 * s_up.at(place.c, d, e) + place.c
+            loop(0, 2, lambda i: feed(theirs + i * (ours - theirs)))
+            for s in both:
+                s.cross(d, e)
+            for s in both:
+                s.fold(d, e)
+            if d == 0:
+                for s in both:
+                    s.turn(e)
+    else:
+        loop(0, up_mat.shape[0] // CHUNK, feed)
+        for s in both:
+            s.step0()
+        for s in both:
+            s.step1()
+        for s in both:
+            s.step2()
+    sums_ref[...] = jnp.zeros_like(sums_ref)
+
+    def finish(i):
+        rows = tile_rows(i, TILE)
+        dnormed = nn(dhid_ref[rows, :], up_mat[...])
+        xhat, inverse = normed_parts(resid_ref[rows, :])
+        sums_ref[0, 2:3, :] += jnp.sum(dnormed * xhat, axis=0, keepdims=True)
+        sums_ref[0, 3:4, :] += jnp.sum(dnormed, axis=0, keepdims=True)
+        dresid = cot_ref[rows, :].astype(F32) + norm_back(dnormed, xhat, inverse, gains_ref[2:3, :])
+        dtok_ref[rows, :] = dresid
+        branch = dresid.astype(BF16)
+        act2_ref[rows, :] = branch
+        dattn_ref[rows, :] = nt(branch, out_mat[...]).astype(BF16)
+
+    loop(0, tok // TILE, finish)
+    for s in both:
+        s.step3()
+    gout_ref[...] = nn(attn_t_ref[...], act2_ref[...]).astype(BF16)
+    s_out.step0()
+    dsum_ref[...] = jnp.zeros_like(dsum_ref)
+
+    def attend_back(span):
+        attend_span_back(
+            span, qkv_ref, psum_ref, wsum_ref, probs_ref, dattn_ref, dhid_ref, dkv_ref, dsum_ref
+        )
+
+    loop(0, quarter, attend_back)
+    s_out.step1()
+    loop(quarter, 2 * quarter, attend_back)
+    s_out.step2()
+    loop(2 * quarter, 3 * quarter, attend_back)
+    s_out.step3()
+    loop(3 * quarter, spans, attend_back)
+
+    wires.settle(sums.sent)
+    dsums_ref[...] = jnp.zeros_like(dsums_ref)
+    for i in range(3):
+        block = lax.rem(place.me + place.devices - 2 + i, place.devices)
+        rows = slice(PSPANS + i * spans, PSPANS + (i + 1) * spans)
+        dsums_ref[pl.ds(block, 1)] = dsum_ref[rows, :].astype(BF16)[None]
+    for i in range(PSPANS // spans):
+        dsums_ref[i] = dsum_ref[i * spans : (i + 1) * spans, :].astype(BF16)
+    s_sum.step0()
+    gq_ref[...] = tn(act_ref[...], dhid_ref[:, :D]).astype(BF16)
+    s_sum.step1()
+    s_q.step0()
+    s_sum.step2()
+    s_q.step1()
+    dwd_ref[...] = s_down.step4() * grad_scale
+    dwu_ref[...] = s_up.step4() * grad_scale
+    dwo_ref[...] = s_out.step4() * grad_scale
+    s_sum.step3()
+    s_q.step2()
+    shares = s_sum.step4()[0] * (1.0 / S)
+    for span in range(spans):
+        rows = slice(span * S, (span + 1) * S)
+        dhid_ref[rows, D : 3 * D] = (dkv_ref[rows, :] + shares[span : span + 1, :]).astype(BF16)
+    gkv_ref[...] = tn(act_ref[...], dhid_ref[:, D : 3 * D]).astype(BF16)
+    s_kv.step0()
+    s_q.step3()
+
+    def last(i):
+        rows = tile_rows(i, TILE)
+        dnormed = nt(dhid_ref[rows, :D], q_mat[...]) + nt(dhid_ref[rows, D : 3 * D], kv_mat[...])
+        xhat, inverse = normed_parts(x_ref[rows, :].astype(F32))
+        sums_ref[0, 0:1, :] += jnp.sum(dnormed * xhat, axis=0, keepdims=True)
+        sums_ref[0, 1:2, :] += jnp.sum(dnormed, axis=0, keepdims=True)
+        dtok_ref[rows, :] += norm_back(dnormed, xhat, inverse, gains_ref[0:1, :])
+
+    def output(i):
+        rows = tile_rows(i, TILE)
+        out_ref[rows, :] = (resid_ref[rows, :] + nn(acted_ref[rows, :], down_mat[...])).astype(BF16)
+
+    half = tok // TILE // 2
+    loop(0, half, last)
+    s_kv.step1()
+    loop(half, 2 * half, last)
+    total = Total(wires, place, sums_ref, came_ref)
+    total.send(0)
+    loop(0, half, output)
+    total.take(0)
+    total.send(1)
+    s_kv.step2()
+    loop(half, 2 * half, output)
+    total.take(1)
+    total.send(2)
+    s_kv.step3()
+    dwq_ref[...] = s_q.step4() * grad_scale
+    total.take(2)
+    total.send(3)
+    dwkv_ref[...] = s_kv.step4() * grad_scale
+    total.take(3)
+    total_ref[...] = sums_ref[4] * grad_scale
     wires.finish()
 
 
-def forward(x, wq, wo, wu, wd, small, docs, with_z):
+def layer(with_z, grad_scale, x, cotangent, wq, wkv, wo, wu, wd, small, docs):
     tok = x.shape[0]
     spans = tok // S
     deep = lax.axis_size("head")
     side = math.isqrt(lax.axis_size("seq") // 2)
     devices = 2 * side * side * deep
+    owned = devices if with_z else devices // deep
+    hidden_size = wu.shape[0] * owned
     whole = pl.BlockSpec(memory_space=VMEM)
-    n = copies_of_gather(side, deep, True) * 6
     shape = jax.ShapeDtypeStruct
+    peers = 1 + 2 * (side - 1) + deep - 1
+    n = 7 * copies_of_gather(side, deep, True) + 7
+    n += 6 * (side * side + (side - 1) * side + side - 1 + deep - 1) + peers
+    held = scatter_scratch(side, deep, 1, (spans, 2 * D), True)
+    for total, columns in ((hidden_size, D), (hidden_size, D), (D, D), (D, D), (D, 2 * D)):
+        held += scatter_scratch(side, deep, total // devices, (columns,), with_z)
     return pl.pallas_call(
-        functools.partial(forward_kernel, with_z),
+        functools.partial(layer_kernel, with_z, grad_scale),
         out_shape=(
             shape((tok, D), BF16),
-            shape((tok, 3 * D), BF16),
-            shape((spans * PAIRS, KEYS, 2 * S), BF16),
-            shape((D, tok), BF16),
-            shape((PSPANS, 2 * D), BF16),
-            shape((WIN, 2 * D), BF16),
-            shape((D, 3 * D), BF16),
-            shape((D, D), BF16),
-            shape((4 * D, D), BF16),
-            shape((4 * D, D), BF16),
+            shape((tok, D), F32),
+            shape((D // owned, D), F32),
+            shape((D // owned, 2 * D), F32),
+            shape((D // owned, D), F32),
+            shape((hidden_size // owned, D), F32),
+            shape((hidden_size // owned, D), F32),
             shape((8, D), F32),
         ),
-        in_specs=[whole] * 7,
-        out_specs=(whole,) * 11,
+        in_specs=[whole] * 9,
+        out_specs=(whole,) * 8,
         scratch_shapes=[
+            pltpu.VMEM((D, D), BF16),
+            pltpu.VMEM((D, 2 * D), BF16),
+            pltpu.VMEM((D, D), BF16),
+            pltpu.VMEM((hidden_size, D), BF16),
+            pltpu.VMEM((hidden_size, D), BF16),
+            pltpu.VMEM((8, D), F32),
             pltpu.VMEM((devices, 8, LANES), F32),
             pltpu.VMEM((1, spans, 2 * D), BF16),
             pltpu.VMEM((devices, spans, 2 * D), BF16),
+            pltpu.VMEM((PSPANS, 2 * D), BF16),
+            pltpu.VMEM((WIN, 2 * D), BF16),
+            pltpu.VMEM((tok, D), BF16),
+            pltpu.VMEM((tok, 3 * D), BF16),
+            pltpu.VMEM((spans * PAIRS, KEYS, 2 * S), BF16),
+            pltpu.VMEM((D, tok), BF16),
+            pltpu.VMEM((tok, D), F32),
+            pltpu.VMEM((tok, D), BF16),
+            pltpu.VMEM((tok, hidden_size), BF16),
+            pltpu.VMEM((tok, hidden_size), BF16),
+            pltpu.VMEM((tok, D), BF16),
+            pltpu.VMEM((hidden_size, D), BF16),
+            pltpu.VMEM((hidden_size, D), BF16),
+            pltpu.VMEM((D, D), BF16),
+            pltpu.VMEM((D, D), BF16),
+            pltpu.VMEM((D, 2 * D), BF16),
+            pltpu.VMEM((tok, 2 * D), F32),
+            pltpu.VMEM((PSPANS + WIN, 2 * D), F32),
+            pltpu.VMEM((5, 8, D), F32),
+            pltpu.VMEM((peers, 8, D), F32),
             pltpu.SemaphoreType.DMA((n,)),
             pltpu.SemaphoreType.DMA((n,)),
+            *held,
         ],
         compiler_params=pltpu.CompilerParams(vmem_limit_bytes=VMEM_LIMIT, collective_id=0, has_side_effects=True),
-        name="gather_and_attend",
-    )(x, wq, wo, wu, wd, small, docs)
-
-
-def attention_back_kernel(
-    spans, qkv_ref, psum_ref, wsum_ref, probs_ref, dattn_ref, dq_ref, dkv_ref, dsum_ref
-):
-    dsum_ref[...] = jnp.zeros_like(dsum_ref)
-
-    def step(span, carry):
-        attend_span_back(
-            span, qkv_ref, psum_ref, wsum_ref, probs_ref, dattn_ref, dq_ref, dkv_ref, dsum_ref
-        )
-        return carry
-
-    lax.fori_loop(0, spans, step, 0)
-
-
-def attention_back(qkv, psum, wsum, probs, dattn):
-    tok = qkv.shape[0]
-    spans = tok // S
-    whole = pl.BlockSpec(memory_space=VMEM)
-    return pl.pallas_call(
-        functools.partial(attention_back_kernel, spans),
-        out_shape=(
-            jax.ShapeDtypeStruct((tok, D), BF16),
-            jax.ShapeDtypeStruct((tok, 2 * D), F32),
-            jax.ShapeDtypeStruct((PSPANS + WIN, 2 * D), F32),
-        ),
-        in_specs=[whole] * 5,
-        out_specs=(whole, whole, whole),
-        compiler_params=pltpu.CompilerParams(vmem_limit_bytes=VMEM_LIMIT),
-        name="attention_back",
-    )(qkv, psum, wsum, probs, dattn)
-
-
-def layer_norm(values, gain, shift):
-    row_mean = jnp.mean(values, axis=-1, keepdims=True)
-    centred = values - row_mean
-    variance = jnp.mean(centred * centred, axis=-1, keepdims=True)
-    return centred * lax.rsqrt(variance + EPS) * gain + shift
-
-
-def gelu_tanh(values):
-    return jax.nn.gelu(values, approximate=True)
+        name="mega_layer",
+    )(x, cotangent, wq, wkv, wo, wu, wd, small, docs)
 
 
 def split_parts(weight):
@@ -439,68 +727,30 @@
 
 def shards(tokens, cotangent, w_qkv, w_out, w_up, w_down, gain_one, shift_one, gain_two, shift_two, span_doc):
     tok = tokens.shape[0]
-    spans = tok // S
     devices = lax.axis_size("seq") * lax.axis_size("head")
     me = lax.axis_index("seq") * lax.axis_size("head") + lax.axis_index("head")
-    first = me * spans
     grad_scale = 1.0 / math.sqrt(tok * devices)
     docs = jnp.concatenate([jnp.full((PSPANS + MOST,), -1, jnp.int32), span_doc, jnp.full((MOST,), -1, jnp.int32)])
-    docs = jnp.broadcast_to(docs[:, None], (docs.shape[0], S))
-
-    def scatter(x, axis=0):
-        return lax.psum_scatter(x, BOTH, scatter_dimension=axis, tiled=True)
-
+    docs = lax.dynamic_slice_in_dim(docs, me * (tok // S), WIN, 0)
+    docs = jnp.broadcast_to(docs[:, None], (WIN, S))
     with_z = w_qkv.shape[0] % 16 == 0
-    weights = (split_parts(w_qkv), w_out, w_up.T, w_down)
+    w_qkv = split_parts(w_qkv)
+    weights = (w_qkv[:, :D], w_qkv[:, D:], w_out, w_up.T, w_down)
     if not with_z:
         weights = tuple(lax.all_gather(w, "head", axis=0, tiled=True) for w in weights)
     small = jnp.stack([gain_one, shift_one, gain_two, shift_two]).astype(F32)
-    small = jnp.pad(small, ((0, 4), (0, LANES - small.shape[1])))[None]
-    act_one, qkv, probs, attn_t, psum, wsum, qkv_mat, out_mat, up_mat, down_mat, gains = forward(
-        tokens, *weights, small, docs, with_z
+    width = small.shape[1]
+    small = jnp.pad(small, ((0, 4), (0, LANES - width)))[None]
+    out_tokens, d_tokens, d_q, d_kv, d_out, d_up, d_down, total = layer(
+        with_z, grad_scale, tokens, cotangent, *weights, small, docs
     )
-    x_rows = tokens.astype(F32)
-    _, back_one = jax.vjp(layer_norm, x_rows, gains[0], gains[1])
-    resid = x_rows + tn(attn_t, out_mat)
-    norm_two, back_two = jax.vjp(layer_norm, resid, gains[2], gains[3])
-    act_two = norm_two.astype(BF16)
-    hidden = nt(act_two, up_mat)
-    acted, back_gelu = jax.vjp(gelu_tanh, hidden)
-    acted = acted.astype(BF16)
-    out_tokens = (resid + nn(acted, down_mat)).astype(BF16)
-    d_hidden = back_gelu(nt(cotangent, down_mat))[0].astype(BF16)
-    grad_down = tn(acted, cotangent)
-    grad_up = tn(d_hidden, act_two)
-    d_resid_norm, grad_gain_two, grad_shift_two = back_two(nn(d_hidden, up_mat))
-    d_resid = cotangent.astype(F32) + d_resid_norm
-    d_branch = d_resid.astype(BF16)
-    grad_out = nn(attn_t, d_branch)
-    d_attn = nt(d_branch, out_mat).astype(BF16)
-    dq, dkv, dsum = attention_back(qkv, psum, wsum, probs, d_attn)
-    flat = jnp.zeros((devices * spans + 2 * MOST, 2 * D), F32)
-    flat = lax.dynamic_update_slice_in_dim(flat, dsum[PSPANS:], first, 0)[MOST:-MOST]
-    row = jnp.arange(flat.shape[0])[:, None]
-    flat = jnp.where(row < PSPANS, 0.0, flat)
-    flat = flat.at[:PSPANS].add(dsum[:PSPANS])
-    span_grads = scatter(flat.astype(BF16)).astype(F32) / S
-    dkv = (dkv.reshape(spans, S, 2 * D) + span_grads[:, None]).reshape(tok, 2 * D)
-    dqkv = jnp.concatenate([dq, dkv.astype(BF16)], axis=1)
-    grad_qkv = tn(act_one, dqkv)
-    d_x_norm, grad_gain_one, grad_shift_one = back_one(nt(dqkv, qkv_mat))
-    d_tokens = d_resid + d_x_norm
-    small_grads = scatter(jnp.stack([grad_gain_one, grad_shift_one, grad_gain_two, grad_shift_two]), 1) * grad_scale
-    return (
-        out_tokens,
-        d_tokens,
-        join_parts(scatter(grad_qkv) * grad_scale),
-        scatter(grad_out) * grad_scale,
-        scatter(grad_up).T * grad_scale,
-        scatter(grad_down) * grad_scale,
-        small_grads[0],
-        small_grads[1],
-        small_grads[2],
-        small_grads[3],
-    )
+    d_qkv = jnp.concatenate([d_q, d_kv], axis=1)
+    if not with_z:
+        d_qkv, d_out, d_up, d_down = (
+            lax.psum_scatter(g, "head", scatter_dimension=0, tiled=True) for g in (d_qkv, d_out, d_up, d_down)
+        )
+    own = lax.dynamic_slice_in_dim(total, me * width, width, 1)
+    return out_tokens, d_tokens, join_parts(d_qkv), d_out, d_up.T, d_down, own[0], own[1], own[2], own[3]
 
 
 def solution(mesh):

time: 961 us -> 151 us (0.16)
  waiting for transfers between devices: 751 us -> 0 us
  matrix products: 54.6 us -> 0 us
  Pallas kernels: 92.5 us -> 136 us
  other arithmetic: 22.1 us -> 2.89 us
  local copies, waits for them, and re-layouts: 24.9 us -> 11.1 us
  between operations: 14.5 us -> 0.72 us
    reduce_scatter x5 -> x0, waiting for transfers between devices: 665 us -> none  [scatter(): return lax.psum_scatter(x, BOTH, scatter_dimension=axis, tiled=True)]
    unnamed x7 -> x0, waiting for transfers between devices: 86.7 us -> none
    dot_general x11 -> x0, matrix products: 54.6 us -> none  [the longest x4 24.1 us: tn(): lax.dot_general(a, b, (((0,), (0,)), ((), ())), preferred_element_type=F32)]
    pallas_call x2 -> x1, Pallas kernels: 92.5 us -> 136 us  [layer(): pl.pallas_call(functools.partial(layer_kernel, with_z, grad_scale), out_s...]
  transfers between devices with their start and end apart: 6 -> 0, of which waited for: 6 -> 0; matrix products, arithmetic and copies ran while one was open for 5% -> 0% of each run, Pallas kernels for 0% -> 0%
where the time goes in v4:
time: 151 us
  Pallas kernels  136 us (90%)
  local copies, waits for them, and re-layouts  11.1 us (7%)
  other arithmetic  2.89 us (2%)
    pallas_call x1, Pallas kernels, layer(): pl.pallas_call(functools.partial(layer_kernel, with_z, grad_scale), out_s...  136 us
    unnamed x13, local copies, waits for them, and re-layouts  5.52 us

profile of v4, /device:TPU:0, one launch (start us, length us, event | category | flops | bytes accessed | tf_op | source)
XLA Modules:
  0.0 151.0 jit_solution(13718399467092542760)
XLA Ops:
  0.7 0.7 pad_add_fusion
  1.4 0.1 dynamic_slice.6
  1.5 1.3 fusion.10.small_ref
  2.8 0.7 broadcast_in_dim.17.docs_ref
  3.5 1.0 reshape.33
  4.5 0.1 reshape.34
  4.6 0.6 slice.24.wq_ref
  5.2 0.6 slice.25.wkv_ref
  5.8 136.4 %mega_layer.1 = (bf16[1024,512]{1,0:T(8,128)(2,1)}, f32[1024,512]{1,0:T(8,128)}, f32[16,512]{1,0:T(8,128)}, f32[16,1024]{1,0:T(8,128)}, f32[16,512]{1,0:T(8,128)...) custom-call(bf16[1024,512]{1,0:T(8,128)(2,1)} %x_ref.1, bf16[1024,512]{1,0:T(8,128)(2,1)} %cot_ref.1, ...), custom_call_target="tpu_custom_call" | custom-call | tf_op jit(solution)/shard_map/mega_layer/pallas_call | solution.py:665
  142.2 0.0 copy-start
  142.2 0.9 constant_dynamic-slice_fusion
  143.1 0.5 slice_bitcast_fusion
  143.6 0.8 pad_maximum_fusion
  144.5 0.1 reshape.35
  144.6 0.1 copy.26
  144.6 0.8 reshape.36
  145.5 2.3 %copy.32 = bf16[1024,512]{1,0:T(8,128)(2,1)} copy(bf16[1024,512]{1,0:T(8,128)(2,1)} %get-tuple-element.40) | data formatting | bytes 2097152
  147.8 0.0 copy-done
  147.8 1.3 copy.33
  149.1 0.0 copy-done.3
  149.1 0.6 copy.34
  149.7 0.0 copy-done.2
  149.7 0.7 copy.35
  150.4 0.7 copy.36
  (7 shorter events, 0.0 us)
Async XLA Ops:
  142.2 5.6 %copy-start = (f32[1024,512]{1,0:T(8,128)S(1)}, f32[1024,512]{1,0:T(8,128)}, u32[]{:S(2)}) copy-start(f32[1024,512]{1,0:T(8,128)} %get-tuple-element.41) | copy-start | bytes 6291460
  147.8 1.3 copy-start.3
  147.8 1.9 %copy-start.2 = (f32[64,512]{1,0:T(8,128)S(1)}, f32[64,512]{1,0:T(8,128)}, u32[]{:S(2)}) copy-start(f32[64,512]{1,0:T(8,128)} %get-tuple-element.23) | copy-start | bytes 393220
  147.8 2.6 %copy-start.1 = (f32[64,512]{1,0:T(8,128)S(1)}, f32[64,512]{1,0:T(8,128)}, u32[]{:S(2)}) copy-start(f32[64,512]{1,0:T(8,128)} %get-tuple-element.45) | copy-start | bytes 393220

commit v5 on v4

--- a/solution.py
+++ b/solution.py
@@ -17,7 +17,8 @@
 WIN = 2 * MOST
 PAIRS = H // 2
 LANES = 2 * HD
-KEYS = S + PSPANS + WIN
+FAR = PSPANS + WIN
+KEYS = S + FAR
 EPS = 1e-05
 MASKED = -1e30
 F32 = jnp.float32
@@ -40,6 +41,18 @@
     return lax.dot_general(a, b, (((0,), (0,)), ((), ())), preferred_element_type=F32)
 
 
+def loop(start, stop, body):
+    def step(i, carry):
+        body(i)
+        return carry
+
+    lax.fori_loop(start, stop, step, 0)
+
+
+def tile_rows(i, size):
+    return pl.ds(pl.multiple_of(i * size, size), size)
+
+
 def summary_bias(first, span, docs_ref):
     index = first + span
     row = lax.broadcasted_iota(jnp.int32, (PSPANS, S), 0)
@@ -50,6 +63,15 @@
     return jnp.concatenate([prompt, window], axis=0).astype(F32)
 
 
+def window_docs(first, spans, span_doc_ref):
+    row = lax.broadcasted_iota(jnp.int32, (WIN, S), 0)
+    docs = jnp.full((WIN, S), -1, jnp.int32)
+    for i in range(MOST + spans):
+        at = first - MOST - PSPANS + i
+        docs = jnp.where((row == i) & (at >= 0), span_doc_ref[jnp.maximum(at, 0)], docs)
+    return docs
+
+
 def head_masks(scale):
     lane = lax.broadcasted_iota(jnp.int32, (1, LANES), 1)
     first = jnp.where(lane < HD, scale, 0.0).astype(BF16)
@@ -65,66 +87,103 @@
     return slice(part * D + pair * LANES, part * D + (pair + 1) * LANES)
 
 
-def all_keys(part, pair, rows, qkv_ref, psum_ref, wsum_ref):
-    cols = pair_cols(part, pair)
-    scols = pair_cols(part - 1, pair)
-    return jnp.concatenate([qkv_ref[rows, cols], psum_ref[:, scols], wsum_ref[:, scols]], axis=0)
-
-
 def unstack(pair_t):
     return jnp.concatenate([pair_t[:HD, :S], pair_t[HD:, S:]], axis=0)
 
 
-def attend_span(span, first, qkv_ref, psum_ref, wsum_ref, docs_ref, attn_t_ref, probs_ref):
-    rows = pl.ds(pl.multiple_of(span * S, S), S)
-    bias = summary_bias(first, span, docs_ref)
+def both_heads(pair):
+    return slice(pair * 2 * S, (pair + 1) * 2 * S)
+
+
+def span_scores(span, qkv_ref, scores_ref):
+    rows = tile_rows(span, S)
     key_row = lax.broadcasted_iota(jnp.int32, (S, S), 0)
     query = lax.broadcasted_iota(jnp.int32, (S, S), 1)
     causal = jnp.where(key_row <= query, 0.0, MASKED).astype(F32)
-    bias = jnp.concatenate([causal, bias], axis=0)
+    causal = jnp.concatenate([causal, causal], axis=1)
+    masks = head_masks(1.0 / math.sqrt(HD))
+    for pair in range(PAIRS):
+        queries = stack_heads(qkv_ref[rows, pair_cols(0, pair)], masks)
+        scores_ref[rows, both_heads(pair)] = nt(qkv_ref[rows, pair_cols(1, pair)], queries) + causal
+
+
+def attend_span(span, first, qkv_ref, sums_ref, sums_t_ref, docs_ref, scores_ref, attn_t_ref, probs_ref):
+    rows = tile_rows(span, S)
+    bias = summary_bias(first, span, docs_ref)
     bias = jnp.concatenate([bias, bias], axis=1)
     masks = head_masks(1.0 / math.sqrt(HD))
     for pair in range(PAIRS):
         queries = stack_heads(qkv_ref[rows, pair_cols(0, pair)], masks)
-        keys = all_keys(1, pair, rows, qkv_ref, psum_ref, wsum_ref)
-        vals = all_keys(2, pair, rows, qkv_ref, psum_ref, wsum_ref)
-        scores = nt(keys, queries) + bias
-        top = jnp.max(scores, axis=0, keepdims=True)
-        grown = jnp.exp(scores - top)
-        share = 1.0 / jnp.sum(grown, axis=0, keepdims=True)
-        probs = (grown * share).astype(BF16)
+        own = scores_ref[rows, both_heads(pair)]
+        far = nt(sums_ref[:, pair_cols(0, pair)], queries) + bias
+        top = jnp.maximum(jnp.max(own, axis=0, keepdims=True), jnp.max(far, axis=0, keepdims=True))
+        own, far = jnp.exp(own - top), jnp.exp(far - top)
+        share = 1.0 / (jnp.sum(own, axis=0, keepdims=True) + jnp.sum(far, axis=0, keepdims=True))
+        probs = jnp.concatenate([(own * share).astype(BF16), (far * share).astype(BF16)], axis=0)
         probs_ref[span * PAIRS + pair] = probs
-        mixed = nn(vals.T, probs)
-        attn_t_ref[pair * LANES : (pair + 1) * LANES, rows] = unstack(mixed).astype(BF16)
-
-
-def attend_span_back(
-    span, qkv_ref, psum_ref, wsum_ref, probs_ref, dattn_ref, dq_ref, dkv_ref, dsum_ref
-):
-    rows = pl.ds(pl.multiple_of(span * S, S), S)
+        vals_t = jnp.concatenate([qkv_ref[rows, pair_cols(2, pair)].T, sums_t_ref[pair_cols(1, pair), :]], axis=1)
+        attn_t_ref[pair * LANES : (pair + 1) * LANES, rows] = unstack(nn(vals_t, probs)).astype(BF16)
+
+
+def summary_back(span, qkv_ref, sums_ref, probs_ref, attn_t_ref, dattn_ref, delta_ref, dsum_ref):
+    rows = tile_rows(span, S)
+    masks = head_masks(1.0 / math.sqrt(HD))
+    ones = head_masks(1.0)
+    for pair in range(PAIRS):
+        cols, vcols = pair_cols(0, pair), pair_cols(1, pair)
+        block = dattn_ref[rows, cols]
+        each = block.T.astype(F32) * attn_t_ref[pair * LANES : (pair + 1) * LANES, rows].astype(F32)
+        delta = jnp.concatenate(
+            [jnp.sum(each[:HD], axis=0, keepdims=True), jnp.sum(each[HD:], axis=0, keepdims=True)], axis=1
+        )
+        delta_ref[pl.ds(span * PAIRS + pair, 1), :] = delta
+        queries = stack_heads(qkv_ref[rows, cols], masks)
+        grads = stack_heads(block, ones)
+        probs = probs_ref[span * PAIRS + pair, S:, :]
+        dprobs = nt(sums_ref[:, vcols], grads)
+        dscores = (probs.astype(F32) * (dprobs - delta)).astype(BF16)
+        dsum_ref[:, cols] += nn(dscores, queries)
+        dsum_ref[:, vcols] += nn(probs, grads)
+        probs_ref[span * PAIRS + pair, S:, :] = dscores
+
+
+def span_back(span, qkv_ref, sums_t_ref, probs_ref, dattn_ref, delta_ref, dqkv_ref, dkv_ref):
+    rows = tile_rows(span, S)
     scale = 1.0 / math.sqrt(HD)
     masks = head_masks(scale)
     ones = head_masks(1.0)
     for pair in range(PAIRS):
-        cols = pair_cols(0, pair)
+        cols, vcols = pair_cols(0, pair), pair_cols(1, pair)
         queries = stack_heads(qkv_ref[rows, cols], masks)
-        keys = all_keys(1, pair, rows, qkv_ref, psum_ref, wsum_ref)
-        vals = all_keys(2, pair, rows, qkv_ref, psum_ref, wsum_ref)
         grads = stack_heads(dattn_ref[rows, cols], ones)
-        probs = probs_ref[span * PAIRS + pair]
-        wide = probs.astype(F32)
-        dprobs = nt(vals, grads)
-        delta = jnp.sum(wide * dprobs, axis=0, keepdims=True)
-        dscores = (wide * (dprobs - delta)).astype(BF16)
-        dq_t = unstack(nn(keys.T, dscores)) * scale
-        dq_ref[rows, cols] = dq_t.T.astype(BF16)
-        dkeys = nn(dscores, queries)
-        dvals = nn(probs, grads)
-        vcols = pair_cols(1, pair)
-        dkv_ref[rows, cols] = dkeys[:S]
-        dkv_ref[rows, vcols] = dvals[:S]
-        dsum_ref[:, cols] += dkeys[S:]
-        dsum_ref[:, vcols] += dvals[S:]
+        probs = probs_ref[span * PAIRS + pair, :S, :]
+        dprobs = nt(qkv_ref[rows, pair_cols(2, pair)], grads)
+        delta = delta_ref[pl.ds(span * PAIRS + pair, 1), :]
+        dscores = (probs.astype(F32) * (dprobs - delta)).astype(BF16)
+        dkv_ref[rows, cols] = nn(dscores, queries)
+        dkv_ref[rows, vcols] = nn(probs, grads)
+        every = jnp.concatenate([dscores, probs_ref[span * PAIRS + pair, S:, :]], axis=0)
+        keys_t = jnp.concatenate([qkv_ref[rows, pair_cols(1, pair)].T, sums_t_ref[cols, :]], axis=1)
+        dq_t = unstack(nn(keys_t, every)) * scale
+        dqkv_ref[rows, cols] = dq_t.T.astype(BF16)
+
+
+def split_heads(block, parts):
+    low = lax.broadcasted_iota(jnp.int32, (1, LANES), 1) < HD
+    for pair in range(PAIRS):
+        one, two, three = [block[:, (3 * pair + i) * LANES : (3 * pair + i + 1) * LANES].astype(F32) for i in range(3)]
+        mixed = jnp.where(low, one, two), pltpu.roll(jnp.where(low, three, one), HD, 1), jnp.where(low, two, three)
+        for part, value in zip(parts, mixed):
+            part[:, pair * LANES : (pair + 1) * LANES] = value.astype(part.dtype)
+
+
+def join_heads(parts, out_ref):
+    low = lax.broadcasted_iota(jnp.int32, (1, LANES), 1) < HD
+    for pair in range(PAIRS):
+        q, k, v = [part[:, pair * LANES : (pair + 1) * LANES] for part in parts]
+        k = pltpu.roll(k, HD, 1)
+        for i, value in enumerate((jnp.where(low, q, k), jnp.where(low, v, q), jnp.where(low, k, v))):
+            out_ref[:, (3 * pair + i) * LANES : (3 * pair + i + 1) * LANES] = value
 
 
 MESH = pl.DeviceIdType.MESH
@@ -220,38 +279,41 @@
         self.sent += self.moves
         self.placed = self.w.local(self.shard, own)
 
-    def _next(self, sources, axis, fresh):
+    def _line(self, step):
+        p, n = self.p, self.p.side
+        y1, x1 = p.along(1, step)
+        turn = 1 - p.c
+        mine = [p.along(0, d) for d in range(n)]
+        return [(turn * y1 + (1 - turn) * y, turn * x + (1 - turn) * x1) for y, x in mine]
+
+    def _send(self, place, device):
+        move = self.w.copy(self.block(*place), self.block(*place), device)
+        self.sent.append(move)
+        return move
+
+    def step1(self):
+        p = self.p
         for move in self.moves:
             move.wait_recv()
+        self.placed.wait()
+        own = (p.y, p.x)
+        self.moves = [self._send(own, d) for d in p.peers(0)]
+        self.turned = [self._send(own, d) for d in p.peers(1)]
+        self.across = [self._send(own, p.sibling())]
+
+    def step2(self):
         p = self.p
-        self.moves = []
-        if axis is not None:
-            self.moves = [self.w.copy(self.block(*s), self.block(*s), d) for d in p.peers(axis) for s in sources]
-        more = [self.w.copy(self.block(*s), self.block(*s), p.sibling()) for s in fresh]
-        self.across += more
-        self.sent += self.moves + more
-
-    def step1(self):
-        self.placed.wait()
-        self.across = []
-        here = [(self.p.y, self.p.x)]
-        self._next(here, 0, here)
-
-    def _line(self, step):
-        p, n = self.p, self.p.side
-        mine = [p.along(0, d) for d in range(n)]
-        if step == 0:
-            return mine
-        y1, x1 = p.along(1, step)
-        turn = 1 - p.c
-        return [(turn * y1 + (1 - turn) * y, turn * x + (1 - turn) * x1) for y, x in mine]
-
-    def step2(self):
-        line = self._line(0)
-        self._next(line, 1, line[1:])
+        for move in self.moves:
+            move.wait_recv()
+        line = self._line(0)[1:]
+        self.turned += [self._send(place, d) for d in p.peers(1) for place in line]
+        self.across += [self._send(place, p.sibling()) for place in line]
 
     def step3(self):
-        self._next([], None, [s for e in range(1, self.p.side) for s in self._line(e)])
+        for move in self.turned:
+            move.wait_recv()
+        p = self.p
+        self.across += [self._send(place, p.sibling()) for e in range(1, p.side) for place in self._line(e)]
 
     def step4(self):
         for move in self.across:
@@ -403,32 +465,26 @@
         self.sums[level + 1] = total
 
 
-def loop(start, stop, body):
-    def step(i, carry):
-        body(i)
-        return carry
-
-    lax.fori_loop(start, stop, step, 0)
-
-
-def tile_rows(i, size):
-    return pl.ds(pl.multiple_of(i * size, size), size)
-
-
 def layer_kernel(
     with_z, grad_scale,
-    x_ref, cot_ref, wq_ref, wkv_ref, wo_ref, wu_ref, wd_ref, small_ref, docs_ref,
-    out_ref, dtok_ref, dwq_ref, dwkv_ref, dwo_ref, dwu_ref, dwd_ref, total_ref,
-    q_mat, kv_mat, out_mat, up_mat, down_mat, gains_ref, small_all, own_sums, sums_all, psum_ref, wsum_ref,
+    x_hbm, cot_hbm, wqkv_ref, wo_ref, wu_ref, wd_ref, gain1_ref, shift1_ref, gain2_ref, shift2_ref, span_doc_ref,
+    out_hbm, dtok_hbm, dwqkv_ref, dwo_hbm, dwu_hbm, dwd_hbm, total_ref,
+    x_ref, cot_ref, dtok_ref, dwo_ref, dwu_ref, dwd_ref, small_ref, docs_ref, own_q, own_k, own_v,
+    q_mat, k_mat, v_mat, out_mat, up_mat, down_mat, gains_ref, small_all, own_sums, sums_all, sums_ref, sums_t_ref,
     act_ref, qkv_ref, probs_ref, attn_t_ref, resid_ref, act2_ref, acted_ref, dhid_ref, dattn_ref,
-    gdown_ref, gup_ref, gout_ref, gq_ref, gkv_ref, dkv_ref, dsum_ref, sums_ref, came_ref, send, recv, *held,
+    gdown_ref, gup_ref, gout_ref, gq_ref, gk_ref, gv_ref, dkv_ref, delta_ref, dsum_ref, levels_ref, came_ref,
+    send, recv, place_sem, *held,
 ):
     place = Place()
     wires = Wires(send, recv)
     tok = x_ref.shape[0]
     spans = tok // S
+    tiles = tok // TILE
     first = place.me * spans
     held = list(held)
+    local = [pltpu.make_async_copy(x_hbm, x_ref, place_sem.at[0]), pltpu.make_async_copy(cot_hbm, cot_ref, place_sem.at[1])]
+    for move in local:
+        move.start()
 
     def gather(shard, full):
         return Gather(wires, place, shard, full, shard.shape[0], with_z)
@@ -439,25 +495,35 @@
 
     small = Gather(wires, place, small_ref, small_all, 1, True)
     sums = Gather(wires, place, own_sums, sums_all, 1, True)
-    g_kv, g_q, g_out = gather(wkv_ref, kv_mat), gather(wq_ref, q_mat), gather(wo_ref, out_mat)
+    g_k, g_v, g_q, g_out = gather(own_k, k_mat), gather(own_v, v_mat), gather(own_q, q_mat), gather(wo_ref, out_mat)
     g_down, g_up = gather(wd_ref, down_mat), gather(wu_ref, up_mat)
-    dsums_ref = sums_all
-    s_sum = scatter(dsums_ref, True)
-    s_down, s_up, s_out, s_q, s_kv = [scatter(g, with_z) for g in (gdown_ref, gup_ref, gout_ref, gq_ref, gkv_ref)]
-
+    s_sum = scatter(sums_all, True)
+    s_down, s_up, s_out, s_q, s_k, s_v = [
+        scatter(g, with_z) for g in (gdown_ref, gup_ref, gout_ref, gq_ref, gk_ref, gv_ref)
+    ]
+
+    width = gain1_ref.shape[1]
+    small_ref[...] = jnp.zeros_like(small_ref)
+    for k, ref in enumerate((gain1_ref, shift1_ref, gain2_ref, shift2_ref)):
+        small_ref[0, k : k + 1, :width] = ref[...].astype(F32)
+    split_heads(wqkv_ref[...], (own_q, own_k, own_v))
     place.greet()
-    for g in (small, g_kv, g_q, g_out, g_down, g_up):
+    for g in (small, g_k, g_v, g_q, g_down, g_out, g_up):
         g.step0()
     small.step1()
-    g_kv.step1()
+    g_k.step1()
+    g_v.step1()
+    small.step2()
+    g_k.step2()
     g_q.step1()
-    small.step2()
-    g_kv.step2()
+    g_v.step2()
+    small.step3()
+    g_k.step3()
     g_q.step2()
-    small.step3()
-    g_kv.step3()
+    docs_ref[...] = window_docs(first, spans, span_doc_ref)
     small.step4()
     gains_ref[...] = spread_small(small_all[...], place.devices)
+    local[0].wait()
 
     def norm(i):
         rows = tile_rows(i, S)
@@ -465,47 +531,56 @@
         act_ref[rows, :] = (xhat * gains_ref[0:1, :] + gains_ref[1:2, :]).astype(BF16)
 
     loop(0, spans, norm)
-    g_kv.step4()
+    g_v.step3()
+    g_k.step4()
+    g_down.step1()
+    g_out.step1()
+
+    def project(mat, part):
+        block = nn(act_ref[...], mat[...]).astype(BF16)
+        qkv_ref[:, part * D : (part + 1) * D] = block
+        if part:
+            mean = jnp.sum(block.astype(F32).reshape(spans, S, D), axis=1) * (1.0 / S)
+            own_sums[0, :, (part - 1) * D : part * D] = mean.astype(BF16)
+
+    project(k_mat, 1)
     g_q.step3()
-    g_out.step1()
-    for part in (0, 1):
-        block = nn(act_ref[...], kv_mat[:, part * D : (part + 1) * D]).astype(BF16)
-        qkv_ref[:, (part + 1) * D : (part + 2) * D] = block
-        mean = jnp.sum(block.astype(F32).reshape(spans, S, D), axis=1) * (1.0 / S)
-        own_sums[0, :, part * D : (part + 1) * D] = mean.astype(BF16)
-        if part == 0:
-            g_down.step1()
+    g_v.step4()
+    project(v_mat, 2)
     sums.step0()
     g_q.step4()
-    qkv_ref[:, :D] = nn(act_ref[...], q_mat[...]).astype(BF16)
+    project(q_mat, 0)
     sums.step1()
+    half = spans // 2
+    loop(0, half, lambda i: span_scores(i, qkv_ref, dkv_ref))
+    sums.step2()
     g_out.step2()
     g_down.step2()
-    sums.step2()
+    loop(half, spans, lambda i: span_scores(i, qkv_ref, dkv_ref))
+    sums.step3()
     g_up.step1()
-    sums.step3()
     sums.step4()
     for i in range(PSPANS // MOST):
         two = sums_all[pl.ds(2 * i, 2)].astype(F32)
-        psum_ref[MOST * i : MOST * (i + 1), :] = two.reshape(MOST, 2 * D).astype(BF16)
+        sums_ref[MOST * i : MOST * (i + 1), :] = two.reshape(MOST, 2 * D).astype(BF16)
     before = sums_all[pl.ds(lax.rem(place.me + place.devices - 2, place.devices), 1)].astype(F32)
     last = sums_all[pl.ds(lax.rem(place.me + place.devices - 1, place.devices), 1)].astype(F32)
     here = sums_all[pl.ds(place.me, 1)].astype(F32)
-    wsum_ref[:MOST, :] = jnp.concatenate([before, last], axis=0).reshape(MOST, 2 * D).astype(BF16)
-    wsum_ref[MOST:, :] = jnp.concatenate([here, jnp.zeros_like(here)], axis=0).reshape(MOST, 2 * D).astype(BF16)
+    nothing = jnp.zeros_like(here)
+    sums_ref[PSPANS : PSPANS + MOST, :] = jnp.concatenate([before, last], axis=0).reshape(MOST, 2 * D).astype(BF16)
+    sums_ref[PSPANS + MOST :, :] = jnp.concatenate([here, nothing], axis=0).reshape(MOST, 2 * D).astype(BF16)
+    sums_t_ref[...] = sums_ref[...].T
 
     def attend(span):
-        attend_span(span, first, qkv_ref, psum_ref, wsum_ref, docs_ref, attn_t_ref, probs_ref)
+        attend_span(span, first, qkv_ref, sums_ref, sums_t_ref, docs_ref, dkv_ref, attn_t_ref, probs_ref)
 
     quarter = spans // 4
     loop(0, quarter, attend)
-    g_up.step2()
     g_out.step3()
     loop(quarter, 2 * quarter, attend)
+    g_up.step2()
     g_down.step3()
-    loop(2 * quarter, 3 * quarter, attend)
-    g_up.step3()
-    loop(3 * quarter, spans, attend)
+    loop(2 * quarter, spans, attend)
     g_out.step4()
 
     def residual(i):
@@ -515,7 +590,9 @@
         xhat, _ = normed_parts(resid)
         act2_ref[rows, :] = (xhat * gains_ref[2:3, :] + gains_ref[3:4, :]).astype(BF16)
 
-    loop(0, tok // TILE, residual)
+    loop(0, tiles, residual)
+    local[1].wait()
+    g_up.step3()
     g_down.step4()
     g_up.step4()
 
@@ -530,6 +607,7 @@
         gup_ref[part, :] = tn(dhid, act2_ref[...]).astype(BF16)
 
     both = (s_down, s_up)
+    waiting = []
     if s_up.group == CHUNK:
         for d, e in s_up.order:
             theirs = 2 * s_up.at(1 - place.c, d, e) + 1 - place.c
@@ -537,116 +615,150 @@
             loop(0, 2, lambda i: feed(theirs + i * (ours - theirs)))
             for s in both:
                 s.cross(d, e)
-            for s in both:
-                s.fold(d, e)
-            if d == 0:
-                for s in both:
-                    s.turn(e)
+            waiting.append((d, e))
+            if len(waiting) > 1:
+                fold_all(both, *waiting.pop(0))
     else:
         loop(0, up_mat.shape[0] // CHUNK, feed)
         for s in both:
             s.step0()
-        for s in both:
-            s.step1()
-        for s in both:
-            s.step2()
-    sums_ref[...] = jnp.zeros_like(sums_ref)
+        waiting = list(s_up.order)
+    levels_ref[...] = jnp.zeros_like(levels_ref)
 
     def finish(i):
         rows = tile_rows(i, TILE)
         dnormed = nn(dhid_ref[rows, :], up_mat[...])
         xhat, inverse = normed_parts(resid_ref[rows, :])
-        sums_ref[0, 2:3, :] += jnp.sum(dnormed * xhat, axis=0, keepdims=True)
-        sums_ref[0, 3:4, :] += jnp.sum(dnormed, axis=0, keepdims=True)
+        levels_ref[0, 2:3, :] += jnp.sum(dnormed * xhat, axis=0, keepdims=True)
+        levels_ref[0, 3:4, :] += jnp.sum(dnormed, axis=0, keepdims=True)
         dresid = cot_ref[rows, :].astype(F32) + norm_back(dnormed, xhat, inverse, gains_ref[2:3, :])
         dtok_ref[rows, :] = dresid
         branch = dresid.astype(BF16)
         act2_ref[rows, :] = branch
         dattn_ref[rows, :] = nt(branch, out_mat[...]).astype(BF16)
 
-    loop(0, tok // TILE, finish)
-    for s in both:
-        s.step3()
+    loop(0, tiles // 2, finish)
+    for d, e in waiting:
+        fold_all(both, d, e)
+    for e in s_up.line[:-1]:
+        for s in both:
+            s.turn(e)
+    loop(tiles // 2, tiles, finish)
     gout_ref[...] = nn(attn_t_ref[...], act2_ref[...]).astype(BF16)
     s_out.step0()
     dsum_ref[...] = jnp.zeros_like(dsum_ref)
 
-    def attend_back(span):
-        attend_span_back(
-            span, qkv_ref, psum_ref, wsum_ref, probs_ref, dattn_ref, dhid_ref, dkv_ref, dsum_ref
-        )
-
-    loop(0, quarter, attend_back)
+    def back_far(span):
+        summary_back(span, qkv_ref, sums_ref, probs_ref, attn_t_ref, dattn_ref, delta_ref, dsum_ref)
+
+    def back_near(span):
+        span_back(span, qkv_ref, sums_t_ref, probs_ref, dattn_ref, delta_ref, dhid_ref, dkv_ref)
+
+    loop(0, quarter, back_far)
     s_out.step1()
-    loop(quarter, 2 * quarter, attend_back)
+    loop(quarter, 2 * quarter, back_far)
+    for s in both:
+        s.turn(0)
+    loop(2 * quarter, 3 * quarter, back_far)
     s_out.step2()
-    loop(2 * quarter, 3 * quarter, attend_back)
-    s_out.step3()
-    loop(3 * quarter, spans, attend_back)
-
+    loop(3 * quarter, spans, back_far)
     wires.settle(sums.sent)
-    dsums_ref[...] = jnp.zeros_like(dsums_ref)
+    sums_all[...] = jnp.zeros_like(sums_all)
     for i in range(3):
         block = lax.rem(place.me + place.devices - 2 + i, place.devices)
         rows = slice(PSPANS + i * spans, PSPANS + (i + 1) * spans)
-        dsums_ref[pl.ds(block, 1)] = dsum_ref[rows, :].astype(BF16)[None]
+        sums_all[pl.ds(block, 1)] = dsum_ref[rows, :].astype(BF16)[None]
     for i in range(PSPANS // spans):
-        dsums_ref[i] = dsum_ref[i * spans : (i + 1) * spans, :].astype(BF16)
+        sums_all[i] = dsum_ref[i * spans : (i + 1) * spans, :].astype(BF16)
     s_sum.step0()
+    loop(0, quarter, back_near)
+    s_sum.step1()
+    loop(quarter, 2 * quarter, back_near)
+    s_sum.step2()
+    loop(2 * quarter, 3 * quarter, back_near)
+    s_sum.step3()
+    for s in both:
+        s.step3()
+    s_out.step3()
+    loop(3 * quarter, spans, back_near)
     gq_ref[...] = tn(act_ref[...], dhid_ref[:, :D]).astype(BF16)
-    s_sum.step1()
     s_q.step0()
-    s_sum.step2()
+    shares = s_sum.step4()[0] * (1.0 / S)
+    for part, g_ref, s in ((0, gk_ref, s_k), (1, gv_ref, s_v)):
+        cols = slice(part * D, (part + 1) * D)
+        for span in range(spans):
+            rows = slice(span * S, (span + 1) * S)
+            dhid_ref[rows, (part + 1) * D : (part + 2) * D] = (dkv_ref[rows, cols] + shares[span : span + 1, cols]).astype(BF16)
+        g_ref[...] = tn(act_ref[...], dhid_ref[:, (part + 1) * D : (part + 2) * D]).astype(BF16)
+        s.step0()
+
+    def write(ref, hbm, i, rows=slice(None)):
+        move = pltpu.make_async_copy(ref.at[rows], hbm.at[rows], place_sem.at[i])
+        move.start()
+        local.append(move)
+
+    def finish_tokens(i):
+        rows = slice(i * TILE, (i + 1) * TILE)
+        dnormed = nt(dhid_ref[rows, :D], q_mat[...]) + nt(dhid_ref[rows, D : 2 * D], k_mat[...])
+        dnormed = dnormed + nt(dhid_ref[rows, 2 * D : 3 * D], v_mat[...])
+        xhat, inverse = normed_parts(x_ref[rows, :].astype(F32))
+        levels_ref[0, 0:1, :] += jnp.sum(dnormed * xhat, axis=0, keepdims=True)
+        levels_ref[0, 1:2, :] += jnp.sum(dnormed, axis=0, keepdims=True)
+        dtok_ref[rows, :] += norm_back(dnormed, xhat, inverse, gains_ref[0:1, :])
+
+    def output(i):
+        rows = slice(i * TILE, (i + 1) * TILE)
+        act2_ref[rows, :] = (resid_ref[rows, :] + nn(acted_ref[rows, :], down_mat[...])).astype(BF16)
+
+    total = Total(wires, place, levels_ref, came_ref)
+    finish_tokens(0)
     s_q.step1()
+    s_k.step1()
+    finish_tokens(1)
+    s_v.step1()
+    finish_tokens(2)
+    s_q.step2()
+    finish_tokens(3)
+    total.send(0)
+    s_k.step2()
+    write(dtok_ref, dtok_hbm, 2)
+    output(0)
+    total.take(0)
+    total.send(1)
+    s_v.step2()
+    output(1)
+    s_q.step3()
+    s_k.step3()
+    output(2)
+    total.take(1)
+    total.send(2)
+    s_v.step3()
+    output(3)
+    write(act2_ref, out_hbm, 3)
     dwd_ref[...] = s_down.step4() * grad_scale
     dwu_ref[...] = s_up.step4() * grad_scale
     dwo_ref[...] = s_out.step4() * grad_scale
-    s_sum.step3()
-    s_q.step2()
-    shares = s_sum.step4()[0] * (1.0 / S)
-    for span in range(spans):
-        rows = slice(span * S, (span + 1) * S)
-        dhid_ref[rows, D : 3 * D] = (dkv_ref[rows, :] + shares[span : span + 1, :]).astype(BF16)
-    gkv_ref[...] = tn(act_ref[...], dhid_ref[:, D : 3 * D]).astype(BF16)
-    s_kv.step0()
-    s_q.step3()
-
-    def last(i):
-        rows = tile_rows(i, TILE)
-        dnormed = nt(dhid_ref[rows, :D], q_mat[...]) + nt(dhid_ref[rows, D : 3 * D], kv_mat[...])
-        xhat, inverse = normed_parts(x_ref[rows, :].astype(F32))
-        sums_ref[0, 0:1, :] += jnp.sum(dnormed * xhat, axis=0, keepdims=True)
-        sums_ref[0, 1:2, :] += jnp.sum(dnormed, axis=0, keepdims=True)
-        dtok_ref[rows, :] += norm_back(dnormed, xhat, inverse, gains_ref[0:1, :])
-
-    def output(i):
-        rows = tile_rows(i, TILE)
-        out_ref[rows, :] = (resid_ref[rows, :] + nn(acted_ref[rows, :], down_mat[...])).astype(BF16)
-
-    half = tok // TILE // 2
-    loop(0, half, last)
-    s_kv.step1()
-    loop(half, 2 * half, last)
-    total = Total(wires, place, sums_ref, came_ref)
-    total.send(0)
-    loop(0, half, output)
-    total.take(0)
-    total.send(1)
-    s_kv.step2()
-    loop(half, 2 * half, output)
-    total.take(1)
-    total.send(2)
-    s_kv.step3()
-    dwq_ref[...] = s_q.step4() * grad_scale
+    write(dwd_ref, dwd_hbm, 4)
+    write(dwu_ref, dwu_hbm, 5)
+    write(dwo_ref, dwo_hbm, 6)
     total.take(2)
     total.send(3)
-    dwkv_ref[...] = s_kv.step4() * grad_scale
+    join_heads((s_q.step4() * grad_scale, s_k.step4() * grad_scale, s_v.step4() * grad_scale), dwqkv_ref)
     total.take(3)
-    total_ref[...] = sums_ref[4] * grad_scale
+    start = place.me * width
+    lanes = pl.ds(pl.multiple_of(start // LANES * LANES, LANES), LANES)
+    total_ref[...] = pltpu.roll(levels_ref[4, :, lanes] * grad_scale, lax.rem(LANES - lax.rem(start, LANES), LANES), 1)
+    for move in local[2:]:
+        move.wait()
     wires.finish()
 
 
-def layer(with_z, grad_scale, x, cotangent, wq, wkv, wo, wu, wd, small, docs):
+def fold_all(scatters, d, e):
+    for s in scatters:
+        s.fold(d, e)
+
+
+def layer(with_z, grad_scale, x, cotangent, wqkv, wo, wu, wd, vectors, span_doc):
     tok = x.shape[0]
     spans = tok // S
     deep = lax.axis_size("head")
@@ -654,31 +766,42 @@
     devices = 2 * side * side * deep
     owned = devices if with_z else devices // deep
     hidden_size = wu.shape[0] * owned
-    whole = pl.BlockSpec(memory_space=VMEM)
+    whole, anywhere = pl.BlockSpec(memory_space=VMEM), pl.BlockSpec(memory_space=pl.ANY)
     shape = jax.ShapeDtypeStruct
     peers = 1 + 2 * (side - 1) + deep - 1
-    n = 7 * copies_of_gather(side, deep, True) + 7
-    n += 6 * (side * side + (side - 1) * side + side - 1 + deep - 1) + peers
+    n = 8 * copies_of_gather(side, deep, True) + 8
+    n += 7 * (side * side + (side - 1) * side + side - 1 + deep - 1) + peers
     held = scatter_scratch(side, deep, 1, (spans, 2 * D), True)
-    for total, columns in ((hidden_size, D), (hidden_size, D), (D, D), (D, D), (D, 2 * D)):
-        held += scatter_scratch(side, deep, total // devices, (columns,), with_z)
+    for total in (hidden_size, hidden_size, D, D, D, D):
+        held += scatter_scratch(side, deep, total // devices, (D,), with_z)
     return pl.pallas_call(
         functools.partial(layer_kernel, with_z, grad_scale),
         out_shape=(
             shape((tok, D), BF16),
             shape((tok, D), F32),
-            shape((D // owned, D), F32),
-            shape((D // owned, 2 * D), F32),
+            shape((D // owned, 3 * D), F32),
             shape((D // owned, D), F32),
             shape((hidden_size // owned, D), F32),
             shape((hidden_size // owned, D), F32),
-            shape((8, D), F32),
+            shape((8, LANES), F32),
         ),
-        in_specs=[whole] * 9,
-        out_specs=(whole,) * 8,
+        in_specs=[anywhere] * 2 + [whole] * 8 + [pl.BlockSpec(memory_space=pltpu.MemorySpace.SMEM)],
+        out_specs=(anywhere, anywhere, whole, anywhere, anywhere, anywhere, whole),
         scratch_shapes=[
+            pltpu.VMEM((tok, D), BF16),
+            pltpu.VMEM((tok, D), BF16),
+            pltpu.VMEM((tok, D), F32),
+            pltpu.VMEM((D // owned, D), F32),
+            pltpu.VMEM((hidden_size // owned, D), F32),
+            pltpu.VMEM((hidden_size // owned, D), F32),
+            pltpu.VMEM((1, 8, LANES), F32),
+            pltpu.VMEM((WIN, S), jnp.int32),
+            pltpu.VMEM((D // owned, D), BF16),
+            pltpu.VMEM((D // owned, D), BF16),
+            pltpu.VMEM((D // owned, D), BF16),
             pltpu.VMEM((D, D), BF16),
-            pltpu.VMEM((D, 2 * D), BF16),
+            pltpu.VMEM((D, D), BF16),
+            pltpu.VMEM((D, D), BF16),
             pltpu.VMEM((D, D), BF16),
             pltpu.VMEM((hidden_size, D), BF16),
             pltpu.VMEM((hidden_size, D), BF16),
@@ -686,8 +809,8 @@
             pltpu.VMEM((devices, 8, LANES), F32),
             pltpu.VMEM((1, spans, 2 * D), BF16),
             pltpu.VMEM((devices, spans, 2 * D), BF16),
-            pltpu.VMEM((PSPANS, 2 * D), BF16),
-            pltpu.VMEM((WIN, 2 * D), BF16),
+            pltpu.VMEM((FAR, 2 * D), BF16),
+            pltpu.VMEM((2 * D, FAR), BF16),
             pltpu.VMEM((tok, D), BF16),
             pltpu.VMEM((tok, 3 * D), BF16),
             pltpu.VMEM((spans * PAIRS, KEYS, 2 * S), BF16),
@@ -701,56 +824,41 @@
             pltpu.VMEM((hidden_size, D), BF16),
             pltpu.VMEM((D, D), BF16),
             pltpu.VMEM((D, D), BF16),
-            pltpu.VMEM((D, 2 * D), BF16),
+            pltpu.VMEM((D, D), BF16),
+            pltpu.VMEM((D, D), BF16),
             pltpu.VMEM((tok, 2 * D), F32),
-            pltpu.VMEM((PSPANS + WIN, 2 * D), F32),
+            pltpu.VMEM((spans * PAIRS, 2 * S), F32),
+            pltpu.VMEM((FAR, 2 * D), F32),
             pltpu.VMEM((5, 8, D), F32),
             pltpu.VMEM((peers, 8, D), F32),
             pltpu.SemaphoreType.DMA((n,)),
             pltpu.SemaphoreType.DMA((n,)),
+            pltpu.SemaphoreType.DMA((7,)),
             *held,
         ],
         compiler_params=pltpu.CompilerParams(vmem_limit_bytes=VMEM_LIMIT, collective_id=0, has_side_effects=True),
         name="mega_layer",
-    )(x, cotangent, wq, wkv, wo, wu, wd, small, docs)
-
-
-def split_parts(weight):
-    rows = weight.shape[0]
-    return weight.reshape(rows, H, 3, HD).transpose(0, 2, 1, 3).reshape(rows, 3 * D)
-
-
-def join_parts(weight):
-    rows = weight.shape[0]
-    return weight.reshape(rows, 3, H, HD).transpose(0, 2, 1, 3).reshape(rows, 3 * D)
+    )(x, cotangent, wqkv, wo, wu, wd, *vectors, span_doc)
 
 
 def shards(tokens, cotangent, w_qkv, w_out, w_up, w_down, gain_one, shift_one, gain_two, shift_two, span_doc):
     tok = tokens.shape[0]
     devices = lax.axis_size("seq") * lax.axis_size("head")
-    me = lax.axis_index("seq") * lax.axis_size("head") + lax.axis_index("head")
     grad_scale = 1.0 / math.sqrt(tok * devices)
-    docs = jnp.concatenate([jnp.full((PSPANS + MOST,), -1, jnp.int32), span_doc, jnp.full((MOST,), -1, jnp.int32)])
-    docs = lax.dynamic_slice_in_dim(docs, me * (tok // S), WIN, 0)
-    docs = jnp.broadcast_to(docs[:, None], (WIN, S))
     with_z = w_qkv.shape[0] % 16 == 0
-    w_qkv = split_parts(w_qkv)
-    weights = (w_qkv[:, :D], w_qkv[:, D:], w_out, w_up.T, w_down)
+    weights = (w_qkv, w_out, w_up.T, w_down)
     if not with_z:
         weights = tuple(lax.all_gather(w, "head", axis=0, tiled=True) for w in weights)
-    small = jnp.stack([gain_one, shift_one, gain_two, shift_two]).astype(F32)
-    width = small.shape[1]
-    small = jnp.pad(small, ((0, 4), (0, LANES - width)))[None]
-    out_tokens, d_tokens, d_q, d_kv, d_out, d_up, d_down, total = layer(
-        with_z, grad_scale, tokens, cotangent, *weights, small, docs
+    vectors = [v[None] for v in (gain_one, shift_one, gain_two, shift_two)]
+    width = gain_one.shape[0]
+    out_tokens, d_tokens, d_qkv, d_out, d_up, d_down, total = layer(
+        with_z, grad_scale, tokens, cotangent, *weights, vectors, span_doc
     )
-    d_qkv = jnp.concatenate([d_q, d_kv], axis=1)
     if not with_z:
         d_qkv, d_out, d_up, d_down = (
             lax.psum_scatter(g, "head", scatter_dimension=0, tiled=True) for g in (d_qkv, d_out, d_up, d_down)
         )
-    own = lax.dynamic_slice_in_dim(total, me * width, width, 1)
-    return out_tokens, d_tokens, join_parts(d_qkv), d_out, d_up.T, d_down, own[0], own[1], own[2], own[3]
+    return out_tokens, d_tokens, d_qkv, d_out, d_up.T, d_down, *(total[k, :width] for k in range(4))
 
 
 def solution(mesh):

time: 151 us -> 123 us (0.81)
  Pallas kernels: 136 us -> 114 us
  local copies, waits for them, and re-layouts: 11.1 us -> 7.54 us
  other arithmetic: 2.89 us -> 0 us
    pallas_call x1, Pallas kernels: 136 us -> 114 us  [layer(): pl.pallas_call(functools.partial(layer_kernel, with_z, grad_scale), out_s...]
    reshape x5 -> x0, local copies, waits for them, and re-layouts: 2.1 us -> none  [the longest x2 1.09 us: split_parts(): weight.reshape(rows, H, 3, HD).transpose(0, 2, 1, 3).reshape(rows, 3 * D)]
    concatenate x2 -> x0, other arithmetic: 1.58 us -> none  [the longest x1 0.85 us: shards(): d_qkv = jnp.concatenate([d_q, d_kv], axis=1)]
    unnamed x13 -> x16, local copies, waits for them, and re-layouts: 5.52 us -> 6.17 us
where the time goes in v5:
time: 123 us
  Pallas kernels  114 us (93%)
  local copies, waits for them, and re-layouts  7.54 us (6%)
    pallas_call x1, Pallas kernels, layer(): pl.pallas_call(functools.partial(layer_kernel, with_z, grad_scale), out_s...  114 us
    unnamed x16, local copies, waits for them, and re-layouts  6.17 us

profile of v5, /device:TPU:0, one launch (start us, length us, event | category | flops | bytes accessed | tf_op | source)
XLA Modules:
  0.0 122.7 jit_solution(10747419311373214532)
XLA Ops:
  0.6 114.4 %mega_layer.1 = (bf16[1024,512]{1,0:T(8,128)(2,1)}, f32[1024,512]{1,0:T(8,128)}, f32[16,1536]{1,0:T(8,128)}, f32[16,512]{1,0:T(8,128)}, f32[64,512]{1,0:T(8,128)}, /*index=5*/f32[64,512]{1,0:T(8,128)}, f32[8,128]{1,0:T(8,128)}) custom-call(bf16[1024,512]{1,0:T(8,128)(2,1)} %x_hbm.1, bf16[1024,512]{1,0:T(8,128)(2,1)} %cot_hbm.1, bf16[16,1536]{1,0:T(8,128)(2,1)} %wqkv_ref.1, ...), custom_call_target="tpu_custom_call" | custom-call | tf_op jit(solution)/shard_map/mega_layer/pallas_call | solution.py:777
  115.1 0.0 copy-start
  115.1 1.4 %slice_bitcast_fusion = (f32[16]{0:T(128)}, f32[16]{0:T(128)}, f32[16]{0:T(128)}, f32[16]{0:T(128)}) fusion(f32[8,128]{1,0:T(8,128)} %get-tuple-element.23), kind=kLoop, calls=%fused_computation | loop fusion | bytes 512 | tf_op jit(solution)/shard_map/squeeze | solution.py:861
  116.5 2.3 %copy.27 = bf16[1024,512]{1,0:T(8,128)(2,1)} copy(bf16[1024,512]{1,0:T(8,128)(2,1)} %get-tuple-element.38) | data formatting | bytes 2097152
  118.7 0.0 copy-done
  118.7 0.0 copy-start.3
  118.7 0.0 copy-start.4
  118.7 0.0 copy-start.2
  118.7 0.0 copy-start.1
  118.7 1.3 %copy.28 = f32[1024,512]{1,0:T(8,128)} copy(f32[1024,512]{1,0:T(8,128)S(1)} %copy-done) | data formatting | bytes 4194304
  120.1 0.0 copy-done.3
  120.1 0.6 copy.29
  120.7 0.0 copy-done.4
  120.7 0.6 copy.30
  121.3 0.0 copy-done.2
  121.3 0.7 copy.31
  122.0 0.0 copy-done.1
  122.0 0.7 copy.32
Async XLA Ops:
  115.1 3.6 %copy-start = (f32[1024,512]{1,0:T(8,128)S(1)}, f32[1024,512]{1,0:T(8,128)}, u32[]{:S(2)}) copy-start(f32[1024,512]{1,0:T(8,128)} %get-tuple-element.39) | copy-start | bytes 6291460
  118.7 1.3 %copy-start.3 = (f32[16,1536]{1,0:T(8,128)S(1)}, f32[16,1536]{1,0:T(8,128)}, u32[]{:S(2)}) copy-start(f32[16,1536]{1,0:T(8,128)} %get-tuple-element.40) | copy-start | bytes 294916
  118.7 2.0 %copy-start.4 = (f32[16,512]{1,0:T(8,128)S(1)}, f32[16,512]{1,0:T(8,128)}, u32[]{:S(2)}) copy-start(f32[16,512]{1,0:T(8,128)} %get-tuple-element.41) | copy-start | bytes 98308
  118.7 2.6 %copy-start.2 = (f32[64,512]{1,0:T(8,128)S(1)}, f32[64,512]{1,0:T(8,128)}, u32[]{:S(2)}) copy-start(f32[64,512]{1,0:T(8,128)} %get-tuple-element.21) | copy-start | bytes 393220
  118.7 3.3 %copy-start.1 = (f32[64,512]{1,0:T(8,128)S(1)}, f32[64,512]{1,0:T(8,128)}, u32[]{:S(2)}) copy-start(f32[64,512]{1,0:T(8,128)} %get-tuple-element.43) | copy-start | bytes 393220

commit v6 on v5

--- a/solution.py
+++ b/solution.py
@@ -217,9 +217,20 @@
             return [(seq, lax.rem(self.z + d, self.deep)) for d in range(1, self.deep)]
         return [(self.seq(*self.along(axis, d), self.c), self.z) for d in range(1, self.side)]
 
+    def spot(self, turn, d, e):
+        n = self.side
+        return lax.rem(self.y + turn * d + (1 - turn) * e, n), lax.rem(self.x + turn * e + (1 - turn) * d, n)
+
+    def steps(self):
+        line = [*range(1, self.side), 0]
+        return [(d, e) for d in line for e in line][:-1]
+
+    def plane(self):
+        return [(self.seq(*self.spot(self.c, d, e), self.c), self.z) for d, e in self.steps()]
+
     def greet(self):
         barrier = pltpu.get_barrier_semaphore()
-        others = [self.sibling(), *self.peers(0), *self.peers(1), *self.peers("z")]
+        others = [self.sibling(), *self.plane(), *self.peers("z")]
         for other in others:
             pl.semaphore_signal(barrier, inc=1, device_id=other, device_id_type=MESH)
         pl.semaphore_wait(barrier, len(others))
@@ -262,9 +273,9 @@
 
 
 class Gather:
-    def __init__(self, wires, place, shard, full, rows, with_z):
+    def __init__(self, wires, place, shard, full, rows, with_z, direct):
         self.w, self.p, self.full, self.shard = wires, place, full, shard
-        self.rows, self.with_z, self.sent = rows, with_z, []
+        self.rows, self.with_z, self.direct, self.sent = rows, with_z, direct, []
         self.group = rows * place.deep if with_z else rows
 
     def block(self, y, x):
@@ -297,12 +308,14 @@
             move.wait_recv()
         self.placed.wait()
         own = (p.y, p.x)
-        self.moves = [self._send(own, d) for d in p.peers(0)]
-        self.turned = [self._send(own, d) for d in p.peers(1)]
+        self.moves = [] if self.direct else [self._send(own, d) for d in p.peers(0)]
+        self.turned = [self._send(own, d) for d in (p.plane() if self.direct else p.peers(1))]
         self.across = [self._send(own, p.sibling())]
 
     def step2(self):
         p = self.p
+        if self.direct:
+            return
         for move in self.moves:
             move.wait_recv()
         line = self._line(0)[1:]
@@ -313,7 +326,10 @@
         for move in self.turned:
             move.wait_recv()
         p = self.p
-        self.across += [self._send(place, p.sibling()) for e in range(1, p.side) for place in self._line(e)]
+        came = [place for e in range(1, p.side) for place in self._line(e)]
+        if self.direct:
+            came += self._line(0)[1:]
+        self.across += [self._send(place, p.sibling()) for place in came]
 
     def step4(self):
         for move in self.across:
@@ -359,9 +375,9 @@
 
 
 class Scatter:
-    def __init__(self, wires, place, grads, held, hop1, hop2, hopz):
+    def __init__(self, wires, place, grads, direct, held, hop1, hop2, hopz):
         self.w, self.p, self.grads, self.held = wires, place, grads, held
-        self.hop1, self.hop2, self.hopz = hop1, hop2, hopz
+        self.direct, self.hop1, self.hop2, self.hopz = direct, hop1, hop2, hopz
         self.group = held.shape[1]
         self.crossed, self.first, self.second, self.third = {}, {}, {}, []
         n = place.side
@@ -369,10 +385,11 @@
         self.order = [(d, e) for d in self.line for e in self.line]
 
     def at(self, turn, d, e):
-        p, n = self.p, self.p.side
-        y = lax.rem(p.y + turn * d + (1 - turn) * e, n)
-        x = lax.rem(p.x + turn * e + (1 - turn) * d, n)
-        return y * n + x
+        y, x = self.p.spot(turn, d, e)
+        return y * self.p.side + x
+
+    def hop(self, d, e):
+        return self.hop1.at[d - 1, e] if d else self.hop2.at[e - 1]
 
     def rows_of(self, j, core):
         return pl.ds(pl.multiple_of((2 * j + core) * self.group, self.group), self.group)
@@ -387,7 +404,10 @@
         j = self.at(p.c, d, e)
         self.crossed[d, e].wait_recv()
         add_into(self.held, j, [self.grads[self.rows_of(j, p.c)]])
-        if d:
+        if self.direct and (d or e):
+            owner = p.seq(*p.spot(p.c, d, e), p.c), p.z
+            self.first[d, e] = self.w.copy(self.held.at[j], self.hop(d, e), owner)
+        elif d:
             self.first[d, e] = self.w.copy(self.held.at[j], self.hop1.at[d - 1, e], p.peers(0)[d - 1])
 
     def turn(self, e):
@@ -408,15 +428,20 @@
             self.fold(d, e)
 
     def step2(self):
-        for e in self.line:
+        for e in self.line if not self.direct else ():
             self.turn(e)
 
     def step3(self):
         p = self.p
-        for move in self.second.values():
-            move.wait_recv()
         self.mine = self.at(p.c, 0, 0)
-        add_into(self.held, self.mine, [self.hop2[e - 1] for e in range(1, p.side)])
+        if self.direct:
+            for move in self.first.values():
+                move.wait_recv()
+            add_into(self.held, self.mine, [self.hop(d, e)[...] for d, e in p.steps()])
+        else:
+            for move in self.second.values():
+                move.wait_recv()
+            add_into(self.held, self.mine, [self.hop2[e - 1] for e in range(1, p.side)])
         if self.hopz is not None:
             self.unit = self.group // p.deep
             for d, other in enumerate(p.peers("z"), 1):
@@ -451,7 +476,7 @@
 
     def send(self, level):
         p = self.p
-        peers = [[p.sibling()], p.peers(0), p.peers(1), p.peers("z")][level]
+        peers = [[p.sibling()], p.plane(), p.peers("z")][level]
         self.moves = []
         for peer in peers:
             self.moves.append(self.w.copy(self.sums.at[level], self.came.at[self.slot], peer))
@@ -468,10 +493,10 @@
 def layer_kernel(
     with_z, grad_scale,
     x_hbm, cot_hbm, wqkv_ref, wo_ref, wu_ref, wd_ref, gain1_ref, shift1_ref, gain2_ref, shift2_ref, span_doc_ref,
-    out_hbm, dtok_hbm, dwqkv_ref, dwo_hbm, dwu_hbm, dwd_hbm, total_ref,
-    x_ref, cot_ref, dtok_ref, dwo_ref, dwu_ref, dwd_ref, small_ref, docs_ref, own_q, own_k, own_v,
+    act2_ref, dtok_ref, dwqkv_ref, dwo_ref, dwu_ref, dwd_ref, total_ref,
+    x_ref, cot_ref, small_ref, docs_ref, own_q, own_k, own_v,
     q_mat, k_mat, v_mat, out_mat, up_mat, down_mat, gains_ref, small_all, own_sums, sums_all, sums_ref, sums_t_ref,
-    act_ref, qkv_ref, probs_ref, attn_t_ref, resid_ref, act2_ref, acted_ref, dhid_ref, dattn_ref,
+    act_ref, qkv_ref, probs_ref, attn_t_ref, resid_ref, acted_ref, dhid_ref, dattn_ref,
     gdown_ref, gup_ref, gout_ref, gq_ref, gk_ref, gv_ref, dkv_ref, delta_ref, dsum_ref, levels_ref, came_ref,
     send, recv, place_sem, *held,
 ):
@@ -486,21 +511,20 @@
     for move in local:
         move.start()
 
-    def gather(shard, full):
-        return Gather(wires, place, shard, full, shard.shape[0], with_z)
-
-    def scatter(grads, z):
+    def gather(shard, full, direct):
+        return Gather(wires, place, shard, full, shard.shape[0], with_z, direct)
+
+    def scatter(grads, z, direct):
         parts = [held.pop(0) for _ in range(4 if z else 3)]
-        return Scatter(wires, place, grads, *parts, *([] if z else [None]))
-
-    small = Gather(wires, place, small_ref, small_all, 1, True)
-    sums = Gather(wires, place, own_sums, sums_all, 1, True)
-    g_k, g_v, g_q, g_out = gather(own_k, k_mat), gather(own_v, v_mat), gather(own_q, q_mat), gather(wo_ref, out_mat)
-    g_down, g_up = gather(wd_ref, down_mat), gather(wu_ref, up_mat)
-    s_sum = scatter(sums_all, True)
-    s_down, s_up, s_out, s_q, s_k, s_v = [
-        scatter(g, with_z) for g in (gdown_ref, gup_ref, gout_ref, gq_ref, gk_ref, gv_ref)
-    ]
+        return Scatter(wires, place, grads, direct, *parts, *([] if z else [None]))
+
+    small = Gather(wires, place, small_ref, small_all, 1, True, True)
+    sums = Gather(wires, place, own_sums, sums_all, 1, True, True)
+    g_k, g_v, g_q = gather(own_k, k_mat, True), gather(own_v, v_mat, True), gather(own_q, q_mat, True)
+    g_out, g_down, g_up = gather(wo_ref, out_mat, False), gather(wd_ref, down_mat, False), gather(wu_ref, up_mat, False)
+    s_sum = scatter(sums_all, True, True)
+    s_down, s_up, s_out = [scatter(g, with_z, False) for g in (gdown_ref, gup_ref, gout_ref)]
+    s_q, s_k, s_v = [scatter(g, with_z, True) for g in (gq_ref, gk_ref, gv_ref)]
 
     width = gain1_ref.shape[1]
     small_ref[...] = jnp.zeros_like(small_ref)
@@ -513,13 +537,9 @@
     small.step1()
     g_k.step1()
     g_v.step1()
-    small.step2()
-    g_k.step2()
     g_q.step1()
-    g_v.step2()
     small.step3()
     g_k.step3()
-    g_q.step2()
     docs_ref[...] = window_docs(first, spans, span_doc_ref)
     small.step4()
     gains_ref[...] = spread_small(small_all[...], place.devices)
@@ -533,8 +553,6 @@
     loop(0, spans, norm)
     g_v.step3()
     g_k.step4()
-    g_down.step1()
-    g_out.step1()
 
     def project(mat, part):
         block = nn(act_ref[...], mat[...]).astype(BF16)
@@ -548,17 +566,17 @@
     g_v.step4()
     project(v_mat, 2)
     sums.step0()
+    g_down.step1()
     g_q.step4()
     project(q_mat, 0)
-    sums.step1()
     half = spans // 2
     loop(0, half, lambda i: span_scores(i, qkv_ref, dkv_ref))
-    sums.step2()
-    g_out.step2()
+    sums.step1()
+    g_out.step1()
+    loop(half, spans, lambda i: span_scores(i, qkv_ref, dkv_ref))
     g_down.step2()
-    loop(half, spans, lambda i: span_scores(i, qkv_ref, dkv_ref))
+    g_up.step1()
     sums.step3()
-    g_up.step1()
     sums.step4()
     for i in range(PSPANS // MOST):
         two = sums_all[pl.ds(2 * i, 2)].astype(F32)
@@ -576,11 +594,13 @@
 
     quarter = spans // 4
     loop(0, quarter, attend)
-    g_out.step3()
+    g_out.step2()
     loop(quarter, 2 * quarter, attend)
     g_up.step2()
     g_down.step3()
-    loop(2 * quarter, spans, attend)
+    loop(2 * quarter, 3 * quarter, attend)
+    g_out.step3()
+    loop(3 * quarter, spans, attend)
     g_out.step4()
 
     def residual(i):
@@ -673,9 +693,7 @@
     s_sum.step0()
     loop(0, quarter, back_near)
     s_sum.step1()
-    loop(quarter, 2 * quarter, back_near)
-    s_sum.step2()
-    loop(2 * quarter, 3 * quarter, back_near)
+    loop(quarter, 3 * quarter, back_near)
     s_sum.step3()
     for s in both:
         s.step3()
@@ -692,11 +710,6 @@
         g_ref[...] = tn(act_ref[...], dhid_ref[:, (part + 1) * D : (part + 2) * D]).astype(BF16)
         s.step0()
 
-    def write(ref, hbm, i, rows=slice(None)):
-        move = pltpu.make_async_copy(ref.at[rows], hbm.at[rows], place_sem.at[i])
-        move.start()
-        local.append(move)
-
     def finish_tokens(i):
         rows = slice(i * TILE, (i + 1) * TILE)
         dnormed = nt(dhid_ref[rows, :D], q_mat[...]) + nt(dhid_ref[rows, D : 2 * D], k_mat[...])
@@ -717,39 +730,27 @@
     finish_tokens(1)
     s_v.step1()
     finish_tokens(2)
-    s_q.step2()
     finish_tokens(3)
     total.send(0)
-    s_k.step2()
-    write(dtok_ref, dtok_hbm, 2)
+    s_q.step3()
     output(0)
+    s_k.step3()
+    output(1)
     total.take(0)
     total.send(1)
-    s_v.step2()
-    output(1)
-    s_q.step3()
-    s_k.step3()
+    s_v.step3()
     output(2)
+    output(3)
     total.take(1)
     total.send(2)
-    s_v.step3()
-    output(3)
-    write(act2_ref, out_hbm, 3)
     dwd_ref[...] = s_down.step4() * grad_scale
     dwu_ref[...] = s_up.step4() * grad_scale
     dwo_ref[...] = s_out.step4() * grad_scale
-    write(dwd_ref, dwd_hbm, 4)
-    write(dwu_ref, dwu_hbm, 5)
-    write(dwo_ref, dwo_hbm, 6)
+    join_heads((s_q.step4() * grad_scale, s_k.step4() * grad_scale, s_v.step4() * grad_scale), dwqkv_ref)
     total.take(2)
-    total.send(3)
-    join_heads((s_q.step4() * grad_scale, s_k.step4() * grad_scale, s_v.step4() * grad_scale), dwqkv_ref)
-    total.take(3)
     start = place.me * width
     lanes = pl.ds(pl.multiple_of(start // LANES * LANES, LANES), LANES)
-    total_ref[...] = pltpu.roll(levels_ref[4, :, lanes] * grad_scale, lax.rem(LANES - lax.rem(start, LANES), LANES), 1)
-    for move in local[2:]:
-        move.wait()
+    total_ref[...] = pltpu.roll(levels_ref[3, :, lanes] * grad_scale, lax.rem(LANES - lax.rem(start, LANES), LANES), 1)
     wires.finish()
 
 
@@ -768,7 +769,7 @@
     hidden_size = wu.shape[0] * owned
     whole, anywhere = pl.BlockSpec(memory_space=VMEM), pl.BlockSpec(memory_space=pl.ANY)
     shape = jax.ShapeDtypeStruct
-    peers = 1 + 2 * (side - 1) + deep - 1
+    peers = 1 + side * side - 1 + deep - 1
     n = 8 * copies_of_gather(side, deep, True) + 8
     n += 7 * (side * side + (side - 1) * side + side - 1 + deep - 1) + peers
     held = scatter_scratch(side, deep, 1, (spans, 2 * D), True)
@@ -777,23 +778,19 @@
     return pl.pallas_call(
         functools.partial(layer_kernel, with_z, grad_scale),
         out_shape=(
-            shape((tok, D), BF16),
-            shape((tok, D), F32),
-            shape((D // owned, 3 * D), F32),
-            shape((D // owned, D), F32),
-            shape((hidden_size // owned, D), F32),
-            shape((hidden_size // owned, D), F32),
-            shape((8, LANES), F32),
+            pltpu.VMEM((tok, D), BF16),
+            pltpu.VMEM((tok, D), F32),
+            pltpu.VMEM((D // owned, 3 * D), F32),
+            pltpu.VMEM((D // owned, D), F32),
+            pltpu.VMEM((hidden_size // owned, D), F32),
+            pltpu.VMEM((hidden_size // owned, D), F32),
+            pltpu.VMEM((8, LANES), F32),
         ),
         in_specs=[anywhere] * 2 + [whole] * 8 + [pl.BlockSpec(memory_space=pltpu.MemorySpace.SMEM)],
-        out_specs=(anywhere, anywhere, whole, anywhere, anywhere, anywhere, whole),
+        out_specs=(whole,) * 7,
         scratch_shapes=[
             pltpu.VMEM((tok, D), BF16),
             pltpu.VMEM((tok, D), BF16),
-            pltpu.VMEM((tok, D), F32),
-            pltpu.VMEM((D // owned, D), F32),
-            pltpu.VMEM((hidden_size // owned, D), F32),
-            pltpu.VMEM((hidden_size // owned, D), F32),
             pltpu.VMEM((1, 8, LANES), F32),
             pltpu.VMEM((WIN, S), jnp.int32),
             pltpu.VMEM((D // owned, D), BF16),
@@ -816,7 +813,6 @@
             pltpu.VMEM((spans * PAIRS, KEYS, 2 * S), BF16),
             pltpu.VMEM((D, tok), BF16),
             pltpu.VMEM((tok, D), F32),
-            pltpu.VMEM((tok, D), BF16),
             pltpu.VMEM((tok, hidden_size), BF16),
             pltpu.VMEM((tok, hidden_size), BF16),
             pltpu.VMEM((tok, D), BF16),
@@ -829,16 +825,39 @@
             pltpu.VMEM((tok, 2 * D), F32),
             pltpu.VMEM((spans * PAIRS, 2 * S), F32),
             pltpu.VMEM((FAR, 2 * D), F32),
-            pltpu.VMEM((5, 8, D), F32),
+            pltpu.VMEM((4, 8, D), F32),
             pltpu.VMEM((peers, 8, D), F32),
             pltpu.SemaphoreType.DMA((n,)),
             pltpu.SemaphoreType.DMA((n,)),
-            pltpu.SemaphoreType.DMA((7,)),
+            pltpu.SemaphoreType.DMA((2,)),
             *held,
         ],
-        compiler_params=pltpu.CompilerParams(vmem_limit_bytes=VMEM_LIMIT, collective_id=0, has_side_effects=True),
+        compiler_params=pltpu.CompilerParams(vmem_limit_bytes=VMEM_LIMIT - 7 * tok * D, collective_id=0, has_side_effects=True),
         name="mega_layer",
     )(x, cotangent, wqkv, wo, wu, wd, *vectors, span_doc)
+
+
+def deliver_kernel(*refs):
+    count = (len(refs) - 1) // 2
+    sems = refs[-1]
+    moves = [pltpu.make_async_copy(refs[i], refs[count + i], sems.at[i]) for i in range(count)]
+    for move in moves:
+        move.start()
+    for move in moves:
+        move.wait()
+
+
+def deliver(arrays):
+    anywhere = pl.BlockSpec(memory_space=pl.ANY)
+    return pl.pallas_call(
+        deliver_kernel,
+        out_shape=[jax.ShapeDtypeStruct(a.shape, a.dtype) for a in arrays],
+        in_specs=[anywhere] * len(arrays),
+        out_specs=[anywhere] * len(arrays),
+        scratch_shapes=[pltpu.SemaphoreType.DMA((len(arrays),))],
+        compiler_params=pltpu.CompilerParams(vmem_limit_bytes=2**20),
+        name="deliver",
+    )(*arrays)
 
 
 def shards(tokens, cotangent, w_qkv, w_out, w_up, w_down, gain_one, shift_one, gain_two, shift_two, span_doc):
@@ -851,8 +870,8 @@
         weights = tuple(lax.all_gather(w, "head", axis=0, tiled=True) for w in weights)
     vectors = [v[None] for v in (gain_one, shift_one, gain_two, shift_two)]
     width = gain_one.shape[0]
-    out_tokens, d_tokens, d_qkv, d_out, d_up, d_down, total = layer(
-        with_z, grad_scale, tokens, cotangent, *weights, vectors, span_doc
+    out_tokens, d_tokens, d_qkv, d_out, d_up, d_down, total = deliver(
+        layer(with_z, grad_scale, tokens, cotangent, *weights, vectors, span_doc)
     )
     if not with_z:
         d_qkv, d_out, d_up, d_down = (

time: 123 us -> 111 us (0.902)
  local copies, waits for them, and re-layouts: 7.54 us -> 0.53 us
  Pallas kernels: 114 us -> 110 us
    pallas_call x1, Pallas kernels: 114 us -> 108 us  [layer(): pl.pallas_call(functools.partial(layer_kernel, with_z, grad_scale), out_s...]
    unnamed x16 -> x0, local copies, waits for them, and re-layouts: 6.17 us -> none
    pallas_call x0 -> x1, Pallas kernels: none -> 1.84 us  [deliver(): pl.pallas_call(deliver_kernel, out_shape=[jax.ShapeDtypeStruct(a.shape, a...]
where the time goes in v6:
time: 111 us
  Pallas kernels  110 us (99%)
    pallas_call x1, Pallas kernels, layer(): pl.pallas_call(functools.partial(layer_kernel, with_z, grad_scale), out_s...  108 us

profile of v6, /device:TPU:0, one launch (start us, length us, event | category | flops | bytes accessed | tf_op | source)
XLA Modules:
  0.0 110.9 jit_solution(12800676118446891843)
XLA Ops:
  0.6 107.9 %mega_layer.1 = (bf16[1024,512]{1,0:T(8,128)(2,1)S(1)}, f32[1024,512]{1,0:T(8,128)S(1)}, f32[16,1536]{1,0:T(8,128)S(1)}, f32[16,512]{1,0:T(8,128)S(1)}, f32[64,5...) custom-call(bf16[1024,512]{1,0:T(8,128)(2,1)} %x_hbm.1, bf16[1024,512]{1,0:T(8,128)(2,1)} %cot_hbm.1, ...), custom_call_target="tpu_custom_call" | custom-call | tf_op jit(solution)/shard_map/mega_layer/pallas_call | solution.py:778
  108.5 1.8 %deliver.1 = (bf16[1024,512]{1,0:T(8,128)(2,1)}, f32[1024,512]{1,0:T(8,128)}, f32[16,1536]{1,0:T(8,128)}, f32[16,512]{1,0:T(8,128)}, f32[64,512]{1,0:T(8,128)}, /*index=5*/f32[64,512]{1,0:T(8,128)}, f32[8,128]{1,0:T(8,128)S(1)}) custom-call(bf16[1024,512]{1,0:T(8,128)(2,1)S(1)} %get-tuple-element.24.refs_0_, f32[1024,512]{1,0:T(8,128)S(1)} %get-tuple-element.25.refs_1_, ...), custom_call_target="tpu_custom_call" | custom-call | tf_op jit(solution)/shard_map/deliver/pallas_call | solution.py:852
  110.4 0.5 slice_bitcast_fusion

commit v7 on v6

--- a/solution.py
+++ b/solution.py
@@ -95,7 +95,7 @@
     return slice(pair * 2 * S, (pair + 1) * 2 * S)
 
 
-def span_scores(span, qkv_ref, scores_ref):
+def span_scores(span, qkv_ref, grown_ref, stats_ref):
     rows = tile_rows(span, S)
     key_row = lax.broadcasted_iota(jnp.int32, (S, S), 0)
     query = lax.broadcasted_iota(jnp.int32, (S, S), 1)
@@ -104,22 +104,30 @@
     masks = head_masks(1.0 / math.sqrt(HD))
     for pair in range(PAIRS):
         queries = stack_heads(qkv_ref[rows, pair_cols(0, pair)], masks)
-        scores_ref[rows, both_heads(pair)] = nt(qkv_ref[rows, pair_cols(1, pair)], queries) + causal
-
-
-def attend_span(span, first, qkv_ref, sums_ref, sums_t_ref, docs_ref, scores_ref, attn_t_ref, probs_ref):
+        scores = nt(qkv_ref[rows, pair_cols(1, pair)], queries) + causal
+        top = jnp.max(scores, axis=0, keepdims=True)
+        grown = jnp.exp(scores - top)
+        grown_ref[rows, both_heads(pair)] = grown
+        stats_ref[0, pl.ds(span * PAIRS + pair, 1), :] = top
+        stats_ref[1, pl.ds(span * PAIRS + pair, 1), :] = jnp.sum(grown, axis=0, keepdims=True)
+
+
+def attend_span(span, first, qkv_ref, sums_ref, sums_t_ref, docs_ref, grown_ref, stats_ref, attn_t_ref, probs_ref):
     rows = tile_rows(span, S)
     bias = summary_bias(first, span, docs_ref)
     bias = jnp.concatenate([bias, bias], axis=1)
     masks = head_masks(1.0 / math.sqrt(HD))
     for pair in range(PAIRS):
         queries = stack_heads(qkv_ref[rows, pair_cols(0, pair)], masks)
-        own = scores_ref[rows, both_heads(pair)]
+        own_top = stats_ref[0, pl.ds(span * PAIRS + pair, 1), :]
+        own_sum = stats_ref[1, pl.ds(span * PAIRS + pair, 1), :]
         far = nt(sums_ref[:, pair_cols(0, pair)], queries) + bias
-        top = jnp.maximum(jnp.max(own, axis=0, keepdims=True), jnp.max(far, axis=0, keepdims=True))
-        own, far = jnp.exp(own - top), jnp.exp(far - top)
-        share = 1.0 / (jnp.sum(own, axis=0, keepdims=True) + jnp.sum(far, axis=0, keepdims=True))
-        probs = jnp.concatenate([(own * share).astype(BF16), (far * share).astype(BF16)], axis=0)
+        top = jnp.maximum(own_top, jnp.max(far, axis=0, keepdims=True))
+        far = jnp.exp(far - top)
+        fade = jnp.exp(own_top - top)
+        share = 1.0 / (own_sum * fade + jnp.sum(far, axis=0, keepdims=True))
+        own = grown_ref[rows, both_heads(pair)] * (fade * share)
+        probs = jnp.concatenate([own.astype(BF16), (far * share).astype(BF16)], axis=0)
         probs_ref[span * PAIRS + pair] = probs
         vals_t = jnp.concatenate([qkv_ref[rows, pair_cols(2, pair)].T, sums_t_ref[pair_cols(1, pair), :]], axis=1)
         attn_t_ref[pair * LANES : (pair + 1) * LANES, rows] = unstack(nn(vals_t, probs)).astype(BF16)
@@ -290,50 +298,51 @@
         self.sent += self.moves
         self.placed = self.w.local(self.shard, own)
 
-    def _line(self, step):
-        p, n = self.p, self.p.side
-        y1, x1 = p.along(1, step)
-        turn = 1 - p.c
-        mine = [p.along(0, d) for d in range(n)]
-        return [(turn * y1 + (1 - turn) * y, turn * x + (1 - turn) * x1) for y, x in mine]
-
     def _send(self, place, device):
         move = self.w.copy(self.block(*place), self.block(*place), device)
         self.sent.append(move)
         return move
 
     def step1(self):
-        p = self.p
+        p, n = self.p, self.p.side
         for move in self.moves:
             move.wait_recv()
         self.placed.wait()
         own = (p.y, p.x)
-        self.moves = [] if self.direct else [self._send(own, d) for d in p.peers(0)]
-        self.turned = [self._send(own, d) for d in (p.plane() if self.direct else p.peers(1))]
-        self.across = [self._send(own, p.sibling())]
+        self.come, self.crossed = {}, {(0, 0): self._send(own, p.sibling())}
+        if self.direct:
+            for (d, e), device in zip(p.steps(), p.plane()):
+                self.come[-d % n, -e % n] = self._send(own, device)
+            return
+        for d, device in enumerate(p.peers(0), 1):
+            self.come[n - d, 0] = self._send(own, device)
+        for e, device in enumerate(p.peers(1), 1):
+            self.come[0, n - e] = self._send(own, device)
 
     def step2(self):
-        p = self.p
-        if self.direct:
-            return
-        for move in self.moves:
-            move.wait_recv()
-        line = self._line(0)[1:]
-        self.turned += [self._send(place, d) for d in p.peers(1) for place in line]
-        self.across += [self._send(place, p.sibling()) for place in line]
+        p, n = self.p, self.p.side
+        for d in range(1, n):
+            self.come[d, 0].wait_recv()
+        for d in range(1, n):
+            place = p.spot(p.c, d, 0)
+            for e, device in enumerate(p.peers(1), 1):
+                self.come[d, n - e] = self._send(place, device)
+            self.crossed[d, 0] = self._send(place, p.sibling())
 
     def step3(self):
-        for move in self.turned:
-            move.wait_recv()
-        p = self.p
-        came = [place for e in range(1, p.side) for place in self._line(e)]
-        if self.direct:
-            came += self._line(0)[1:]
-        self.across += [self._send(place, p.sibling()) for place in came]
+        p, n = self.p, self.p.side
+        rest = [(d, e) for e in range(n) for d in range(n) if (d, e) not in self.crossed]
+        for d, e in rest:
+            self.come[d, e].wait_recv()
+        for d, e in rest:
+            self.crossed[d, e] = self._send(p.spot(p.c, d, e), p.sibling())
+
+    def ready(self, d, e):
+        self.crossed[d, e].wait_recv()
 
     def step4(self):
-        for move in self.across:
-            move.wait_recv()
+        for d, e in self.crossed:
+            self.ready(d, e)
 
 
 def spread_small(gathered, devices):
@@ -361,10 +370,10 @@
 
 def gelu_parts(h):
     square = h * h
-    t = jnp.tanh(0.7978845608 * (h + 0.044715 * h * square))
-    half = 0.5 * (1.0 + t)
-    slope = 0.7978845608 * (1.0 + 3 * 0.044715 * square)
-    return h * half, half + 0.5 * h * (1.0 - t * t) * slope
+    half = 0.5 + 0.5 * jnp.tanh(h * (0.7978845608 + (0.7978845608 * 0.044715) * square))
+    acted = h * half
+    slope = 2 * 0.7978845608 + (6 * 0.7978845608 * 0.044715) * square
+    return acted, half + acted * (1.0 - half) * slope
 
 
 def add_into(held, index, others):
@@ -497,7 +506,7 @@
     x_ref, cot_ref, small_ref, docs_ref, own_q, own_k, own_v,
     q_mat, k_mat, v_mat, out_mat, up_mat, down_mat, gains_ref, small_all, own_sums, sums_all, sums_ref, sums_t_ref,
     act_ref, qkv_ref, probs_ref, attn_t_ref, resid_ref, acted_ref, dhid_ref, dattn_ref,
-    gdown_ref, gup_ref, gout_ref, gq_ref, gk_ref, gv_ref, dkv_ref, delta_ref, dsum_ref, levels_ref, came_ref,
+    gdown_ref, gup_ref, gout_ref, gq_ref, gk_ref, gv_ref, dkv_ref, stats_ref, delta_ref, dsum_ref, levels_ref, came_ref,
     send, recv, place_sem, *held,
 ):
     place = Place()
@@ -532,14 +541,14 @@
         small_ref[0, k : k + 1, :width] = ref[...].astype(F32)
     split_heads(wqkv_ref[...], (own_q, own_k, own_v))
     place.greet()
-    for g in (small, g_k, g_v, g_q, g_down, g_out, g_up):
+    for g in (small, g_k, g_v, g_q, g_down, g_out):
         g.step0()
     small.step1()
     g_k.step1()
     g_v.step1()
-    g_q.step1()
     small.step3()
     g_k.step3()
+    g_q.step1()
     docs_ref[...] = window_docs(first, spans, span_doc_ref)
     small.step4()
     gains_ref[...] = spread_small(small_all[...], place.devices)
@@ -563,20 +572,20 @@
 
     project(k_mat, 1)
     g_q.step3()
+    g_down.step1()
+    g_out.step1()
     g_v.step4()
     project(v_mat, 2)
     sums.step0()
-    g_down.step1()
+    g_up.step0()
     g_q.step4()
     project(q_mat, 0)
     half = spans // 2
-    loop(0, half, lambda i: span_scores(i, qkv_ref, dkv_ref))
+    loop(0, half, lambda i: span_scores(i, qkv_ref, dkv_ref, stats_ref))
     sums.step1()
-    g_out.step1()
-    loop(half, spans, lambda i: span_scores(i, qkv_ref, dkv_ref))
-    g_down.step2()
-    g_up.step1()
+    loop(half, spans, lambda i: span_scores(i, qkv_ref, dkv_ref, stats_ref))
     sums.step3()
+    g_out.step2()
     sums.step4()
     for i in range(PSPANS // MOST):
         two = sums_all[pl.ds(2 * i, 2)].astype(F32)
@@ -590,15 +599,13 @@
     sums_t_ref[...] = sums_ref[...].T
 
     def attend(span):
-        attend_span(span, first, qkv_ref, sums_ref, sums_t_ref, docs_ref, dkv_ref, attn_t_ref, probs_ref)
+        attend_span(span, first, qkv_ref, sums_ref, sums_t_ref, docs_ref, dkv_ref, stats_ref, attn_t_ref, probs_ref)
 
     quarter = spans // 4
+    g_up.step1()
     loop(0, quarter, attend)
-    g_out.step2()
-    loop(quarter, 2 * quarter, attend)
-    g_up.step2()
-    g_down.step3()
-    loop(2 * quarter, 3 * quarter, attend)
+    g_down.step2()
+    loop(quarter, 3 * quarter, attend)
     g_out.step3()
     loop(3 * quarter, spans, attend)
     g_out.step4()
@@ -612,9 +619,7 @@
 
     loop(0, tiles, residual)
     local[1].wait()
-    g_up.step3()
-    g_down.step4()
-    g_up.step4()
+    g_up.step2()
 
     def feed(i):
         part = tile_rows(i, CHUNK)
@@ -627,9 +632,15 @@
         gup_ref[part, :] = tn(dhid, act2_ref[...]).astype(BF16)
 
     both = (s_down, s_up)
+    blocks = [(d, e) for e in range(place.side) for d in range(place.side)]
     waiting = []
     if s_up.group == CHUNK:
-        for d, e in s_up.order:
+        for d, e in blocks:
+            if (d, e) == (0, 1):
+                g_down.step3()
+                g_up.step3()
+            g_down.ready(d, e)
+            g_up.ready(d, e)
             theirs = 2 * s_up.at(1 - place.c, d, e) + 1 - place.c
             ours = 2 * s_up.at(place.c, d, e) + place.c
             loop(0, 2, lambda i: feed(theirs + i * (ours - theirs)))
@@ -639,6 +650,9 @@
             if len(waiting) > 1:
                 fold_all(both, *waiting.pop(0))
     else:
+        for g in (g_down, g_up):
+            g.step3()
+            g.step4()
         loop(0, up_mat.shape[0] // CHUNK, feed)
         for s in both:
             s.step0()
@@ -660,9 +674,6 @@
     loop(0, tiles // 2, finish)
     for d, e in waiting:
         fold_all(both, d, e)
-    for e in s_up.line[:-1]:
-        for s in both:
-            s.turn(e)
     loop(tiles // 2, tiles, finish)
     gout_ref[...] = nn(attn_t_ref[...], act2_ref[...]).astype(BF16)
     s_out.step0()
@@ -677,11 +688,10 @@
     loop(0, quarter, back_far)
     s_out.step1()
     loop(quarter, 2 * quarter, back_far)
-    for s in both:
-        s.turn(0)
-    loop(2 * quarter, 3 * quarter, back_far)
-    s_out.step2()
-    loop(3 * quarter, spans, back_far)
+    for e in s_up.line:
+        for s in both:
+            s.turn(e)
+    loop(2 * quarter, spans, back_far)
     wires.settle(sums.sent)
     sums_all[...] = jnp.zeros_like(sums_all)
     for i in range(3):
@@ -693,6 +703,7 @@
     s_sum.step0()
     loop(0, quarter, back_near)
     s_sum.step1()
+    s_out.step2()
     loop(quarter, 3 * quarter, back_near)
     s_sum.step3()
     for s in both:
@@ -732,17 +743,17 @@
     finish_tokens(2)
     finish_tokens(3)
     total.send(0)
-    s_q.step3()
     output(0)
-    s_k.step3()
-    output(1)
     total.take(0)
     total.send(1)
-    s_v.step3()
+    s_q.step3()
+    output(1)
+    s_k.step3()
     output(2)
-    output(3)
     total.take(1)
     total.send(2)
+    s_v.step3()
+    output(3)
     dwd_ref[...] = s_down.step4() * grad_scale
     dwu_ref[...] = s_up.step4() * grad_scale
     dwo_ref[...] = s_out.step4() * grad_scale
@@ -823,6 +834,7 @@
             pltpu.VMEM((D, D), BF16),
             pltpu.VMEM((D, D), BF16),
             pltpu.VMEM((tok, 2 * D), F32),
+            pltpu.VMEM((2, spans * PAIRS, 2 * S), F32),
             pltpu.VMEM((spans * PAIRS, 2 * S), F32),
             pltpu.VMEM((FAR, 2 * D), F32),
             pltpu.VMEM((4, 8, D), F32),

time: 111 us -> 106 us (0.955)
  Pallas kernels: 110 us -> 104 us
    pallas_call x1, Pallas kernels: 108 us -> 103 us  [layer(): pl.pallas_call(functools.partial(layer_kernel, with_z, grad_scale), out_s...]
where the time goes in v7:
time: 106 us
  Pallas kernels  104 us (98%)
    pallas_call x1, Pallas kernels, layer(): pl.pallas_call(functools.partial(layer_kernel, with_z, grad_scale), out_s...  103 us

profile of v7, /device:TPU:0, one launch (start us, length us, event | category | flops | bytes accessed | tf_op | source)
XLA Modules:
  0.0 105.6 jit_solution(15489694188337048515)
XLA Ops:
  0.6 102.6 %mega_layer.1 = (bf16[1024,512]{1,0:T(8,128)(2,1)S(1)}, f32[1024,512]{1,0:T(8,128)S(1)}, f32[16,1536]{1,0:T(8,128)S(1)}, f32[16,512]{1,0:T(8,128)S(1)}, f32[64,5...) custom-call(bf16[1024,512]{1,0:T(8,128)(2,1)} %x_hbm.1, bf16[1024,512]{1,0:T(8,128)(2,1)} %cot_hbm.1, ...), custom_call_target="tpu_custom_call" | custom-call | tf_op jit(solution)/shard_map/mega_layer/pallas_call | solution.py:789
  103.3 1.8 %deliver.1 = (bf16[1024,512]{1,0:T(8,128)(2,1)}, f32[1024,512]{1,0:T(8,128)}, f32[16,1536]{1,0:T(8,128)}, f32[16,512]{1,0:T(8,128)}, f32[64,512]{1,0:T(8,128)}, /*index=5*/f32[64,512]{1,0:T(8,128)}, f32[8,128]{1,0:T(8,128)S(1)}) custom-call(bf16[1024,512]{1,0:T(8,128)(2,1)S(1)} %get-tuple-element.24.refs_0_, f32[1024,512]{1,0:T(8,128)S(1)} %get-tuple-element.25.refs_1_, ...), custom_call_target="tpu_custom_call" | custom-call | tf_op jit(solution)/shard_map/deliver/pallas_call | solution.py:864
  105.1 0.5 slice_bitcast_fusion

commit v8 on v7

--- a/solution.py
+++ b/solution.py
@@ -244,105 +244,121 @@
         pl.semaphore_wait(barrier, len(others))
 
 
+def wait_bytes(ref, sem):
+    pltpu.make_async_copy(ref, ref, sem).wait()
+
+
 class Wires:
-    def __init__(self, send, recv):
-        self.send, self.recv, self.used, self.sent = send, recv, 0, []
-
-    def copy(self, src, dst, device):
-        i = self.used
+    def __init__(self, sems):
+        self.sems, self.used, self.unsent = sems, 0, []
+
+    def sem(self):
         self.used += 1
-        move = pltpu.make_async_remote_copy(
-            src_ref=src, dst_ref=dst, send_sem=self.send.at[i], recv_sem=self.recv.at[i],
-            device_id=device, device_id_type=MESH,
-        )
-        move.start()
-        self.sent.append(move)
-        return move
-
-    def local(self, src, dst):
-        i = self.used
-        self.used += 1
-        move = pltpu.make_async_copy(src, dst, self.send.at[i])
-        move.start()
-        return move
-
-    def settle(self, moves):
-        for move in moves:
-            move.wait_send()
-        done = {id(move) for move in moves}
-        self.sent = [move for move in self.sent if id(move) not in done]
+        return self.sems.at[self.used - 1]
+
+    def copy(self, src, dst, device, sent, came):
+        pltpu.make_async_remote_copy(
+            src_ref=src, dst_ref=dst, send_sem=sent, recv_sem=came, device_id=device, device_id_type=MESH
+        ).start()
 
     def finish(self):
-        self.settle(list(self.sent))
-
-
-def copies_of_gather(side, deep, with_z):
-    return 1 + (deep - 1 if with_z else 0) + (side - 1) + (side - 1) * side + side * side
+        for ref, sem in self.unsent:
+            wait_bytes(ref, sem)
+
+
+def semaphores(side):
+    return 5 * 5 + 3 * 8 + 3 * (side * side + side + 3) + 4 * 4 + 4
 
 
 class Gather:
     def __init__(self, wires, place, shard, full, rows, with_z, direct):
         self.w, self.p, self.full, self.shard = wires, place, full, shard
-        self.rows, self.with_z, self.direct, self.sent = rows, with_z, direct, []
+        self.rows, self.with_z, self.direct = rows, with_z, direct
         self.group = rows * place.deep if with_z else rows
+        self.out, self.local, self.deep = wires.sem(), wires.sem(), wires.sem()
+        self.level, self.cross = wires.sem(), wires.sem()
+        if not direct:
+            self.column, self.cross_row, self.cross_rest = wires.sem(), wires.sem(), wires.sem()
+        sent = (2 * place.side**2 - 1) * self.group + (place.deep - 1 if with_z else 0) * rows
+        self.unsent = (full.at[pl.ds(0, sent)], self.out)
+        wires.unsent.append(self.unsent)
+        self.done = set()
 
     def block(self, y, x):
         start = self.p.seq(y, x, self.p.c) * self.group
         return self.full.at[pl.ds(pl.multiple_of(start, self.group), self.group)]
+
+    def _send(self, place, device, came):
+        self.w.copy(self.block(*place), self.block(*place), device, self.out, came)
+
+    def _wait(self, groups, sem):
+        wait_bytes(self.full.at[pl.ds(0, groups * self.group)], sem)
 
     def step0(self):
         p = self.p
         start = pl.multiple_of(p.me * self.rows, self.rows) if self.with_z else p.seq(p.y, p.x, p.c) * self.rows
         own = self.full.at[pl.ds(start, self.rows)]
-        self.moves = [self.w.copy(self.shard, own, d) for d in p.peers("z")] if self.with_z else []
-        self.sent += self.moves
-        self.placed = self.w.local(self.shard, own)
-
-    def _send(self, place, device):
-        move = self.w.copy(self.block(*place), self.block(*place), device)
-        self.sent.append(move)
-        return move
+        for device in p.peers("z") if self.with_z else ():
+            self.w.copy(self.shard, own, device, self.out, self.deep)
+        self.placed = pltpu.make_async_copy(self.shard, own, self.local)
+        self.placed.start()
 
     def step1(self):
-        p, n = self.p, self.p.side
-        for move in self.moves:
-            move.wait_recv()
+        p = self.p
+        if self.with_z:
+            wait_bytes(self.full.at[pl.ds(0, (p.deep - 1) * self.rows)], self.deep)
         self.placed.wait()
         own = (p.y, p.x)
-        self.come, self.crossed = {}, {(0, 0): self._send(own, p.sibling())}
         if self.direct:
-            for (d, e), device in zip(p.steps(), p.plane()):
-                self.come[-d % n, -e % n] = self._send(own, device)
-            return
-        for d, device in enumerate(p.peers(0), 1):
-            self.come[n - d, 0] = self._send(own, device)
-        for e, device in enumerate(p.peers(1), 1):
-            self.come[0, n - e] = self._send(own, device)
+            for device in p.plane():
+                self._send(own, device, self.level)
+        else:
+            for device in p.peers(0):
+                self._send(own, device, self.level)
+            for device in p.peers(1):
+                self._send(own, device, self.column)
+        self._send(own, p.sibling(), self.cross)
 
     def step2(self):
         p, n = self.p, self.p.side
-        for d in range(1, n):
-            self.come[d, 0].wait_recv()
+        self._wait(n - 1, self.level)
         for d in range(1, n):
             place = p.spot(p.c, d, 0)
-            for e, device in enumerate(p.peers(1), 1):
-                self.come[d, n - e] = self._send(place, device)
-            self.crossed[d, 0] = self._send(place, p.sibling())
+            for device in p.peers(1):
+                self._send(place, device, self.column)
+            self._send(place, p.sibling(), self.cross_row)
 
     def step3(self):
         p, n = self.p, self.p.side
-        rest = [(d, e) for e in range(n) for d in range(n) if (d, e) not in self.crossed]
-        for d, e in rest:
-            self.come[d, e].wait_recv()
-        for d, e in rest:
-            self.crossed[d, e] = self._send(p.spot(p.c, d, e), p.sibling())
+        if self.direct:
+            self._wait(n * n - 1, self.level)
+            for d, e in p.steps():
+                self._send(p.spot(p.c, d, e), p.sibling(), self.cross)
+        else:
+            self._wait(n * (n - 1), self.column)
+            for e in range(1, n):
+                for d in range(n):
+                    self._send(p.spot(p.c, d, e), p.sibling(), self.cross_rest)
 
     def ready(self, d, e):
-        self.crossed[d, e].wait_recv()
+        n = self.p.side
+        sems = (1, self.cross), (n - 1, self.cross_row), (n * (n - 1), self.cross_rest)
+        which = 2 if e else 1 if d else 0
+        if which not in self.done:
+            self.done.add(which)
+            self._wait(*sems[which])
 
     def step4(self):
-        for d, e in self.crossed:
+        n = self.p.side
+        if self.direct:
+            self._wait(n * n, self.cross)
+            return
+        for d, e in [(0, 0), *self.p.steps()]:
             self.ready(d, e)
+
+    def settle(self):
+        wait_bytes(*self.unsent)
+        self.w.unsent = [pair for pair in self.w.unsent if pair is not self.unsent]
 
 
 def spread_small(gathered, devices):
@@ -384,95 +400,110 @@
 
 
 class Scatter:
-    def __init__(self, wires, place, grads, direct, held, hop1, hop2, hopz):
+    def __init__(self, wires, place, grads, mode, held, hop, hopz):
         self.w, self.p, self.grads, self.held = wires, place, grads, held
-        self.direct, self.hop1, self.hop2, self.hopz = direct, hop1, hop2, hopz
+        self.mode, self.hops, self.hopz = mode, hop, hopz
         self.group = held.shape[1]
-        self.crossed, self.first, self.second, self.third = {}, {}, {}, []
+        self.unit = self.group // place.deep
         n = place.side
         self.line = [*range(1, n), 0]
         self.order = [(d, e) for d in self.line for e in self.line]
+        self.out, self.deep = wires.sem(), wires.sem()
+        if mode == "axes":
+            self.crossed = {step: wires.sem() for step in self.order}
+            self.first = [wires.sem() for _ in range(n)]
+            self.second = wires.sem()
+        else:
+            self.cross, self.level = wires.sem(), wires.sem()
+        sent = (2 * n * n - 1) * self.group + (0 if hopz is None else self.group - self.unit)
+        wires.unsent.append((grads.at[pl.ds(0, sent)], self.out))
 
     def at(self, turn, d, e):
         y, x = self.p.spot(turn, d, e)
         return y * self.p.side + x
 
     def hop(self, d, e):
-        return self.hop1.at[d - 1, e] if d else self.hop2.at[e - 1]
+        return self.hops.at[self.order.index((d, e))]
 
     def rows_of(self, j, core):
         return pl.ds(pl.multiple_of((2 * j + core) * self.group, self.group), self.group)
 
-    def cross(self, d, e):
+    def unit_rows(self, d):
+        p = self.p
+        return pl.ds(pl.multiple_of(lax.rem(p.z + d, p.deep) * self.unit, self.unit), self.unit)
+
+    def owner(self, d, e):
+        p = self.p
+        return p.seq(*p.spot(p.c, d, e), p.c), p.z
+
+    def send(self, src, dst, device, came):
+        self.w.copy(src, dst, device, self.out, came)
+
+    def cross_over(self, d, e):
         p = self.p
         j = self.at(1 - p.c, d, e)
-        self.crossed[d, e] = self.w.copy(self.grads.at[self.rows_of(j, 1 - p.c)], self.held.at[j], p.sibling())
+        came = self.crossed[d, e] if self.mode == "axes" else self.cross
+        self.send(self.grads.at[self.rows_of(j, 1 - p.c)], self.held.at[j], p.sibling(), came)
 
     def fold(self, d, e):
         p = self.p
         j = self.at(p.c, d, e)
-        self.crossed[d, e].wait_recv()
+        if self.mode == "axes":
+            wait_bytes(self.held.at[j], self.crossed[d, e])
         add_into(self.held, j, [self.grads[self.rows_of(j, p.c)]])
-        if self.direct and (d or e):
-            owner = p.seq(*p.spot(p.c, d, e), p.c), p.z
-            self.first[d, e] = self.w.copy(self.held.at[j], self.hop(d, e), owner)
-        elif d:
-            self.first[d, e] = self.w.copy(self.held.at[j], self.hop1.at[d - 1, e], p.peers(0)[d - 1])
+        if self.mode == "axes" and d:
+            self.send(self.held.at[j], self.hop(d, e), p.peers(0)[d - 1], self.first[e])
+        if self.mode == "direct" and (d or e):
+            self.send(self.held.at[j], self.hop(d, e), self.owner(d, e), self.level)
 
     def turn(self, e):
         p, n = self.p, self.p.side
         j = self.at(p.c, 0, e)
-        for d in range(1, n):
-            self.first[d, e].wait_recv()
-        add_into(self.held, j, [self.hop1[d - 1, e] for d in range(1, n)])
+        wait_bytes(self.held.at[pl.ds(0, n - 1)], self.first[e])
+        add_into(self.held, j, [self.hop(d, e)[...] for d in range(1, n)])
         if e:
-            self.second[e] = self.w.copy(self.held.at[j], self.hop2.at[e - 1], p.peers(1)[e - 1])
+            self.send(self.held.at[j], self.hop(0, e), p.peers(1)[e - 1], self.second)
 
     def step0(self):
         for d, e in self.order:
-            self.cross(d, e)
+            self.cross_over(d, e)
 
     def step1(self):
+        if self.mode != "axes":
+            wait_bytes(self.held, self.cross)
         for d, e in self.order:
             self.fold(d, e)
 
     def step2(self):
-        for e in self.line if not self.direct else ():
+        for e in self.line if self.mode == "axes" else ():
             self.turn(e)
 
     def step3(self):
         p = self.p
         self.mine = self.at(p.c, 0, 0)
-        if self.direct:
-            for move in self.first.values():
-                move.wait_recv()
+        if self.mode == "direct":
+            wait_bytes(self.hops, self.level)
             add_into(self.held, self.mine, [self.hop(d, e)[...] for d, e in p.steps()])
         else:
-            for move in self.second.values():
-                move.wait_recv()
-            add_into(self.held, self.mine, [self.hop2[e - 1] for e in range(1, p.side)])
+            wait_bytes(self.held.at[pl.ds(0, p.side - 1)], self.second)
+            add_into(self.held, self.mine, [self.hop(0, e)[...] for e in range(1, p.side)])
         if self.hopz is not None:
-            self.unit = self.group // p.deep
             for d, other in enumerate(p.peers("z"), 1):
-                self.third.append(self.w.copy(self.held.at[self.mine, self.unit_rows(d)], self.hopz.at[d - 1], other))
-
-    def unit_rows(self, d):
-        p = self.p
-        return pl.ds(pl.multiple_of(lax.rem(p.z + d, p.deep) * self.unit, self.unit), self.unit)
+                self.send(self.held.at[self.mine, self.unit_rows(d)], self.hopz.at[d - 1], other, self.deep)
 
     def step4(self):
         if self.hopz is None:
             return self.held[self.mine].astype(F32)
         total = self.held[self.mine, self.unit_rows(0)].astype(F32)
-        for d, move in enumerate(self.third):
-            move.wait_recv()
+        wait_bytes(self.hopz, self.deep)
+        for d in range(self.p.deep - 1):
             total = total + self.hopz[d].astype(F32)
         return total
 
 
 def scatter_scratch(side, deep, unit, tail, with_z):
     group = deep * unit
-    shapes = [(side * side, group), (side - 1, side, group), (side - 1, group)]
+    shapes = [(side * side, group), (side * side - 1, group)]
     if with_z:
         shapes.append((deep - 1, unit))
     return [pltpu.VMEM((*shape, *tail), BF16) for shape in shapes]
@@ -481,21 +512,22 @@
 class Total:
     def __init__(self, wires, place, sums, came):
         self.w, self.p, self.sums, self.came = wires, place, sums, came
-        self.slot = 0
+        self.out, self.slot = wires.sem(), 0
+        wires.unsent.append((came, self.out))
 
     def send(self, level):
         p = self.p
         peers = [[p.sibling()], p.plane(), p.peers("z")][level]
-        self.moves = []
+        self.sem, self.first, self.count = self.w.sem(), self.slot, len(peers)
         for peer in peers:
-            self.moves.append(self.w.copy(self.sums.at[level], self.came.at[self.slot], peer))
+            self.w.copy(self.sums.at[level], self.came.at[self.slot], peer, self.out, self.sem)
             self.slot += 1
 
     def take(self, level):
+        wait_bytes(self.came.at[pl.ds(self.first, self.count)], self.sem)
         total = self.sums[level]
-        for i, move in enumerate(self.moves):
-            move.wait_recv()
-            total = total + self.came[self.slot - len(self.moves) + i]
+        for i in range(self.count):
+            total = total + self.came[self.first + i]
         self.sums[level + 1] = total
 
 
@@ -507,10 +539,10 @@
     q_mat, k_mat, v_mat, out_mat, up_mat, down_mat, gains_ref, small_all, own_sums, sums_all, sums_ref, sums_t_ref,
     act_ref, qkv_ref, probs_ref, attn_t_ref, resid_ref, acted_ref, dhid_ref, dattn_ref,
     gdown_ref, gup_ref, gout_ref, gq_ref, gk_ref, gv_ref, dkv_ref, stats_ref, delta_ref, dsum_ref, levels_ref, came_ref,
-    send, recv, place_sem, *held,
+    sems, place_sem, *held,
 ):
     place = Place()
-    wires = Wires(send, recv)
+    wires = Wires(sems)
     tok = x_ref.shape[0]
     spans = tok // S
     tiles = tok // TILE
@@ -523,17 +555,17 @@
     def gather(shard, full, direct):
         return Gather(wires, place, shard, full, shard.shape[0], with_z, direct)
 
-    def scatter(grads, z, direct):
-        parts = [held.pop(0) for _ in range(4 if z else 3)]
-        return Scatter(wires, place, grads, direct, *parts, *([] if z else [None]))
+    def scatter(grads, z, mode):
+        parts = [held.pop(0) for _ in range(3 if z else 2)]
+        return Scatter(wires, place, grads, mode, *parts, *([] if z else [None]))
 
     small = Gather(wires, place, small_ref, small_all, 1, True, True)
     sums = Gather(wires, place, own_sums, sums_all, 1, True, True)
     g_k, g_v, g_q = gather(own_k, k_mat, True), gather(own_v, v_mat, True), gather(own_q, q_mat, True)
     g_out, g_down, g_up = gather(wo_ref, out_mat, False), gather(wd_ref, down_mat, False), gather(wu_ref, up_mat, False)
-    s_sum = scatter(sums_all, True, True)
-    s_down, s_up, s_out = [scatter(g, with_z, False) for g in (gdown_ref, gup_ref, gout_ref)]
-    s_q, s_k, s_v = [scatter(g, with_z, True) for g in (gq_ref, gk_ref, gv_ref)]
+    s_sum = scatter(sums_all, True, "direct")
+    s_down, s_up, s_out = [scatter(g, with_z, "axes") for g in (gdown_ref, gup_ref, gout_ref)]
+    s_q, s_k, s_v = [scatter(g, with_z, "direct") for g in (gq_ref, gk_ref, gv_ref)]
 
     width = gain1_ref.shape[1]
     small_ref[...] = jnp.zeros_like(small_ref)
@@ -645,7 +677,7 @@
             ours = 2 * s_up.at(place.c, d, e) + place.c
             loop(0, 2, lambda i: feed(theirs + i * (ours - theirs)))
             for s in both:
-                s.cross(d, e)
+                s.cross_over(d, e)
             waiting.append((d, e))
             if len(waiting) > 1:
                 fold_all(both, *waiting.pop(0))
@@ -692,7 +724,7 @@
         for s in both:
             s.turn(e)
     loop(2 * quarter, spans, back_far)
-    wires.settle(sums.sent)
+    sums.settle()
     sums_all[...] = jnp.zeros_like(sums_all)
     for i in range(3):
         block = lax.rem(place.me + place.devices - 2 + i, place.devices)
@@ -781,8 +813,6 @@
     whole, anywhere = pl.BlockSpec(memory_space=VMEM), pl.BlockSpec(memory_space=pl.ANY)
     shape = jax.ShapeDtypeStruct
     peers = 1 + side * side - 1 + deep - 1
-    n = 8 * copies_of_gather(side, deep, True) + 8
-    n += 7 * (side * side + (side - 1) * side + side - 1 + deep - 1) + peers
     held = scatter_scratch(side, deep, 1, (spans, 2 * D), True)
     for total in (hidden_size, hidden_size, D, D, D, D):
         held += scatter_scratch(side, deep, total // devices, (D,), with_z)
@@ -839,8 +869,7 @@
             pltpu.VMEM((FAR, 2 * D), F32),
             pltpu.VMEM((4, 8, D), F32),
             pltpu.VMEM((peers, 8, D), F32),
-            pltpu.SemaphoreType.DMA((n,)),
-            pltpu.SemaphoreType.DMA((n,)),
+            pltpu.SemaphoreType.DMA((semaphores(side),)),
             pltpu.SemaphoreType.DMA((2,)),
             *held,
         ],

time: 106 us -> 104 us (0.981)
  Pallas kernels: 104 us -> 102 us
    pallas_call x1, Pallas kernels: 103 us -> 101 us  [layer(): pl.pallas_call(functools.partial(layer_kernel, with_z, grad_scale), out_s...]
where the time goes in v8:
time: 104 us
  Pallas kernels  102 us (98%)
    pallas_call x1, Pallas kernels, layer(): pl.pallas_call(functools.partial(layer_kernel, with_z, grad_scale), out_s...  101 us

profile of v8, /device:TPU:0, one launch (start us, length us, event | category | flops | bytes accessed | tf_op | source)
XLA Modules:
  0.0 103.6 jit_solution(18147148615543494891)
XLA Ops:
  0.6 100.5 %mega_layer.1 = (bf16[1024,512]{1,0:T(8,128)(2,1)S(1)}, f32[1024,512]{1,0:T(8,128)S(1)}, f32[16,1536]{1,0:T(8,128)S(1)}, f32[16,512]{1,0:T(8,128)S(1)}, f32[64,5...) custom-call(bf16[1024,512]{1,0:T(8,128)(2,1)} %x_hbm.1, bf16[1024,512]{1,0:T(8,128)(2,1)} %cot_hbm.1, ...), custom_call_target="tpu_custom_call" | custom-call | tf_op jit(solution)/shard_map/mega_layer/pallas_call | solution.py:819
  101.2 1.8 %deliver.1 = (bf16[1024,512]{1,0:T(8,128)(2,1)}, f32[1024,512]{1,0:T(8,128)}, f32[16,1536]{1,0:T(8,128)}, f32[16,512]{1,0:T(8,128)}, f32[64,512]{1,0:T(8,128)}, /*index=5*/f32[64,512]{1,0:T(8,128)}, f32[8,128]{1,0:T(8,128)S(1)}) custom-call(bf16[1024,512]{1,0:T(8,128)(2,1)S(1)} %get-tuple-element.24.refs_0_, f32[1024,512]{1,0:T(8,128)S(1)} %get-tuple-element.25.refs_1_, ...), custom_call_target="tpu_custom_call" | custom-call | tf_op jit(solution)/shard_map/deliver/pallas_call | solution.py:893
  103.0 0.5 slice_bitcast_fusion

commit v9 on v8

--- a/solution.py
+++ b/solution.py
@@ -26,6 +26,7 @@
 VMEM = pltpu.MemorySpace.VMEM
 VMEM_LIMIT = 67043328
 TILE = 256
+TOGETHER = 2
 CHUNK = 256
 
 
@@ -41,12 +42,12 @@
     return lax.dot_general(a, b, (((0,), (0,)), ((), ())), preferred_element_type=F32)
 
 
-def loop(start, stop, body):
+def loop(start, stop, body, unroll=1):
     def step(i, carry):
         body(i)
         return carry
 
-    lax.fori_loop(start, stop, step, 0)
+    lax.fori_loop(start, stop, step, 0, unroll=unroll)
 
 
 def tile_rows(i, size):
@@ -591,7 +592,7 @@
         xhat, _ = normed_parts(x_ref[rows, :].astype(F32))
         act_ref[rows, :] = (xhat * gains_ref[0:1, :] + gains_ref[1:2, :]).astype(BF16)
 
-    loop(0, spans, norm)
+    loop(0, spans, norm, 4)
     g_v.step3()
     g_k.step4()
 
@@ -613,9 +614,9 @@
     g_q.step4()
     project(q_mat, 0)
     half = spans // 2
-    loop(0, half, lambda i: span_scores(i, qkv_ref, dkv_ref, stats_ref))
+    loop(0, half, lambda i: span_scores(i, qkv_ref, dkv_ref, stats_ref), TOGETHER)
     sums.step1()
-    loop(half, spans, lambda i: span_scores(i, qkv_ref, dkv_ref, stats_ref))
+    loop(half, spans, lambda i: span_scores(i, qkv_ref, dkv_ref, stats_ref), TOGETHER)
     sums.step3()
     g_out.step2()
     sums.step4()
@@ -635,11 +636,11 @@
 
     quarter = spans // 4
     g_up.step1()
-    loop(0, quarter, attend)
+    loop(0, quarter, attend, TOGETHER)
     g_down.step2()
-    loop(quarter, 3 * quarter, attend)
+    loop(quarter, 3 * quarter, attend, TOGETHER)
     g_out.step3()
-    loop(3 * quarter, spans, attend)
+    loop(3 * quarter, spans, attend, TOGETHER)
     g_out.step4()
 
     def residual(i):
@@ -649,7 +650,7 @@
         xhat, _ = normed_parts(resid)
         act2_ref[rows, :] = (xhat * gains_ref[2:3, :] + gains_ref[3:4, :]).astype(BF16)
 
-    loop(0, tiles, residual)
+    loop(0, tiles, residual, 2)
     local[1].wait()
     g_up.step2()
 
@@ -675,7 +676,7 @@
             g_up.ready(d, e)
             theirs = 2 * s_up.at(1 - place.c, d, e) + 1 - place.c
             ours = 2 * s_up.at(place.c, d, e) + place.c
-            loop(0, 2, lambda i: feed(theirs + i * (ours - theirs)))
+            loop(0, 2, lambda i: feed(theirs + i * (ours - theirs)), 2)
             for s in both:
                 s.cross_over(d, e)
             waiting.append((d, e))
@@ -703,10 +704,10 @@
         act2_ref[rows, :] = branch
         dattn_ref[rows, :] = nt(branch, out_mat[...]).astype(BF16)
 
-    loop(0, tiles // 2, finish)
+    loop(0, tiles // 2, finish, 2)
     for d, e in waiting:
         fold_all(both, d, e)
-    loop(tiles // 2, tiles, finish)
+    loop(tiles // 2, tiles, finish, 2)
     gout_ref[...] = nn(attn_t_ref[...], act2_ref[...]).astype(BF16)
     s_out.step0()
     dsum_ref[...] = jnp.zeros_like(dsum_ref)
@@ -717,13 +718,13 @@
     def back_near(span):
         span_back(span, qkv_ref, sums_t_ref, probs_ref, dattn_ref, delta_ref, dhid_ref, dkv_ref)
 
-    loop(0, quarter, back_far)
+    loop(0, quarter, back_far, TOGETHER)
     s_out.step1()
-    loop(quarter, 2 * quarter, back_far)
+    loop(quarter, 2 * quarter, back_far, TOGETHER)
     for e in s_up.line:
         for s in both:
             s.turn(e)
-    loop(2 * quarter, spans, back_far)
+    loop(2 * quarter, spans, back_far, TOGETHER)
     sums.settle()
     sums_all[...] = jnp.zeros_like(sums_all)
     for i in range(3):
@@ -733,15 +734,15 @@
     for i in range(PSPANS // spans):
         sums_all[i] = dsum_ref[i * spans : (i + 1) * spans, :].astype(BF16)
     s_sum.step0()
-    loop(0, quarter, back_near)
+    loop(0, quarter, back_near, TOGETHER)
     s_sum.step1()
     s_out.step2()
-    loop(quarter, 3 * quarter, back_near)
+    loop(quarter, 3 * quarter, back_near, TOGETHER)
     s_sum.step3()
     for s in both:
         s.step3()
     s_out.step3()
-    loop(3 * quarter, spans, back_near)
+    loop(3 * quarter, spans, back_near, TOGETHER)
     gq_ref[...] = tn(act_ref[...], dhid_ref[:, :D]).astype(BF16)
     s_q.step0()
     shares = s_sum.step4()[0] * (1.0 / S)
@@ -782,9 +783,9 @@
     output(1)
     s_k.step3()
     output(2)
+    s_v.step3()
     total.take(1)
     total.send(2)
-    s_v.step3()
     output(3)
     dwd_ref[...] = s_down.step4() * grad_scale
     dwu_ref[...] = s_up.step4() * grad_scale

time: 104 us -> 102 us (0.981)
  Pallas kernels: 102 us -> 100 us
    pallas_call x1, Pallas kernels: 101 us -> 98.5 us  [layer(): pl.pallas_call(functools.partial(layer_kernel, with_z, grad_scale), out_s...]
where the time goes in v9:
time: 102 us
  Pallas kernels  100 us (98%)
    pallas_call x1, Pallas kernels, layer(): pl.pallas_call(functools.partial(layer_kernel, with_z, grad_scale), out_s...  98.5 us

profile of v9, /device:TPU:0, one launch (start us, length us, event | category | flops | bytes accessed | tf_op | source)
XLA Modules:
  0.0 101.5 jit_solution(17950668250661594371)
XLA Ops:
  0.6 98.5 %mega_layer.1 = (bf16[1024,512]{1,0:T(8,128)(2,1)S(1)}, f32[1024,512]{1,0:T(8,128)S(1)}, f32[16,1536]{1,0:T(8,128)S(1)}, f32[16,512]{1,0:T(8,128)S(1)}, f32[64,5...) custom-call(bf16[1024,512]{1,0:T(8,128)(2,1)} %x_hbm.1, bf16[1024,512]{1,0:T(8,128)(2,1)} %cot_hbm.1, ...), custom_call_target="tpu_custom_call" | custom-call | tf_op jit(solution)/shard_map/mega_layer/pallas_call | solution.py:820
  99.1 1.8 %deliver.1 = (bf16[1024,512]{1,0:T(8,128)(2,1)}, f32[1024,512]{1,0:T(8,128)}, f32[16,1536]{1,0:T(8,128)}, f32[16,512]{1,0:T(8,128)}, f32[64,512]{1,0:T(8,128)}, /*index=5*/f32[64,512]{1,0:T(8,128)}, f32[8,128]{1,0:T(8,128)S(1)}) custom-call(bf16[1024,512]{1,0:T(8,128)(2,1)S(1)} %get-tuple-element.24.refs_0_, f32[1024,512]{1,0:T(8,128)S(1)} %get-tuple-element.25.refs_1_, ...), custom_call_target="tpu_custom_call" | custom-call | tf_op jit(solution)/shard_map/deliver/pallas_call | solution.py:894
  101.0 0.5 slice_bitcast_fusion

commit v10 on v9

--- a/solution.py
+++ b/solution.py
@@ -721,10 +721,12 @@
     loop(0, quarter, back_far, TOGETHER)
     s_out.step1()
     loop(quarter, 2 * quarter, back_far, TOGETHER)
-    for e in s_up.line:
+    for e in s_up.line[:-1]:
         for s in both:
             s.turn(e)
     loop(2 * quarter, spans, back_far, TOGETHER)
+    for s in both:
+        s.turn(0)
     sums.settle()
     sums_all[...] = jnp.zeros_like(sums_all)
     for i in range(3):
@@ -779,14 +781,14 @@
     output(0)
     total.take(0)
     total.send(1)
+    output(1)
     s_q.step3()
-    output(1)
+    output(2)
     s_k.step3()
-    output(2)
+    output(3)
     s_v.step3()
     total.take(1)
     total.send(2)
-    output(3)
     dwd_ref[...] = s_down.step4() * grad_scale
     dwu_ref[...] = s_up.step4() * grad_scale
     dwo_ref[...] = s_out.step4() * grad_scale

time: 102 us -> 102 us (level)
  no operation moved by 1% of the time
where the time goes in v10:
time: 102 us
  Pallas kernels  100 us (98%)
    pallas_call x1, Pallas kernels, layer(): pl.pallas_call(functools.partial(layer_kernel, with_z, grad_scale), out_s...  98.5 us

profile of v10, /device:TPU:0, one launch (start us, length us, event | category | flops | bytes accessed | tf_op | source)
XLA Modules:
  0.0 101.5 jit_solution(2364430358178382171)
XLA Ops:
  0.6 98.5 %mega_layer.1 = (bf16[1024,512]{1,0:T(8,128)(2,1)S(1)}, f32[1024,512]{1,0:T(8,128)S(1)}, f32[16,1536]{1,0:T(8,128)S(1)}, f32[16,512]{1,0:T(8,128)S(1)}, f32[64,5...) custom-call(bf16[1024,512]{1,0:T(8,128)(2,1)} %x_hbm.1, bf16[1024,512]{1,0:T(8,128)(2,1)} %cot_hbm.1, ...), custom_call_target="tpu_custom_call" | custom-call | tf_op jit(solution)/shard_map/mega_layer/pallas_call | solution.py:822
  99.1 1.8 %deliver.1 = (bf16[1024,512]{1,0:T(8,128)(2,1)}, f32[1024,512]{1,0:T(8,128)}, f32[16,1536]{1,0:T(8,128)}, f32[16,512]{1,0:T(8,128)}, f32[64,512]{1,0:T(8,128)}, /*index=5*/f32[64,512]{1,0:T(8,128)}, f32[8,128]{1,0:T(8,128)S(1)}) custom-call(bf16[1024,512]{1,0:T(8,128)(2,1)S(1)} %get-tuple-element.24.refs_0_, f32[1024,512]{1,0:T(8,128)S(1)} %get-tuple-element.25.refs_1_, ...), custom_call_target="tpu_custom_call" | custom-call | tf_op jit(solution)/shard_map/deliver/pallas_call | solution.py:896
  101.0 0.5 slice_bitcast_fusion
